TPU v7x, 256 devices: a whole 4x4x8 slice. The times are simulated.
256 devices in a mesh: vocab: 32 (over x, z), dp: 8 (over y, core).
Axes of the slice: x: 4, y: 4, z: 8, core: 2. Of those that a mesh axis runs over, the one named last changes fastest.
Arguments:
- teacher_hidden: bfloat16 [1024, 5376], P('dp'), may hold values from -48 to 48
- student_hidden: bfloat16 [1024, 2560], P('dp'), may hold values from -48 to 48
- teacher_codes: bfloat16 [131072, 5376], P(('vocab', 'dp')), may hold values from -8 to 7, as said below
- teacher_scales: float32 [131072, 42], P(('vocab', 'dp')), may hold values from 0.003 to 0.07
- student_weight: bfloat16 [131072, 2560], P(('vocab', 'dp')), may hold values from -1 to 1
- loss_scale: bfloat16 [1024], P('dp'), may hold values from 2 to 20
Outputs:
- kl: float32 [1024], P('dp')
- grad_hidden: bfloat16 [1024, 2560], P('dp', 'vocab')
- grad_weight: bfloat16 [131072, 2560], P(('vocab', 'dp'))
Inputs may be any that keep to these rules, and one draw needn't show every extreme that they name: `teacher_codes`: whole numbers.
All inputs are finite; a program needn't handle non-finite values.
Results may differ from a plain program's by a relative error of at most 0.0085.
Values may be sent and summed in bfloat16 or wider, within the bound.
No kernel may reach another device: no remote copies, remote signals or barrier semaphores. Data moves between devices by JAX's collectives and lax.ppermute only.
A program may use at most 128 MiB of HBM per device.

v0:
```python
import jax
import jax.numpy as jnp
from jax import lax
from jax.sharding import Mesh
from jax.sharding import PartitionSpec as P

GROUP = 128
DP = ("dp_0", "dp_1")
VOCAB_DP = ("vocab_0", "vocab_1", "dp_0", "dp_1")
VOCAB = ("vocab_0", "vocab_1")


def in_one_piece(arrays, axis, dim, along):
    columns = [a.reshape(*a.shape[:along], -1) for a in arrays]
    both = jnp.concatenate(columns, axis=along)
    whole, at, done = (lax.all_gather(both, axis, axis=dim, tiled=True), 0, [])
    for a, column in zip(arrays, columns):
        share = whole[..., at : at + column.shape[along]]
        done.append(share.reshape(*share.shape[:along], *a.shape[along:]))
        at += column.shape[along]
    return tuple(done)


def all_in_one(x, axis):
    leaves = jax.tree.leaves(x)
    order = sorted(range(len(leaves)), key=lambda k: -leaves[k].size)
    width = (1, *leaves[order[0]].shape)[-1]
    lines = [
        jnp.pad(leaves[k].reshape(-1), (0, -leaves[k].size % width)).reshape(-1, width)
        for k in order
    ]
    both, at, found = (lax.all_gather(jnp.concatenate(lines), axis), 0, {})
    for k, line in zip(order, lines):
        share = both[:, at : at + len(line)].reshape(len(both), -1)
        found[k] = share[:, : leaves[k].size].reshape(-1, *leaves[k].shape)
        at += len(line)
    numbers = iter(range(len(leaves)))
    return jax.tree.map(lambda _: found[next(numbers)], x)


def joined_all(x, axes, combine):
    for axis in axes:
        pieces = all_in_one(x, axis)
        x = jax.tree.map(lambda part: part[0], pieces)
        for k in range(1, lax.axis_size(axis)):
            x = combine(x, jax.tree.map(lambda part: part[k], pieces))
    return x


def cut_along(x, dim, size):
    before, after = (x.shape[:dim], x.shape[dim + 1 :])
    return jnp.moveaxis(x.reshape(*before, size, -1, *after), dim, 0)


def sum_at_owner(x, axis, dim):
    size = lax.axis_size(axis)
    blocks = lax.all_to_all(cut_along(x, dim, size), axis, 0, 0, tiled=True)
    return jnp.sum(blocks, axis=0)


def dequantize(code_values, scales):
    row_count = code_values.shape[0]
    grouped = code_values.astype(jnp.float32).reshape(row_count, -1, GROUP) * scales[:, :, None]
    return grouped.reshape(row_count, -1).astype(jnp.bfloat16)


def contract_last(left_rows, right_rows):
    return lax.dot_general(
        left_rows, right_rows, (((1,), (1,)), ((), ())), preferred_element_type=jnp.float32
    )


def combine_stats(earlier, later):
    teacher_top = jnp.maximum(earlier[0], later[0])
    left_teacher = jnp.exp(earlier[0] - teacher_top)
    right_teacher = jnp.exp(later[0] - teacher_top)
    student_top = jnp.maximum(earlier[3], later[3])
    left_student = jnp.exp(earlier[3] - student_top)
    right_student = jnp.exp(later[3] - student_top)
    return (
        teacher_top,
        earlier[1] * left_teacher + later[1] * right_teacher,
        earlier[2] * left_teacher + later[2] * right_teacher,
        student_top,
        earlier[4] * left_student + later[4] * right_student,
    )


def local(
    teacher_hidden, student_hidden, teacher_codes, teacher_scales, student_weight, loss_scale
):
    tok_rows = teacher_hidden.shape[0]
    teacher_all, student_all, scale_all = in_one_piece(
        (teacher_hidden, student_hidden, loss_scale), DP, 0, 1
    )
    teacher_table = dequantize(teacher_codes, teacher_scales)
    teacher_logits = contract_last(teacher_all, teacher_table)
    student_logits = contract_last(student_all, student_weight)
    teacher_local = jnp.max(teacher_logits, axis=1)
    student_local = jnp.max(student_logits, axis=1)
    teacher_exp = jnp.exp(teacher_logits - teacher_local[:, None])
    student_exp = jnp.exp(student_logits - student_local[:, None])
    teacher_top, teacher_total, cross_total, student_top, student_total = joined_all(
        (
            teacher_local,
            jnp.sum(teacher_exp, axis=1),
            jnp.sum(teacher_exp * (teacher_logits - student_logits), axis=1),
            student_local,
            jnp.sum(student_exp, axis=1),
        ),
        VOCAB_DP,
        combine_stats,
    )
    teacher_lse = teacher_top + jnp.log(teacher_total)
    student_lse = student_top + jnp.log(student_total)
    divergence = cross_total / teacher_total - teacher_lse + student_lse
    own_start = lax.axis_index(DP) * tok_rows
    kl = lax.dynamic_slice_in_dim(divergence, own_start, tok_rows, 0)
    teacher_prob = jnp.exp(teacher_logits - teacher_lse[:, None])
    student_prob = jnp.exp(student_logits - student_lse[:, None])
    logit_grad = (scale_all.astype(jnp.float32)[:, None] * (student_prob - teacher_prob)).astype(
        jnp.bfloat16
    )
    grad_weight = lax.dot_general(
        logit_grad, student_all, (((0,), (0,)), ((), ())), preferred_element_type=jnp.float32
    ).astype(jnp.bfloat16)
    token_part = lax.psum_scatter(
        jnp.dot(logit_grad, student_weight, preferred_element_type=jnp.float32),
        DP,
        scatter_dimension=0,
        tiled=True,
    )
    grad_hidden = sum_at_owner(token_part, VOCAB, 1).astype(jnp.bfloat16)
    return (kl, grad_hidden, grad_weight)


def solution(mesh):
    split = Mesh(mesh.devices.reshape(4, 8, 4, 2), ("vocab_0", "vocab_1", "dp_0", "dp_1"))
    return jax.shard_map(
        local,
        mesh=split,
        in_specs=(
            P(DP, None),
            P(DP, None),
            P(VOCAB_DP, None),
            P(VOCAB_DP, None),
            P(VOCAB_DP, None),
            P(DP),
        ),
        out_specs=(P(DP), P(DP, VOCAB), P(VOCAB_DP, None)),
        check_vma=False,
    )
```

profile of v0, /device:TPU:8, one launch (start us, length us, event | category | flops | bytes accessed | tf_op | source)
XLA Modules:
  0.0 297.4 jit_solution(4016099578054267569)
XLA Ops:
  7.2 0.9 copy.14
  8.2 3.0 %pad_maximum_fusion = bf16[128,7937]{1,0:T(8,128)(2,1)} fusion(bf16[128,1]{1,0:T(8,128)(2,1)S(1)} %copy.14, bf16[128,2560]{1,0:T(8,128)(2,1)} %param.7, bf16[128,5376]{1,0:T(8,128)(2,1)} %param.6), kind=kLoop, calls=%fused_computation.14 | loop fusion | flops 6095616 | bytes 4063744 | tf_op jit(solution)/shard_map/concatenate | solution.py:15
  11.2 8.3 %copy.15 = bf16[512,5376]{0,1:T(8,128)(2,1)} copy(bf16[512,5376]{1,0:T(8,128)(2,1)} %param.8) | data formatting | bytes 11010048 | tf_op args[2]
  19.6 6.1 %fusion.2 = bf16[512,5376]{0,1:T(8,128)(2,1)} fusion(bf16[512,5376]{0,1:T(8,128)(2,1)} %copy.15, f32[512,42]{0,1:T(8,128)S(1)} %copy-done.5), kind=kLoop, calls=%fused_computation.3 | loop fusion | flops 8257536 | bytes 11096064 | tf_op jit(solution)/shard_map/convert_element_type | solution.py:64
  25.6 74.6 %all-gather.10.cloned.1.call-done = bf16[1024,7937]{1,0:T(8,128)(2,1)} async-done(((bf16[128,7937]{1,0:T(8,128)(2,1)}), bf16[1024,7937]{1,0:T(8,128)(2,1)}) %all-gather.10.cloned.1.call-update) | async-done | bytes 16254992 | tf_op jit(solution)/shard_map/all_gather | solution.py:16
  100.2 5.0 %fusion.166 = (f32[1024]{0:T(1024)S(1)}, f32[1024,512]{0,1:T(8,128)S(1)}) fusion(bf16[512,2560]{1,0:T(8,128)(2,1)S(1)} %copy-done, bf16[1024,7937]{1,0:T(8,128)(2,1)} %all-gather.10.cloned.1.call-done), kind=kOutput, calls=%fused_computation.276 | convolution fusion | flops 2684877824 | bytes 9965568 | tf_op jit(solution)/shard_map/dot_general | solution.py:68
  105.3 9.5 %fusion.165 = (f32[1024]{0:T(1024)S(1)}, f32[1024,512]{0,1:T(8,128)S(1)}) fusion(bf16[512,5376]{0,1:T(8,128)(2,1)S(1)} %copy-done.3, bf16[1024,7937]{1,0:T(8,128)(2,1)} %all-gather.10.cloned.1.call-done), kind=kOutput, calls=%fused_computation.275 | convolution fusion | flops 5637667840 | bytes 18616320 | tf_op jit(solution)/shard_map/dot_general | solution.py:68
  114.8 0.8 multiply_reduce_fusion
  115.6 0.5 copy-done.2
  116.2 12.3 %all-gather.4 = f32[4,5,1024]{2,1,0:T(8,128)S(1)} all-gather(f32[1,5,1024]{2,1,0:T(8,128)S(1)} %bitcast.847), channel_id=2, replica_groups=mesh['vocab_0'=4,'vocab_1'=8,'dp_0'=4,'dp_1'=2] {'vocab_0'}, dimensions={0}, use_global_device_ids=true | all-gather | bytes 102400 | tf_op jit(solution)/shard_map/all_gather | solution.py:32
  128.7 26.2 %all-gather.5 = f32[8,5,1024]{2,1,0:T(8,128)S(1)} all-gather(f32[1,5,1024]{2,1,0:T(8,128)S(1)} %bitcast.848), channel_id=3, replica_groups=mesh['vocab_0'=4,'vocab_1'=8,'dp_0'=4,'dp_1'=2] {'vocab_1'}, dimensions={0}, use_global_device_ids=true | all-gather | bytes 184320 | tf_op jit(solution)/shard_map/all_gather | solution.py:32
  155.3 11.1 %all-gather.6 = f32[4,5,1024]{2,1,0:T(8,128)S(1)} all-gather(f32[1,5,1024]{2,1,0:T(8,128)S(1)} %bitcast.849), channel_id=4, replica_groups=mesh['vocab_0'=4,'vocab_1'=8,'dp_0'=4,'dp_1'=2] {'dp_0'}, dimensions={0}, use_global_device_ids=true | all-gather | bytes 102400 | tf_op jit(solution)/shard_map/all_gather | solution.py:32
  166.6 1.9 all-gather.7
  168.5 1.1 convert_reduce_fusion
  169.6 2.8 multiply_convert_fusion
  172.4 1.0 copy-done.4
  173.4 5.5 %fusion.167 = f32[1024,2560]{1,0:T(8,128)} fusion(bf16[1024,512]{0,1:T(8,128)(2,1)S(1)} %multiply_convert_fusion, bf16[512,2560]{1,0:T(8,128)(2,1)S(1)} %copy-done), kind=kOutput, calls=%fused_computation.277 | convolution fusion | flops 2684354560 | bytes 14155776 | tf_op jit(solution)/shard_map/dot_general | solution.py:128
  178.9 62.1 %reduce-scatter.2.cloned.1.call-done = f32[128,2560]{1,0:T(8,128)} async-done(((f32[1024,2560]{1,0:T(8,128)}), f32[128,2560]{1,0:T(8,128)}) %reduce-scatter.2.cloned.1.call-update) | async-done | bytes 1310736 | tf_op jit(solution)/shard_map/reduce_scatter | solution.py:127
  241.0 2.8 copy.16
  243.8 10.2 %all-to-all-start = ((f32[32,128,80]{1,2,0:T(8,128)}), f32[32,128,80]{1,2,0:T(8,128)}, u32[]{:S(2)}, u32[]{:S(2)}) async-start(f32[32,128,80]{1,2,0:T(8,128)} %bitcast.846), calls=%async_computation.1 | async-start | bytes 2621440 | tf_op jit(solution)/shard_map/all_to_all | solution.py:57
  254.0 0.6 dynamic_slice.3
  254.5 7.2 %fusion.7 = bf16[512,2560]{1,0:T(8,128)(2,1)} fusion(bf16[1024,512]{0,1:T(8,128)(2,1)} %copy-done.4, bf16[1024,7937]{1,0:T(8,128)(2,1)} %all-gather.10.cloned.1.call-done), kind=kOutput, calls=%fused_computation.8 | convolution fusion | flops 2685665280 | bytes 8912896 | tf_op jit(solution)/shard_map/dot_general | solution.py:124
  261.7 26.8 %all-to-all-done = f32[32,128,80]{1,2,0:T(8,128)} async-done(((f32[32,128,80]{1,2,0:T(8,128)}), f32[32,128,80]{1,2,0:T(8,128)}, u32[]{:S(2)}, u32[]{:S(2)}) %all-to-all-start) | async-done | bytes 1310752 | tf_op jit(solution)/shard_map/all_to_all | solution.py:57
  288.6 2.0 reduce_sum.39
  (27 shorter events, 1.0 us)
Async XLA Ops:
  7.2 93.1 %copy-start = (bf16[512,2560]{1,0:T(8,128)(2,1)S(1)}, bf16[512,2560]{1,0:T(8,128)(2,1)}, u32[]{:S(2)}) copy-start(bf16[512,2560]{1,0:T(8,128)(2,1)} %param.10) | copy-start | bytes 7864324
  7.2 93.1 %all-gather.10.cloned.1.call-start = ((), (), s32[]{:S(2)}) async-start(), calls=%async_computation.2 | async-start | bytes 18579456 | tf_op jit(solution)/shard_map/all_gather | solution.py:16
  11.2 8.4 %copy-start.5 = (f32[512,42]{0,1:T(8,128)S(1)}, f32[512,42]{0,1:T(8,128)}, u32[]{:S(2)}) copy-start(f32[512,42]{0,1:T(8,128)} %param.9) | copy-start | bytes 258052
  11.2 229.8 %reduce-scatter.2.cloned.1.call-start = ((), (), s32[]{:S(2)}) async-start(), calls=%async_computation.3 | async-start | bytes 11796480 | tf_op jit(solution)/shard_map/reduce_scatter | solution.py:127
  100.2 5.0 %copy-start.3 = (bf16[512,5376]{0,1:T(8,128)(2,1)S(1)}, bf16[512,5376]{0,1:T(8,128)(2,1)}, u32[]{:S(2)}) copy-start(bf16[512,5376]{0,1:T(8,128)(2,1)} %fusion.2) | copy-start | bytes 16515076
  105.3 9.5 %copy-start.1 = (f32[1024,512]{0,1:T(8,128)}, f32[1024,512]{0,1:T(8,128)S(1)}, u32[]{:S(2)}) copy-start(f32[1024,512]{0,1:T(8,128)S(1)} %get-tuple-element.40) | copy-start | bytes 6291460
  114.8 1.3 copy-start.2
  172.4 1.0 copy-start.4
  243.8 44.8 %all-to-all-start = ((f32[32,128,80]{1,2,0:T(8,128)}), f32[32,128,80]{1,2,0:T(8,128)}, u32[]{:S(2)}, u32[]{:S(2)}) async-start(f32[32,128,80]{1,2,0:T(8,128)} %bitcast.846), calls=%async_computation.1 | async-start | bytes 2621440 | tf_op jit(solution)/shard_map/all_to_all | solution.py:57
Sparse Core Ops, SparseCore 0:
  11.3 88.8 all-gather.9
  179.0 61.9 reduce-scatter.1
where the time goes:
time: 299 us; the launch traced here: 297 us
  waiting for transfers between devices  164 us (55%)
  blocking collectives  51.4 us (17%)
  matrix products  27.2 us (9%)
  other arithmetic  16.4 us (5%)
  local copies, waits for them, and re-layouts  14.3 us (5%)
  between operations  14.2 us (5%)
  starting transfers between devices  10.2 us (3%)
    all_gather x1, waiting for transfers between devices, in_one_piece(): whole, at, done = (lax.all_gather(both, axis, axis=dim, tiled=True), 0, [])  74.6 us
    reduce_scatter x1, waiting for transfers between devices, local(): lax.psum_scatter(jnp.dot(logit_grad, student_weight, preferred_element_ty...  62.1 us
    all_gather x4, blocking collectives, all_in_one(): both, at, found = (lax.all_gather(jnp.concatenate(lines), axis), 0, {})  51.4 us
    all_to_all x1, waiting for transfers between devices, sum_at_owner(): blocks = lax.all_to_all(cut_along(x, dim, size), axis, 0, 0, tiled=True)  26.8 us
    dot_general x2, matrix products, contract_last(): lax.dot_general(left_rows, right_rows, (((1,), (1,)), ((), ())), preferre...  14.5 us
    all_to_all x1, starting transfers between devices, sum_at_owner(): blocks = lax.all_to_all(cut_along(x, dim, size), axis, 0, 0, tiled=True)  10.2 us
    unnamed x13, local copies, waits for them, and re-layouts  9.83 us
    dot_general x1, matrix products, local(): lax.dot_general(logit_grad, student_all, (((0,), (0,)), ((), ())), prefer...  7.19 us
  transfers between devices with their start and end apart: 3, of which 3 were waited for; matrix products, arithmetic and copies ran while one was open for 7% of the time, Pallas kernels for 0%

commit v1 on v0

v1 whole, which is shorter than its diff:
```python
import jax
import jax.numpy as jnp
from jax import lax
from jax.sharding import Mesh
from jax.sharding import PartitionSpec as P

GROUP = 128
AXES = ("x", "z", "y", "c")
DP = ("y", "c")
VOCAB = ("x", "z")
F32, BF16 = jnp.float32, jnp.bfloat16


def shift(a, axis, by):
    n = lax.axis_size(axis)
    return lax.ppermute(a, axis, [((i + by) % n, i) for i in range(n)])


def rolled(blocks, start):
    n = blocks.shape[0]
    return lax.dynamic_slice_in_dim(jnp.concatenate([blocks, blocks[:-1]]), start % n, n, 0)


def dequantize(code_values, scales):
    row_count = code_values.shape[0]
    grouped = code_values.astype(F32).reshape(row_count, -1, GROUP) * scales[:, :, None]
    return grouped.reshape(row_count, -1).astype(BF16)


def rows_by_tokens(rows, tokens):
    return lax.dot_general(rows, tokens, (((1,), (1,)), ((), ())), preferred_element_type=F32)


def to_all(a, axes):
    n = lax.axis_size(axes)
    return lax.all_to_all(jnp.broadcast_to(a[None], (n, *a.shape)), axes, 0, 0, tiled=True)


def combine(stats):
    teacher_top = jnp.max(stats[:, 0], axis=0)
    student_top = jnp.max(stats[:, 3], axis=0)
    teacher_factor = jnp.exp(stats[:, 0] - teacher_top)
    student_factor = jnp.exp(stats[:, 3] - student_top)
    return jnp.stack(
        [
            teacher_top,
            jnp.sum(stats[:, 1] * teacher_factor, axis=0),
            jnp.sum(stats[:, 2] * teacher_factor, axis=0),
            student_top,
            jnp.sum(stats[:, 4] * student_factor, axis=0),
        ]
    )


def local(
    teacher_hidden, student_hidden, teacher_codes, teacher_scales, student_weight, loss_scale
):
    tok, width_t = teacher_hidden.shape
    width_s = student_hidden.shape[1]
    n_x, n_z, n_y = (lax.axis_size(a) for a in ("x", "z", "y"))
    x, y = lax.axis_index("x"), lax.axis_index("y")
    part = tok // n_x

    hidden = jnp.concatenate([teacher_hidden, student_hidden], axis=1)
    quarter = shift(lax.dynamic_slice_in_dim(hidden, x * part, part, 0), "y", 2)
    after, before = shift(hidden, "y", 1), shift(hidden, "y", 3)
    quarters = jnp.stack([quarter, *(shift(quarter, "x", k) for k in range(1, n_x))])
    opposite = rolled(quarters, n_x - x).reshape(tok, -1)

    table = dequantize(teacher_codes, teacher_scales)
    weight_p = shift(student_weight, "c", 1)
    table_p = shift(table, "c", 1)

    pairs = (jnp.concatenate([hidden, opposite]), jnp.concatenate([after, before]))
    logits, stats = [], []
    for pair in pairs:
        pt, ps = pair[:, :width_t], pair[:, width_t:]
        t = [rows_by_tokens(rows, pt) for rows in (table, table_p)]
        s = [rows_by_tokens(rows, ps) for rows in (student_weight, weight_p)]
        t_top = jnp.maximum(jnp.max(t[0], axis=0), jnp.max(t[1], axis=0))
        s_top = jnp.maximum(jnp.max(s[0], axis=0), jnp.max(s[1], axis=0))
        t_sum = cross = s_sum = 0.0
        for a, b in zip(t, s):
            e = jnp.exp(a - t_top)
            t_sum += jnp.sum(e, axis=0)
            cross += jnp.sum(e * (a - b), axis=0)
            s_sum += jnp.sum(jnp.exp(b - s_top), axis=0)
        logits.append((t, s))
        stats.append(jnp.stack([t_top, t_sum, cross, s_top, s_sum]).reshape(5, 2, tok))
    rel = jnp.stack([stats[0][:, 0], stats[1][:, 0], stats[0][:, 1], stats[1][:, 1]])
    scale_row = loss_scale.astype(F32)[None, None]
    scale_rel = jnp.concatenate([scale_row, jnp.zeros((n_y - 1, 1, tok), F32)])
    block_abs = rolled(jnp.concatenate([rel, scale_rel], axis=1), n_y - y)
    seen = to_all(block_abs.transpose(1, 0, 2).reshape(6, -1), ("x", "y"))
    scales = jnp.sum(seen[:n_y, 5], axis=0)
    totals = combine(to_all(combine(seen), "z"))
    t_lse = totals[0] + jnp.log(totals[1])
    s_lse = totals[3] + jnp.log(totals[4])
    divergence = totals[2] / totals[1] - t_lse + s_lse
    back = rolled(jnp.stack([t_lse, s_lse, scales, divergence]).reshape(4, n_y, tok).transpose(1, 0, 2), y)
    kl = back[0, 3]

    own, other = [], []
    for p, (t, s) in enumerate(logits):
        tl, sl, sc = (jnp.concatenate([back[p, i], back[p + 2, i]]) for i in range(3))
        for k, out in ((0, own), (1, other)):
            out.append((sc * (jnp.exp(s[k] - sl) - jnp.exp(t[k] - tl))).astype(BF16))
    own, other = jnp.concatenate(own, axis=1), jnp.concatenate(other, axis=1)
    from_p = shift(other, "c", 1)
    students = jnp.concatenate([p[:, width_t:] for p in pairs])
    students_p = shift(students, "c", 1)

    def into(rows, tokens):
        return jnp.dot(rows, tokens, preferred_element_type=F32)

    grad_t = lax.dot_general(
        jnp.concatenate([student_weight, weight_p]),
        jnp.concatenate([own, other]),
        (((0,), (0,)), ((), ())),
        preferred_element_type=F32,
    ).astype(BF16)
    blocks = grad_t.reshape(n_x, width_s // n_x, n_y, tok).transpose(2, 0, 1, 3)
    blocks = jnp.stack([blocks[0], blocks[2], blocks[1], blocks[3]])
    blocks = rolled(blocks, n_y - y).transpose(1, 0, 2, 3)
    blocks = blocks.reshape(n_x * n_y, width_s // n_x, tok)
    got = lax.all_to_all(blocks, ("x", "y"), 0, 0, tiled=True)
    got = jnp.sum(got.astype(F32), axis=0).astype(BF16).reshape(n_z, -1, tok)
    got = lax.all_to_all(got, "z", 0, 0, tiled=True)
    grad_hidden = jnp.sum(got.astype(F32), axis=0).astype(BF16).T

    grad_weight = (into(own, students) + into(from_p, students_p)).astype(BF16)
    return kl, grad_hidden, grad_weight


def solution(mesh):
    split = Mesh(mesh.devices.reshape(4, 8, 4, 2), AXES)
    rows = P(("x", "z", "y", "c"), None)
    return jax.shard_map(
        local,
        mesh=split,
        in_specs=(P(DP, None), P(DP, None), rows, rows, rows, P(DP)),
        out_specs=(P(DP), P(DP, VOCAB), rows),
        check_vma=False,
    )
```

time: 299 us -> 222 us (0.74)
  waiting for transfers between devices: 164 us -> 74 us
  blocking collectives: 51.4 us -> 0 us
  starting transfers between devices: 10.2 us -> 39.1 us
  local copies, waits for them, and re-layouts: 14.3 us -> 41.1 us
  matrix products: 27.2 us -> 48.1 us
  between operations: 14.2 us -> 1.22 us
    all_gather x1 -> x0, waiting for transfers between devices: 74.6 us -> none  [in_one_piece(): whole, at, done = (lax.all_gather(both, axis, axis=dim, tiled=True), 0, [])]
    reduce_scatter x1 -> x0, waiting for transfers between devices: 62.1 us -> none  [local(): lax.psum_scatter(jnp.dot(logit_grad, student_weight, preferred_element_ty...]
    all_gather x4 -> x0, blocking collectives: 51.4 us -> none  [all_in_one(): both, at, found = (lax.all_gather(jnp.concatenate(lines), axis), 0, {})]
    ppermute x0 -> x10, waiting for transfers between devices: none -> 36.5 us  [shift(): return lax.ppermute(a, axis, [((i + by) % n, i) for i in range(n)])]
    dot_general x4 -> x11, matrix products: 27.2 us -> 48.1 us  [the longest x8 30.9 us: rows_by_tokens(): lax.dot_general(rows, tokens, (((1,), (1,)), ((), ())), preferred_element...]
    all_to_all x1 -> x4, starting transfers between devices: 10.2 us -> 27.2 us  [the longest x2 14.8 us: to_all(): lax.all_to_all(jnp.broadcast_to(a[None], (n, *a.shape)), axes, 0, 0, tile...]
    ppermute x0 -> x10, starting transfers between devices: none -> 11.9 us  [shift(): return lax.ppermute(a, axis, [((i + by) % n, i) for i in range(n)])]
    all_to_all x1 -> x4, waiting for transfers between devices: 26.8 us -> 37.5 us  [the longest x1 20.6 us: local(): got = lax.all_to_all(blocks, ('x', 'y'), 0, 0, tiled=True)]
  transfers between devices with their start and end apart: 3 -> 14, of which waited for: 3 -> 8; matrix products, arithmetic and copies ran while one was open for 7% -> 38% of each run, Pallas kernels for 0% -> 0%
where the time goes in v1:
time: 222 us; the launch traced here: 221 us
  waiting for transfers between devices  74 us (33%)
  matrix products  48.1 us (22%)
  local copies, waits for them, and re-layouts  41.1 us (19%)
  starting transfers between devices  39.1 us (18%)
  other arithmetic  17.4 us (8%)
    ppermute x10, waiting for transfers between devices, shift(): return lax.ppermute(a, axis, [((i + by) % n, i) for i in range(n)])  36.5 us
    dot_general x8, matrix products, rows_by_tokens(): lax.dot_general(rows, tokens, (((1,), (1,)), ((), ())), preferred_element...  30.9 us
    all_to_all x1, waiting for transfers between devices, local(): got = lax.all_to_all(blocks, ('x', 'y'), 0, 0, tiled=True)  20.6 us
    unnamed x66, local copies, waits for them, and re-layouts  16.7 us
    all_to_all x2, starting transfers between devices, to_all(): lax.all_to_all(jnp.broadcast_to(a[None], (n, *a.shape)), axes, 0, 0, tile...  14.8 us
    all_to_all x2, waiting for transfers between devices, to_all(): lax.all_to_all(jnp.broadcast_to(a[None], (n, *a.shape)), axes, 0, 0, tile...  12.9 us
    ppermute x10, starting transfers between devices, shift(): return lax.ppermute(a, axis, [((i + by) % n, i) for i in range(n)])  11.9 us
    dot_general x2, matrix products, into(): return jnp.dot(rows, tokens, preferred_element_type=F32)  11.1 us
  transfers between devices with their start and end apart: 14, of which 8 were waited for; matrix products, arithmetic and copies ran while one was open for 38% of the time, Pallas kernels for 0%

profile of v1, /device:TPU:8, one launch (start us, length us, event | category | flops | bytes accessed | tf_op | source)
XLA Modules:
  0.0 221.0 jit_solution(8774365778262278394)
XLA Ops:
  9.6 8.3 %copy.55 = bf16[512,5376]{0,1:T(8,128)(2,1)} copy(bf16[512,5376]{1,0:T(8,128)(2,1)} %param.8) | data formatting | bytes 11010048 | tf_op args[2]
  17.9 6.2 %fusion = bf16[512,5376]{0,1:T(8,128)(2,1)} fusion(bf16[512,5376]{0,1:T(8,128)(2,1)} %copy.55, f32[512,42]{0,1:T(8,128)S(1)} %copy-done.19), kind=kLoop, calls=%fused_computation.1 | loop fusion | flops 8257536 | bytes 11096064 | tf_op jit(solution)/shard_map/convert_element_type | solution.py:27
  24.5 2.8 %collective-permute-start.1 = (bf16[32,7936]{1,0:T(8,128)(2,1)S(1)}, bf16[32,7936]{1,0:T(8,128)(2,1)S(1)}, u32[]{:S(2)}, u32[]{:S(2)}) collective-permute-start(bf16[32,7936]{1,0:T(8,128)(2,1)S(1)} %collective-permute-done), channel_id=1, source_target_pairs={{64,0},{128,64},{192,128},{0,192},{65,1},{129,65},{193,129},{1,193... | collective-permute-start | bytes 1523720 | tf_op jit(solution)/shard_map/ppermute | solution.py:16
  27.4 11.0 %collective-permute-done.1 = bf16[32,7936]{1,0:T(8,128)(2,1)S(1)} collective-permute-done((bf16[32,7936]{1,0:T(8,128)(2,1)S(1)}, bf16[32,7936]{1,0:T(8,128)(2,1)S(1)}, u32[]{:S(2)}, u32[]{:S(2)}) %collective-permute-start.1) | collective-permute-done | bytes 507936 | tf_op jit(solution)/shard_map/ppermute | solution.py:16
  41.2 11.4 %collective-permute-done.2 = bf16[32,7936]{1,0:T(8,128)(2,1)S(1)} collective-permute-done((bf16[32,7936]{1,0:T(8,128)(2,1)S(1)}, bf16[32,7936]{1,0:T(8,128)(2,1)S(1)}, u32[]{:S(2)}, u32[]{:S(2)}) %collective-permute-start.2) | collective-permute-done | bytes 507936 | tf_op jit(solution)/shard_map/ppermute | solution.py:16
  53.9 12.3 %collective-permute-done.3 = bf16[32,7936]{1,0:T(8,128)(2,1)S(1)} collective-permute-done((bf16[32,7936]{1,0:T(8,128)(2,1)S(1)}, bf16[32,7936]{1,0:T(8,128)(2,1)S(1)}, u32[]{:S(2)}, u32[]{:S(2)}) %collective-permute-start.3) | collective-permute-done | bytes 507936 | tf_op jit(solution)/shard_map/ppermute | solution.py:16
  72.2 5.4 %fusion.98 = (f32[256]{0:T(256)S(1)}, f32[512,256]{1,0:T(8,128)}) fusion(bf16[512,5376]{0,1:T(8,128)(2,1)} %fusion, bf16[128,7936]{1,0:T(8,128)(2,1)} %constant_dynamic-update-slice_fusion, bf16[128,7936]{1,0:T(8,128)(2,1)S(1)} %bitcast.263), kind=kOutput, calls=%fused_computation.203 | convolution fusion | flops 1414921984 | bytes 10093568 | tf_op jit(solution)/shard_map/dot_general | solution.py:31
  86.9 5.8 %fusion.102 = (f32[256]{0:T(256)S(1)}, f32[512,256]{1,0:T(8,128)}) fusion(bf16[512,5376]{0,1:T(8,128)(2,1)} %fusion, bf16[256,7936]{1,0:T(8,128)(2,1)} %copy-done.7), kind=kOutput, calls=%fused_computation.207 | convolution fusion | flops 1409416960 | bytes 8782848 | tf_op jit(solution)/shard_map/dot_general | solution.py:31
  92.7 3.4 %fusion.101 = (f32[256]{0:T(256)S(1)}, f32[256,512]{1,0:T(8,128)}) fusion(bf16[256,2560]{1,0:T(8,128)(2,1)S(1)} %pad_maximum_fusion.1, bf16[512,2560]{1,0:T(8,128)(2,1)} %collective-permute-done.5), kind=kOutput, calls=%fused_computation.206 | convolution fusion | flops 671219456 | bytes 4457472 | tf_op jit(solution)/shard_map/dot_general | solution.py:31
  98.2 3.8 %fusion.105 = (f32[256]{0:T(256)S(1)}, f32[256,512]{1,0:T(8,128)}) fusion(bf16[512,2560]{1,0:T(8,128)(2,1)} %collective-permute-done.5, bf16[256,7936]{1,0:T(8,128)(2,1)} %copy-done.7), kind=kOutput, calls=%fused_computation.210 | convolution fusion | flops 671219456 | bytes 4457472 | tf_op jit(solution)/shard_map/dot_general | solution.py:31
  104.1 4.8 %fusion.99 = (f32[256]{0:T(256)S(1)}, f32[512,256]{1,0:T(8,128)S(1)}) fusion(bf16[512,5376]{0,1:T(8,128)(2,1)} %collective-permute-done.4, bf16[128,7936]{1,0:T(8,128)(2,1)} %constant_dynamic-update-slice_fusion, bf16[128,7936]{1,0:T(8,128)(2,1)S(1)} %bitcast.264), kind=kOutput, calls=%fused_computation.204 | convolution fusion | flops 1414921984 | bytes 10093568 | tf_op jit(solution)/shard_map/dot_general | solution.py:31
  109.4 4.3 %fusion.103 = (f32[256]{0:T(256)S(1)}, f32[512,256]{1,0:T(8,128)S(1)}) fusion(bf16[512,5376]{0,1:T(8,128)(2,1)} %collective-permute-done.4, bf16[256,7936]{1,0:T(8,128)(2,1)S(1)} %copy-done.8), kind=kOutput, calls=%fused_computation.208 | convolution fusion | flops 1409416960 | bytes 8782848 | tf_op jit(solution)/shard_map/dot_general | solution.py:31
  115.4 6.3 %all-to-all-start = ((f32[16,6,512]{2,1,0:T(8,128)}), f32[16,6,512]{2,1,0:T(8,128)S(1)}, u32[]{:S(2)}, u32[]{:S(2)}) async-start(f32[16,6,512]{2,1,0:T(8,128)} %broadcast_in_dim.11), calls=%async_computation | async-start | bytes 524288 | tf_op jit(solution)/shard_map/all_to_all | solution.py:36
  123.1 5.6 %all-to-all-done = f32[16,6,512]{2,1,0:T(8,128)S(1)} async-done(((f32[16,6,512]{2,1,0:T(8,128)}), f32[16,6,512]{2,1,0:T(8,128)S(1)}, u32[]{:S(2)}, u32[]{:S(2)}) %all-to-all-start) | async-done | bytes 196640 | tf_op jit(solution)/shard_map/all_to_all | solution.py:36
  129.6 8.5 %all-to-all-start.1 = ((f32[8,5,512]{2,1,0:T(8,128)}), f32[8,5,512]{2,1,0:T(8,128)S(1)}, u32[]{:S(2)}, u32[]{:S(2)}) async-start(f32[8,5,512]{2,1,0:T(8,128)} %broadcast_in_dim.12), calls=%async_computation.1 | async-start | bytes 262144 | tf_op jit(solution)/shard_map/all_to_all | solution.py:36
  139.7 7.4 %all-to-all-done.1 = f32[8,5,512]{2,1,0:T(8,128)S(1)} async-done(((f32[8,5,512]{2,1,0:T(8,128)}), f32[8,5,512]{2,1,0:T(8,128)S(1)}, u32[]{:S(2)}, u32[]{:S(2)}) %all-to-all-start.1) | async-done | bytes 81952 | tf_op jit(solution)/shard_map/all_to_all | solution.py:36
  150.8 6.2 %fusion.5 = bf16[2560,512]{1,0:T(8,128)(2,1)} fusion(bf16[512,2560]{1,0:T(8,128)(2,1)} %collective-permute-done.5, bf16[512,2560]{1,0:T(8,128)(2,1)S(1)} %copy-done.23, bf16[512,256]{1,0:T(8,128)(2,1)S(1)} %get-tuple-element.63, bf16[512,256]{1,0:T(8,128)(2,1)S(1)} %get-tuple-element.61, bf16[512,256]{1,0:T(8,128)(2,1)S(1)} %get-tuple-element.62, ...), kind=kOutput, calls=%fused_computation.7 | convolution fusion | flops 2700345344 | bytes 8912896 | tf_op jit(solution)/shard_map/dot_general | solution.py:116
  157.0 4.9 %reshape.357 = bf16[4,640,4,128]{3,2,1,0:T(4,128)(2,1)} reshape(bf16[2560,512]{1,0:T(8,128)(2,1)} %fusion.5) | data formatting | bytes 5242880 | tf_op jit(solution)/shard_map/reshape | solution.py:122
  166.5 5.9 %all-to-all-start.2 = ((bf16[16,640,128]{2,1,0:T(8,128)(2,1)}), bf16[16,640,128]{2,1,0:T(8,128)(2,1)}, u32[]{:S(2)}, u32[]{:S(2)}) async-start(bf16[16,640,128]{2,1,0:T(8,128)(2,1)} %bitcast.261), calls=%async_computation.2 | async-start | bytes 5242880 | tf_op jit(solution)/shard_map/all_to_all | solution.py:126
  175.4 5.6 %fusion.106 = f32[512,2560]{1,0:T(8,128)} fusion(bf16[512,512]{1,0:T(8,128)(2,1)S(1)} %collective-permute-done.8, bf16[512,2560]{1,0:T(8,128)(2,1)} %collective-permute-done.9), kind=kOutput, calls=%fused_computation.211 | convolution fusion | flops 1342177280 | bytes 8388608 | tf_op jit(solution)/shard_map/dot_general | solution.py:114
  181.0 20.6 %all-to-all-done.2 = bf16[16,640,128]{2,1,0:T(8,128)(2,1)} async-done(((bf16[16,640,128]{2,1,0:T(8,128)(2,1)}), bf16[16,640,128]{2,1,0:T(8,128)(2,1)}, u32[]{:S(2)}, u32[]{:S(2)}) %all-to-all-start.2) | async-done | bytes 2621472 | tf_op jit(solution)/shard_map/all_to_all | solution.py:126
  204.4 6.5 %all-to-all-start.3 = ((bf16[8,80,128]{2,1,0:T(8,128)(2,1)}), bf16[8,80,128]{2,1,0:T(8,128)(2,1)S(1)}, u32[]{:S(2)}, u32[]{:S(2)}) async-start(bf16[8,80,128]{2,1,0:T(8,128)(2,1)} %bitcast.59), calls=%async_computation.3 | async-start | bytes 327680 | tf_op jit(solution)/shard_map/all_to_all | solution.py:128
  210.9 5.5 %add_convert_fusion = bf16[512,2560]{1,0:T(8,128)(2,1)} fusion(f32[512,2560]{1,0:T(8,128)} %fusion.106, bf16[512,256]{1,0:T(8,128)(2,1)S(1)} %get-tuple-element.62, bf16[512,256]{1,0:T(8,128)(2,1)S(1)} %get-tuple-element.60, bf16[256,2560]{1,0:T(8,128)(2,1)S(1)} %slice.166, bf16[256,2560]{1,0:T(8,128)(2,1)S(1)} %pad_maximum_fusion.1), kind=kOutput, calls=%fused_computation.6 | convolution fusion | flops 1351090176 | bytes 11010048 | tf_op jit(solution)/shard_map/dot_general | solution.py:114
  216.4 3.9 %all-to-all-done.3 = bf16[8,80,128]{2,1,0:T(8,128)(2,1)S(1)} async-done(((bf16[8,80,128]{2,1,0:T(8,128)(2,1)}), bf16[8,80,128]{2,1,0:T(8,128)(2,1)S(1)}, u32[]{:S(2)}, u32[]{:S(2)}) %all-to-all-start.3) | async-done | bytes 163872 | tf_op jit(solution)/shard_map/all_to_all | solution.py:128
  (141 shorter events, 53.5 us)
Async XLA Ops:
  5.2 12.7 %copy-start.19 = (f32[512,42]{0,1:T(8,128)S(1)}, f32[512,42]{0,1:T(8,128)}, u32[]{:S(2)}) copy-start(f32[512,42]{0,1:T(8,128)} %param.9) | copy-start | bytes 258052
  5.2 19.4 %collective-permute-start = (bf16[32,7936]{1,0:T(8,128)(2,1)S(1)}, bf16[32,7936]{1,0:T(8,128)(2,1)S(1)}, u32[]{:S(2)}, u32[]{:S(2)}) collective-permute-start(bf16[32,7936]{1,0:T(8,128)(2,1)S(1)} %constant_dynamic-slice_fusion.2), channel_id=1, source_target_pairs={{4,0},{6,2},{0,4},{2,6},{5,1},{7,3},{1,5},{3,7},{12,8},{14,10},{8,... | collective-permute-start | bytes 1523720 | tf_op jit(solution)/shard_map/ppermute | solution.py:16
  7.6 70.0 %collective-permute-start.6 = (bf16[128,7936]{1,0:T(8,128)(2,1)}, bf16[128,7936]{1,0:T(8,128)(2,1)}, u32[]{:S(2)}, u32[]{:S(2)}) collective-permute-start(bf16[128,7936]{1,0:T(8,128)(2,1)} %constant_dynamic-update-slice_fusion), channel_id=1, source_target_pairs={{2,0},{4,2},{6,4},{0,6},{3,1},{5,3},{7,5},{1,7},{10,8},{12,10},{14... | collective-permute-start | bytes 6094856 | tf_op jit(solution)/shard_map/ppermute | solution.py:16
  8.9 70.4 %collective-permute-start.7 = (bf16[128,7936]{1,0:T(8,128)(2,1)}, bf16[128,7936]{1,0:T(8,128)(2,1)}, u32[]{:S(2)}, u32[]{:S(2)}) collective-permute-start(bf16[128,7936]{1,0:T(8,128)(2,1)} %constant_dynamic-update-slice_fusion), channel_id=1, source_target_pairs={{6,0},{0,2},{2,4},{4,6},{7,1},{1,3},{3,5},{5,7},{14,8},{8,10},{10,... | collective-permute-start | bytes 6094856 | tf_op jit(solution)/shard_map/ppermute | solution.py:16
  9.6 83.1 %collective-permute-start.5 = (bf16[512,2560]{1,0:T(8,128)(2,1)}, bf16[512,2560]{1,0:T(8,128)(2,1)}, u32[]{:S(2)}, u32[]{:S(2)}) collective-permute-start(bf16[512,2560]{1,0:T(8,128)(2,1)} %param.10), channel_id=1, source_target_pairs={{1,0},{0,1},{3,2},{2,3},{5,4},{4,5},{7,6},{6,7},{9,8},{8,9},{11,10... | collective-permute-start | bytes 7864328 | tf_op jit(solution)/shard_map/ppermute | solution.py:16
  17.9 6.7 %copy-start.20 = (bf16[128]{0:T(256)(128)(2,1)S(1)}, bf16[128]{0:T(256)(128)(2,1)}, u32[]{:S(2)}) copy-start(bf16[128]{0:T(256)(128)(2,1)} %param.11) | copy-start | bytes 772
  24.0 80.0 %collective-permute-start.4 = (bf16[512,5376]{0,1:T(8,128)(2,1)}, bf16[512,5376]{0,1:T(8,128)(2,1)}, u32[]{:S(2)}, u32[]{:S(2)}) collective-permute-start(bf16[512,5376]{0,1:T(8,128)(2,1)} %fusion), channel_id=1, source_target_pairs={{1,0},{0,1},{3,2},{2,3},{5,4},{4,5},{7,6},{6,7},{9,8},{8,9},{11,10... | collective-permute-start | bytes 16515080 | tf_op jit(solution)/shard_map/ppermute | solution.py:16
  24.5 13.8 %collective-permute-start.1 = (bf16[32,7936]{1,0:T(8,128)(2,1)S(1)}, bf16[32,7936]{1,0:T(8,128)(2,1)S(1)}, u32[]{:S(2)}, u32[]{:S(2)}) collective-permute-start(bf16[32,7936]{1,0:T(8,128)(2,1)S(1)} %collective-permute-done), channel_id=1, source_target_pairs={{64,0},{128,64},{192,128},{0,192},{65,1},{129,65},{193,129},{1,193... | collective-permute-start | bytes 1523720 | tf_op jit(solution)/shard_map/ppermute | solution.py:16
  38.4 14.1 %collective-permute-start.2 = (bf16[32,7936]{1,0:T(8,128)(2,1)S(1)}, bf16[32,7936]{1,0:T(8,128)(2,1)S(1)}, u32[]{:S(2)}, u32[]{:S(2)}) collective-permute-start(bf16[32,7936]{1,0:T(8,128)(2,1)S(1)} %collective-permute-done), channel_id=1, source_target_pairs={{128,0},{192,64},{0,128},{64,192},{129,1},{193,65},{1,129},{65,193... | collective-permute-start | bytes 1523720 | tf_op jit(solution)/shard_map/ppermute | solution.py:16
  52.5 13.7 %collective-permute-start.3 = (bf16[32,7936]{1,0:T(8,128)(2,1)S(1)}, bf16[32,7936]{1,0:T(8,128)(2,1)S(1)}, u32[]{:S(2)}, u32[]{:S(2)}) collective-permute-start(bf16[32,7936]{1,0:T(8,128)(2,1)S(1)} %collective-permute-done), channel_id=1, source_target_pairs={{192,0},{0,64},{64,128},{128,192},{193,1},{1,65},{65,129},{129,193... | collective-permute-start | bytes 1523720 | tf_op jit(solution)/shard_map/ppermute | solution.py:16
  104.0 4.8 %copy-start = (f32[256,512]{0,1:T(8,128)S(1)}, f32[256,512]{0,1:T(8,128)}, u32[]{:S(2)}) copy-start(f32[256,512]{0,1:T(8,128)} %copy.56) | copy-start | bytes 1572868
  104.0 4.8 %copy-start.6 = (f32[256,512]{0,1:T(8,128)S(1)}, f32[256,512]{0,1:T(8,128)}, u32[]{:S(2)}) copy-start(f32[256,512]{0,1:T(8,128)} %copy.57) | copy-start | bytes 1572868
  104.0 4.8 %copy-start.9 = (f32[512,256]{1,0:T(8,128)S(1)}, f32[512,256]{1,0:T(8,128)}, u32[]{:S(2)}) copy-start(f32[512,256]{1,0:T(8,128)} %get-tuple-element.67) | copy-start | bytes 1572868
  104.0 5.3 %copy-start.8 = (bf16[256,7936]{1,0:T(8,128)(2,1)S(1)}, bf16[256,7936]{1,0:T(8,128)(2,1)}, u32[]{:S(2)}) copy-start(bf16[256,7936]{1,0:T(8,128)(2,1)} %copy-done.7) | copy-start | bytes 12189700
  108.8 4.9 %copy-start.12 = (f32[512,256]{1,0:T(8,128)}, f32[512,256]{1,0:T(8,128)S(1)}, u32[]{:S(2)}) copy-start(f32[512,256]{1,0:T(8,128)S(1)} %get-tuple-element.69) | copy-start | bytes 1572868
  115.4 13.3 %all-to-all-start = ((f32[16,6,512]{2,1,0:T(8,128)}), f32[16,6,512]{2,1,0:T(8,128)S(1)}, u32[]{:S(2)}, u32[]{:S(2)}) async-start(f32[16,6,512]{2,1,0:T(8,128)} %broadcast_in_dim.11), calls=%async_computation | async-start | bytes 524288 | tf_op jit(solution)/shard_map/all_to_all | solution.py:36
  129.6 17.5 %all-to-all-start.1 = ((f32[8,5,512]{2,1,0:T(8,128)}), f32[8,5,512]{2,1,0:T(8,128)S(1)}, u32[]{:S(2)}, u32[]{:S(2)}) async-start(f32[8,5,512]{2,1,0:T(8,128)} %broadcast_in_dim.12), calls=%async_computation.1 | async-start | bytes 262144 | tf_op jit(solution)/shard_map/all_to_all | solution.py:36
  138.0 9.9 %copy-start.1 = (f32[256,512]{0,1:T(8,128)S(1)}, f32[256,512]{0,1:T(8,128)}, u32[]{:S(2)}) copy-start(f32[256,512]{0,1:T(8,128)} %copy.56) | copy-start | bytes 1572868
  139.7 33.8 %collective-permute-start.9 = (bf16[512,2560]{1,0:T(8,128)(2,1)}, bf16[512,2560]{1,0:T(8,128)(2,1)}, u32[]{:S(2)}, u32[]{:S(2)}) collective-permute-start(bf16[512,2560]{1,0:T(8,128)(2,1)} %pad_maximum_fusion), channel_id=1, source_target_pairs={{1,0},{0,1},{3,2},{2,3},{5,4},{4,5},{7,6},{6,7},{9,8},{8,9},{11,10... | collective-permute-start | bytes 7864328 | tf_op jit(solution)/shard_map/ppermute | solution.py:16
  150.4 6.6 %copy-start.17 = (bf16[512,256]{1,0:T(8,128)(2,1)}, bf16[512,256]{1,0:T(8,128)(2,1)S(1)}, u32[]{:S(2)}) copy-start(bf16[512,256]{1,0:T(8,128)(2,1)S(1)} %get-tuple-element.63) | copy-start | bytes 786436
  166.5 5.9 %copy-start.16 = (bf16[512,256]{1,0:T(8,128)(2,1)S(1)}, bf16[512,256]{1,0:T(8,128)(2,1)}, u32[]{:S(2)}) copy-start(bf16[512,256]{1,0:T(8,128)(2,1)} %copy-done.15) | copy-start | bytes 786436
  166.5 35.1 %all-to-all-start.2 = ((bf16[16,640,128]{2,1,0:T(8,128)(2,1)}), bf16[16,640,128]{2,1,0:T(8,128)(2,1)}, u32[]{:S(2)}, u32[]{:S(2)}) async-start(bf16[16,640,128]{2,1,0:T(8,128)(2,1)} %bitcast.261), calls=%async_computation.2 | async-start | bytes 5242880 | tf_op jit(solution)/shard_map/all_to_all | solution.py:126
  173.4 2.0 collective-permute-start.8
  204.4 16.0 %all-to-all-start.3 = ((bf16[8,80,128]{2,1,0:T(8,128)(2,1)}), bf16[8,80,128]{2,1,0:T(8,128)(2,1)S(1)}, u32[]{:S(2)}, u32[]{:S(2)}) async-start(bf16[8,80,128]{2,1,0:T(8,128)(2,1)} %bitcast.59), calls=%async_computation.3 | async-start | bytes 327680 | tf_op jit(solution)/shard_map/all_to_all | solution.py:128
  (14 other events, 40.7 us)

commit v2 on v1

v2 whole, which is shorter than its diff:
```python
import functools

import jax
import jax.numpy as jnp
from jax import lax
from jax.experimental import pallas as pl
from jax.experimental.pallas import tpu as pltpu
from jax.sharding import Mesh
from jax.sharding import PartitionSpec as P

GROUP = 128
AXES = ("x", "z", "y", "c")
DP = ("y", "c")
VOCAB = ("x", "z")
F32, BF16 = jnp.float32, jnp.bfloat16


def shift(a, axis, by):
    n = lax.axis_size(axis)
    return lax.ppermute(a, axis, [((i + by) % n, i) for i in range(n)])


def rolled(blocks, start):
    n = blocks.shape[0]
    return lax.dynamic_slice_in_dim(jnp.concatenate([blocks, blocks[:-1]]), start % n, n, 0)


NT = (((1,), (1,)), ((), ()))
VMEM_LIMIT = 56 * 1024 * 1024
DEQUANT_ROWS = 128
LOGIT_ROWS = 256


def dequant_kernel(own_steps, own_ref, other_ref, own_scale_ref, other_scale_ref, out_ref):
    def write(codes_ref, scale_ref):
        for g in range(codes_ref.shape[1] // GROUP):
            at = slice(g * GROUP, (g + 1) * GROUP)
            wide = codes_ref[:, at].astype(F32) * scale_ref[:, g : g + 1]
            out_ref[:, at] = wide.astype(BF16)

    @pl.when(pl.program_id(0) < own_steps)
    def _():
        write(own_ref, own_scale_ref)

    @pl.when(pl.program_id(0) >= own_steps)
    def _():
        write(other_ref, other_scale_ref)


def dequantize(codes, codes_p, scales, scales_p):
    rows, width = codes.shape
    steps = rows // DEQUANT_ROWS

    def own(i):
        return (jnp.minimum(i, steps - 1), 0)

    def other(i):
        return (jnp.maximum(i - steps, 0), 0)

    return pl.pallas_call(
        functools.partial(dequant_kernel, steps),
        grid=(2 * steps,),
        in_specs=[
            pl.BlockSpec((DEQUANT_ROWS, width), own),
            pl.BlockSpec((DEQUANT_ROWS, width), other),
            pl.BlockSpec((DEQUANT_ROWS, scales.shape[1]), own),
            pl.BlockSpec((DEQUANT_ROWS, scales.shape[1]), other),
        ],
        out_specs=pl.BlockSpec((DEQUANT_ROWS, width), lambda i: (i, 0)),
        out_shape=jax.ShapeDtypeStruct((2 * rows, width), BF16),
        compiler_params=pltpu.CompilerParams(vmem_limit_bytes=VMEM_LIMIT),
        cost_estimate=pl.CostEstimate(
            flops=2 * rows * width, transcendentals=0, bytes_accessed=8 * rows * width
        ),
        name="dequantize",
    )(codes, codes_p, scales, scales_p)


def logits_kernel(width_t, a_hbm, b_hbm, table_ref, weight_ref, t_ref, s_ref, stat_ref, pair, sem):
    step = pl.program_id(0)
    tok = a_hbm.shape[0]

    @pl.when(step == 0)
    def _():
        copies = [
            pltpu.make_async_copy(a_hbm, pair.at[pl.ds(0, tok)], sem.at[0]),
            pltpu.make_async_copy(b_hbm, pair.at[pl.ds(tok, tok)], sem.at[1]),
        ]
        for copy in copies:
            copy.start()
        for copy in copies:
            copy.wait()

    t = lax.dot_general(table_ref[...], pair[:, :width_t], NT, preferred_element_type=F32)
    s = lax.dot_general(weight_ref[...], pair[:, width_t:], NT, preferred_element_type=F32)
    t_ref[...] = t
    s_ref[...] = s
    t_top = jnp.max(t, axis=0, keepdims=True)
    s_top = jnp.max(s, axis=0, keepdims=True)

    def sums(t_top, s_top):
        e = jnp.exp(t - t_top)
        return (
            jnp.sum(e, axis=0, keepdims=True),
            jnp.sum(e * (t - s), axis=0, keepdims=True),
            jnp.sum(jnp.exp(s - s_top), axis=0, keepdims=True),
        )

    @pl.when(step == 0)
    def _():
        total, cross, s_total = sums(t_top, s_top)
        for k, row in enumerate((t_top, total, cross, s_top, s_total)):
            stat_ref[k : k + 1] = row
        stat_ref[5:8] = jnp.zeros((3, t.shape[1]), F32)

    @pl.when(step > 0)
    def _():
        t_old, s_old = stat_ref[0:1], stat_ref[3:4]
        t_new, s_new = jnp.maximum(t_old, t_top), jnp.maximum(s_old, s_top)
        total, cross, s_total = sums(t_new, s_new)
        t_keep, s_keep = jnp.exp(t_old - t_new), jnp.exp(s_old - s_new)
        stat_ref[0:1] = t_new
        stat_ref[1:2] = stat_ref[1:2] * t_keep + total
        stat_ref[2:3] = stat_ref[2:3] * t_keep + cross
        stat_ref[3:4] = s_new
        stat_ref[4:5] = stat_ref[4:5] * s_keep + s_total


def logits_of(a, b, table, weight):
    rows, width_t = table.shape
    width_s = weight.shape[1]
    tokens = 2 * a.shape[0]
    tile = jax.ShapeDtypeStruct((rows, tokens), F32)
    return pl.pallas_call(
        functools.partial(logits_kernel, width_t),
        grid=(rows // LOGIT_ROWS,),
        in_specs=[
            pl.BlockSpec(memory_space=pl.ANY),
            pl.BlockSpec(memory_space=pl.ANY),
            pl.BlockSpec((LOGIT_ROWS, width_t), lambda i: (i, 0)),
            pl.BlockSpec((LOGIT_ROWS, width_s), lambda i: (i, 0)),
        ],
        out_specs=[
            pl.BlockSpec((LOGIT_ROWS, tokens), lambda i: (i, 0)),
            pl.BlockSpec((LOGIT_ROWS, tokens), lambda i: (i, 0)),
            pl.BlockSpec((8, tokens), lambda i: (0, 0)),
        ],
        out_shape=[tile, tile, jax.ShapeDtypeStruct((8, tokens), F32)],
        scratch_shapes=[
            pltpu.VMEM((tokens, width_t + width_s), BF16),
            pltpu.SemaphoreType.DMA((2,)),
        ],
        compiler_params=pltpu.CompilerParams(vmem_limit_bytes=VMEM_LIMIT),
        cost_estimate=pl.CostEstimate(
            flops=2 * rows * tokens * (width_t + width_s),
            transcendentals=2 * rows * tokens,
            bytes_accessed=2 * (rows + tokens) * (width_t + width_s) + 8 * rows * tokens,
        ),
        name="logits",
    )(a, b, table, weight)


def grad_kernel(y_ref, rows_ref, t0, s0, t1, s1, turned_ref, own_ref, other_ref, out_ref):
    half = own_ref.shape[0]
    n_y, tok = out_ref.shape[1], out_ref.shape[3]

    @pl.when(pl.program_id(0) == 0)
    def _():
        for p, (t, s) in enumerate(((t0, s0), (t1, s1))):
            at = slice(2 * p * tok, 2 * (p + 1) * tok)
            t_lse, s_lse, scale = (rows_ref[k : k + 1, at] for k in range(3))
            for q, ref in enumerate((own_ref, other_ref)):
                rows = slice(q * half, (q + 1) * half)
                gap = jnp.exp(s[rows] - s_lse) - jnp.exp(t[rows] - t_lse)
                ref[:, at] = (scale * gap).astype(BF16)

    total = jnp.dot(turned_ref[:, :half], own_ref[...], preferred_element_type=F32)
    total += jnp.dot(turned_ref[:, half:], other_ref[...], preferred_element_type=F32)
    for k, r in enumerate((0, 2, 1, 3)):
        at = lax.rem(y_ref[0] + r, n_y)
        out_ref[0, at] = total[:, k * tok : (k + 1) * tok].astype(BF16)


def gradients(y, rows, logits, turned, n_x, n_y):
    (t0, s0), (t1, s1) = logits
    vocab, tokens = t0.shape
    width = turned.shape[0]
    lg = jax.ShapeDtypeStruct((vocab // 2, 2 * tokens), BF16)
    whole = pl.BlockSpec((vocab, tokens), lambda i, y: (0, 0))
    lg_spec = pl.BlockSpec((vocab // 2, 2 * tokens), lambda i, y: (0, 0))
    cut = (width // n_x, 2 * tokens // n_y)
    return pl.pallas_call(
        grad_kernel,
        grid_spec=pltpu.PrefetchScalarGridSpec(
            num_scalar_prefetch=1,
            grid=(n_x,),
            in_specs=[
                pl.BlockSpec(rows.shape, lambda i, y: (0, 0)),
                whole,
                whole,
                whole,
                whole,
                pl.BlockSpec((width // n_x, vocab), lambda i, y: (i, 0)),
            ],
            out_specs=[lg_spec, lg_spec, pl.BlockSpec((1, n_y, *cut), lambda i, y: (i, 0, 0, 0))],
        ),
        out_shape=[lg, lg, jax.ShapeDtypeStruct((n_x, n_y, *cut), BF16)],
        compiler_params=pltpu.CompilerParams(vmem_limit_bytes=VMEM_LIMIT),
        cost_estimate=pl.CostEstimate(
            flops=4 * vocab * tokens * width,
            transcendentals=4 * vocab * tokens,
            bytes_accessed=2 * width * (vocab + 2 * tokens) + 20 * vocab * tokens,
        ),
        name="gradients",
    )(y, rows, t0, s0, t1, s1, turned)


def to_all(a, axes):
    n = lax.axis_size(axes)
    return lax.all_to_all(jnp.broadcast_to(a[None], (n, *a.shape)), axes, 0, 0, tiled=True)


def combine(stats):
    teacher_top = jnp.max(stats[:, 0], axis=0)
    student_top = jnp.max(stats[:, 3], axis=0)
    teacher_factor = jnp.exp(stats[:, 0] - teacher_top)
    student_factor = jnp.exp(stats[:, 3] - student_top)
    return jnp.stack(
        [
            teacher_top,
            jnp.sum(stats[:, 1] * teacher_factor, axis=0),
            jnp.sum(stats[:, 2] * teacher_factor, axis=0),
            student_top,
            jnp.sum(stats[:, 4] * student_factor, axis=0),
        ]
    )


def local(
    teacher_hidden, student_hidden, teacher_codes, teacher_scales, student_weight, loss_scale
):
    tok, width_t = teacher_hidden.shape
    width_s = student_hidden.shape[1]
    n_x, n_z, n_y = (lax.axis_size(a) for a in ("x", "z", "y"))
    x, y = lax.axis_index("x"), lax.axis_index("y")
    part = tok // n_x

    hidden = jnp.concatenate([teacher_hidden, student_hidden], axis=1)
    quarter = shift(lax.dynamic_slice_in_dim(hidden, x * part, part, 0), "y", 2)
    after, before = shift(hidden, "y", 1), shift(hidden, "y", 3)
    codes_p = shift(teacher_codes, "c", 1)
    weight_p = shift(student_weight, "c", 1)
    scales_p = shift(teacher_scales, "c", 1)
    quarter, codes_p, weight_p, scales_p = lax.optimization_barrier(
        (quarter, codes_p, weight_p, scales_p)
    )
    quarters = jnp.stack([quarter, *(shift(quarter, "x", k) for k in range(1, n_x))])
    opposite = rolled(quarters, n_x - x).reshape(tok, -1)

    table = dequantize(teacher_codes, codes_p, teacher_scales, scales_p)
    weight = jnp.concatenate([student_weight, weight_p])
    turned = weight.T

    t0, s0, stats0 = logits_of(hidden, opposite, table, weight)
    t1, s1, stats1 = logits_of(after, before, table, weight)
    pieces = [stats0[:, :tok], stats1[:, :tok], stats0[:, tok:], stats1[:, tok:]]
    row = lax.broadcasted_iota(jnp.int32, (8, tok), 0)
    pieces[0] = jnp.where(row == 5, loss_scale.astype(F32)[None], pieces[0])
    twice = jnp.concatenate(pieces + pieces[:-1], axis=1)
    mine = lax.dynamic_slice_in_dim(twice, lax.rem(n_y - y, n_y) * tok, n_y * tok, 1)
    seen = to_all(mine, ("x", "y"))
    scales = jnp.sum(seen[:n_y, 5], axis=0)
    totals = combine(to_all(combine(seen), "z"))
    t_lse = totals[0] + jnp.log(totals[1])
    s_lse = totals[3] + jnp.log(totals[4])
    divergence = totals[2] / totals[1] - t_lse + s_lse
    found = jnp.stack([t_lse, s_lse, scales, divergence])
    found = jnp.concatenate([found, jnp.zeros_like(found)])
    found = jnp.concatenate([found, found[:, : (n_y - 1) * tok]], axis=1)
    found = lax.dynamic_slice_in_dim(found, y * tok, n_y * tok, 1)
    kl = found[3, :tok]
    order = [found[:, k * tok : (k + 1) * tok] for k in (0, 2, 1, 3)]
    own, other, blocks = gradients(
        y.astype(jnp.int32)[None],
        jnp.concatenate(order, axis=1),
        ((t0, s0), (t1, s1)),
        turned,
        n_x,
        n_y,
    )
    from_p = shift(other, "c", 1)
    students = jnp.concatenate([p[:, width_t:] for p in (hidden, opposite, after, before)])
    students_p = shift(students, "c", 1)

    blocks = blocks.reshape(n_x * n_y, width_s // n_x, tok)
    got = lax.all_to_all(blocks, ("x", "y"), 0, 0, tiled=True)
    got = jnp.sum(got.astype(F32), axis=0).astype(BF16).reshape(n_z, -1, tok)
    got = lax.all_to_all(got, "z", 0, 0, tiled=True)
    grad_hidden = jnp.sum(got.astype(F32), axis=0).astype(BF16).T

    grad_weight = jnp.dot(own, students, preferred_element_type=F32)
    grad_weight += jnp.dot(from_p, students_p, preferred_element_type=F32)
    return kl, grad_hidden, grad_weight.astype(BF16)


def solution(mesh):
    split = Mesh(mesh.devices.reshape(4, 8, 4, 2), AXES)
    rows = P(("x", "z", "y", "c"), None)
    return jax.shard_map(
        local,
        mesh=split,
        in_specs=(P(DP, None), P(DP, None), rows, rows, rows, P(DP)),
        out_specs=(P(DP), P(DP, VOCAB), rows),
        check_vma=False,
    )
```

time: 222 us -> 201 us (0.905)
  Pallas kernels: 0 us -> 46.4 us
  matrix products: 48.1 us -> 11.9 us
  waiting for transfers between devices: 74 us -> 59.2 us
  local copies, waits for them, and re-layouts: 41.1 us -> 34.2 us
  starting transfers between devices: 39.1 us -> 33.6 us
  other arithmetic: 17.4 us -> 12.9 us
    pallas_call x0 -> x4, Pallas kernels: none -> 46.4 us  [the longest x2 24.9 us: logits_of(): pl.pallas_call(functools.partial(logits_kernel, width_t), grid=(rows // L...]
    dot_general x11 -> x2, matrix products: 48.1 us -> 11.9 us  [the longest x1 6.29 us: local(): grad_weight = jnp.dot(own, students, preferred_element_type=F32)]
    ppermute x10 -> x11, waiting for transfers between devices: 36.5 us -> 21 us  [shift(): return lax.ppermute(a, axis, [((i + by) % n, i) for i in range(n)])]
    convert_element_type x3 -> x1, other arithmetic: 8.55 us -> 0.01 us  [local(): pieces[0] = jnp.where(row == 5, loss_scale.astype(F32)[None], pieces[0])]
    dot_general x4 -> x0, local copies, waits for them, and re-layouts: 8.13 us -> none  [rows_by_tokens(): lax.dot_general(rows, tokens, (((1,), (1,)), ((), ())), preferred_element...]
    reshape x2 -> x0, local copies, waits for them, and re-layouts: 7.16 us -> none  [local(): blocks = grad_t.reshape(n_x, width_s // n_x, n_y, tok).transpose(2, 0, 1, 3)]
    transpose x1, other arithmetic: 0.02 us -> 7.06 us  [local(): turned = weight.T]
    concatenate x1 -> x3, local copies, waits for them, and re-layouts: 1.85 us -> 8.58 us  [the longest x1 7.86 us: local(): weight = jnp.concatenate([student_weight, weight_p])]
  transfers between devices with their start and end apart: 14 -> 15, of which waited for: 8 -> 9; matrix products, arithmetic and copies ran while one was open for 38% -> 24% of each run, Pallas kernels for 0% -> 17%
where the time goes in v2:
time: 201 us; the launch traced here: 199 us
  waiting for transfers between devices  59.2 us (29%)
  Pallas kernels  46.4 us (23%)
  local copies, waits for them, and re-layouts  34.2 us (17%)
  starting transfers between devices  33.6 us (17%)
  other arithmetic  12.9 us (6%)
  matrix products  11.9 us (6%)
    pallas_call x2, Pallas kernels, logits_of(): pl.pallas_call(functools.partial(logits_kernel, width_t), grid=(rows // L...  24.9 us
    all_to_all x1, waiting for transfers between devices, local(): got = lax.all_to_all(blocks, ('x', 'y'), 0, 0, tiled=True)  24.4 us
    ppermute x11, waiting for transfers between devices, shift(): return lax.ppermute(a, axis, [((i + by) % n, i) for i in range(n)])  21 us
    all_to_all x2, starting transfers between devices, to_all(): lax.all_to_all(jnp.broadcast_to(a[None], (n, *a.shape)), axes, 0, 0, tile...  15.7 us
    unnamed x29, local copies, waits for them, and re-layouts  14.5 us
    pallas_call x1, Pallas kernels, dequantize(): pl.pallas_call(functools.partial(dequant_kernel, steps), grid=(2 * steps,...  12.9 us
    all_to_all x2, waiting for transfers between devices, to_all(): lax.all_to_all(jnp.broadcast_to(a[None], (n, *a.shape)), axes, 0, 0, tile...  10.8 us
    ppermute x11, starting transfers between devices, shift(): return lax.ppermute(a, axis, [((i + by) % n, i) for i in range(n)])  9.48 us
  transfers between devices with their start and end apart: 15, of which 9 were waited for; matrix products, arithmetic and copies ran while one was open for 24% of the time, Pallas kernels for 17%

profile of v2, /device:TPU:8, one launch (start us, length us, event | category | flops | bytes accessed | tf_op | source)
XLA Modules:
  0.0 199.1 jit_solution(9140521565149105271)
XLA Ops:
  0.7 3.1 %copy.27 = bf16[512,2560]{0,1:T(8,128)(2,1)S(1)} copy(bf16[512,2560]{1,0:T(8,128)(2,1)} %param.10) | data formatting | bytes 5242880 | tf_op args[4]
  4.3 2.5 %constant_dynamic-update-slice_fusion.1 = bf16[128,7936]{1,0:T(8,128)(2,1)} fusion(bf16[128,5376]{1,0:T(8,128)(2,1)} %param.6), kind=kLoop, calls=%fused_computation.11 | loop fusion | bytes 2752512
  7.7 1.9 constant_dynamic-slice_fusion.2
  9.6 2.3 %collective-permute-start = (bf16[32,7936]{1,0:T(8,128)(2,1)}, bf16[32,7936]{1,0:T(8,128)(2,1)}, u32[]{:S(2)}, u32[]{:S(2)}) collective-permute-start(bf16[32,7936]{1,0:T(8,128)(2,1)} %constant_dynamic-slice_fusion.2), channel_id=1, source_target_pairs={{4,0},{6,2},{0,4},{2,6},{5,1},{7,3},{1,5},{3,7},{12,8},{14,10},{8,... | collective-permute-start | bytes 1523720 | tf_op jit(solution)/shard_map/ppermute | solution.py:20
  16.7 9.2 %collective-permute-done = bf16[32,7936]{1,0:T(8,128)(2,1)} collective-permute-done((bf16[32,7936]{1,0:T(8,128)(2,1)}, bf16[32,7936]{1,0:T(8,128)(2,1)}, u32[]{:S(2)}, u32[]{:S(2)}) %collective-permute-start) | collective-permute-done | bytes 507936 | tf_op jit(solution)/shard_map/ppermute | solution.py:20
  25.9 2.8 %collective-permute-start.4 = (bf16[32,7936]{1,0:T(8,128)(2,1)}, bf16[32,7936]{1,0:T(8,128)(2,1)}, u32[]{:S(2)}, u32[]{:S(2)}) collective-permute-start(bf16[32,7936]{1,0:T(8,128)(2,1)} %collective-permute-done), channel_id=1, source_target_pairs={{64,0},{128,64},{192,128},{0,192},{65,1},{129,65},{193,129},{1,193... | collective-permute-start | bytes 1523720 | tf_op jit(solution)/shard_map/ppermute | solution.py:20
  30.3 1.9 bitcast_dynamic-update-slice_fusion.5
  32.2 7.1 %fusion.19 = (bf16[2560,1024]{1,0:T(8,128)(2,1)}, bf16[1024,2560]{0,1:T(8,128)(2,1)}) fusion(bf16[512,2560]{0,1:T(8,128)(2,1)} %collective-permute-done.2, bf16[512,2560]{0,1:T(8,128)(2,1)S(1)} %copy.27), kind=kLoop, calls=%fused_computation.63 | loop fusion | flops 10485760 | bytes 15728640 | tf_op jit(solution)/shard_map/transpose | solution.py:262
  39.3 7.9 %copy.31.weight_ref = bf16[1024,2560]{1,0:T(8,128)(2,1)} copy(bf16[1024,2560]{0,1:T(8,128)(2,1)} %get-tuple-element.38) | data formatting | bytes 10485760 | tf_op jit(solution)/shard_map/concatenate | solution.py:261
  47.2 12.9 %dequantize.1.table_ref = bf16[1024,5376]{1,0:T(8,128)(2,1)} custom-call(bf16[512,5376]{1,0:T(8,128)(2,1)} %own_ref.1, bf16[512,5376]{1,0:T(8,128)(2,1)} %collective-permute-done.1.other_ref, f32[512,42]{1,0:T(8,128)} %copy-done.5, f32[512,42]{1,0:T(8,128)} %collective-permute-done.3.other_scale_ref), custom_call_target="tpu_custom_call" | custom-call | flops 5505024 | bytes 22020096 | tf_op jit(solution)/shard_map/dequantize/pallas_call | solution.py:60
  60.1 8.4 %collective-permute-done.7.a_hbm = bf16[128,7936]{1,0:T(8,128)(2,1)} collective-permute-done((bf16[128,7936]{1,0:T(8,128)(2,1)}, bf16[128,7936]{1,0:T(8,128)(2,1)}, u32[]{:S(2)}, u32[]{:S(2)}) %collective-permute-start.7) | collective-permute-done | bytes 2031648 | tf_op jit(solution)/shard_map/ppermute | solution.py:20
  68.7 12.4 %logits.3 = (f32[1024,256]{1,0:T(8,128)}, f32[1024,256]{1,0:T(8,128)}, f32[8,256]{1,0:T(8,128)}) custom-call(bf16[128,7936]{1,0:T(8,128)(2,1)} %collective-permute-done.7.a_hbm, bf16[128,7936]{1,0:T(8,128)(2,1)} %collective-permute-done.8.b_hbm, bf16[1024,5376]{1,0:T(8,128)(2,1)} %dequantize.1.table_ref, bf16[1024,2560]{1,0:T(8,128)(2,1)} %copy.31.weight_ref), custom_call_target="tpu_custom_call" | custom-call | flops 4160749568 | bytes 22413312 | tf_op jit(solution)/shard_map/logits/pallas_call | solution.py:134
  89.0 12.4 %logits.2 = (f32[1024,256]{1,0:T(8,128)}, f32[1024,256]{1,0:T(8,128)}, f32[8,256]{1,0:T(8,128)}) custom-call(bf16[128,7936]{1,0:T(8,128)(2,1)} %constant_dynamic-update-slice_fusion.a_hbm, bf16[128,7936]{1,0:T(8,128)(2,1)} %bitcast.96, bf16[1024,5376]{1,0:T(8,128)(2,1)} %dequantize.1.table_ref, bf16[1024,2560]{1,0:T(8,128)(2,1)} %copy.31.weight_ref), custom_call_target="tpu_custom_call" | custom-call | flops 4160749568 | bytes 22413312 | tf_op jit(solution)/shard_map/logits/pallas_call | solution.py:134
  105.1 7.2 %all-to-all-start = ((f32[16,8,512]{2,1,0:T(8,128)}), f32[16,8,512]{2,1,0:T(8,128)S(1)}, u32[]{:S(2)}, u32[]{:S(2)}) async-start(f32[16,8,512]{2,1,0:T(8,128)} %broadcast_in_dim.17), calls=%async_computation | async-start | bytes 524288 | tf_op jit(solution)/shard_map/all_to_all | solution.py:220
  116.2 3.4 %all-to-all-done = f32[16,8,512]{2,1,0:T(8,128)S(1)} async-done(((f32[16,8,512]{2,1,0:T(8,128)}), f32[16,8,512]{2,1,0:T(8,128)S(1)}, u32[]{:S(2)}, u32[]{:S(2)}) %all-to-all-start) | async-done | bytes 262176 | tf_op jit(solution)/shard_map/all_to_all | solution.py:220
  120.5 8.5 %all-to-all-start.1 = ((f32[8,5,512]{2,1,0:T(8,128)}), f32[8,5,512]{2,1,0:T(8,128)S(1)}, u32[]{:S(2)}, u32[]{:S(2)}) async-start(f32[8,5,512]{2,1,0:T(8,128)} %broadcast_in_dim.18), calls=%async_computation.1 | async-start | bytes 262144 | tf_op jit(solution)/shard_map/all_to_all | solution.py:220
  130.6 7.4 %all-to-all-done.1 = f32[8,5,512]{2,1,0:T(8,128)S(1)} async-done(((f32[8,5,512]{2,1,0:T(8,128)}), f32[8,5,512]{2,1,0:T(8,128)S(1)}, u32[]{:S(2)}, u32[]{:S(2)}) %all-to-all-start.1) | async-done | bytes 81952 | tf_op jit(solution)/shard_map/all_to_all | solution.py:220
  138.9 8.6 %gradients.1 = (bf16[512,512]{1,0:T(8,128)(2,1)}, bf16[512,512]{1,0:T(8,128)(2,1)}, bf16[4,4,640,128]{3,2,1,0:T(8,128)(2,1)}) custom-call(s32[1]{0:T(128)} %bitcast.21.y_ref, f32[8,512]{1,0:T(8,128)} %pad_maximum_fusion.2.rows_ref, f32[1024,256]{1,0:T(8,128)} %get-tuple-element.22.t0, f32[1024,256]{1,0:T(8,128)} %get-tuple-element.23.s0, ...), custom_call_target="tpu_custom_call" | custom-call | flops 2684354560 | bytes 13107200 | tf_op jit(solution)/shard_map/gradients/pallas_call | solution.py:192
  147.6 5.0 %all-to-all-start.2 = ((bf16[16,640,128]{2,1,0:T(8,128)(2,1)}), bf16[16,640,128]{2,1,0:T(8,128)(2,1)S(1)}, u32[]{:S(2)}, u32[]{:S(2)}) async-start(bf16[16,640,128]{2,1,0:T(8,128)(2,1)} %bitcast.98), calls=%async_computation.2 | async-start | bytes 5242880 | tf_op jit(solution)/shard_map/all_to_all | solution.py:296
  154.7 5.6 %fusion.22 = f32[512,2560]{1,0:T(8,128)} fusion(bf16[512,512]{1,0:T(8,128)(2,1)S(1)} %collective-permute-done.9, bf16[512,2560]{1,0:T(8,128)(2,1)} %collective-permute-done.10), kind=kOutput, calls=%fused_computation.66 | convolution fusion | flops 1342177280 | bytes 8388608 | tf_op jit(solution)/shard_map/dot_general | solution.py:302
  160.3 24.4 %all-to-all-done.2 = bf16[16,640,128]{2,1,0:T(8,128)(2,1)S(1)} async-done(((bf16[16,640,128]{2,1,0:T(8,128)(2,1)}), bf16[16,640,128]{2,1,0:T(8,128)(2,1)S(1)}, u32[]{:S(2)}, u32[]{:S(2)}) %all-to-all-start.2) | async-done | bytes 2621472 | tf_op jit(solution)/shard_map/all_to_all | solution.py:296
  185.7 3.4 %all-to-all-start.3 = ((bf16[8,80,128]{2,1,0:T(8,128)(2,1)}), bf16[8,80,128]{2,1,0:T(8,128)(2,1)S(1)}, u32[]{:S(2)}, u32[]{:S(2)}) async-start(bf16[8,80,128]{2,1,0:T(8,128)(2,1)} %bitcast.24), calls=%async_computation.3 | async-start | bytes 327680 | tf_op jit(solution)/shard_map/all_to_all | solution.py:298
  189.1 6.3 %add_convert_fusion = bf16[512,2560]{1,0:T(8,128)(2,1)} fusion(f32[512,2560]{1,0:T(8,128)} %fusion.22, bf16[512,512]{1,0:T(8,128)(2,1)} %get-tuple-element.27, bf16[128,2560]{1,0:T(8,128)(2,1)} %copy-done.2, bf16[128,2560]{1,0:T(8,128)(2,1)} %copy-done.1, bf16[128,2560]{1,0:T(8,128)(2,1)} %copy-done.3, bf16[128,2560]{1,0:T(8,128)(2,1)S(1)} %copy-done), kind=kOutput, calls=%fused_computation.1 | convolution fusion | flops 1355284480 | bytes 11010048 | tf_op jit(solution)/shard_map/dot_general | solution.py:301
  195.4 3.1 %all-to-all-done.3 = bf16[8,80,128]{2,1,0:T(8,128)(2,1)S(1)} async-done(((bf16[8,80,128]{2,1,0:T(8,128)(2,1)}), bf16[8,80,128]{2,1,0:T(8,128)(2,1)S(1)}, u32[]{:S(2)}, u32[]{:S(2)}) %all-to-all-start.3) | async-done | bytes 163872 | tf_op jit(solution)/shard_map/all_to_all | solution.py:298
  (78 shorter events, 30.6 us)
Async XLA Ops:
  0.6 6.2 %copy-start = (bf16[128,2560]{1,0:T(8,128)(2,1)S(1)}, bf16[128,2560]{1,0:T(8,128)(2,1)}, u32[]{:S(2)}) copy-start(bf16[128,2560]{1,0:T(8,128)(2,1)} %param.7) | copy-start | bytes 1966084
  0.6 25.2 %collective-permute-start.1 = (bf16[512,5376]{1,0:T(8,128)(2,1)}, bf16[512,5376]{1,0:T(8,128)(2,1)}, u32[]{:S(2)}, u32[]{:S(2)}) collective-permute-start(bf16[512,5376]{1,0:T(8,128)(2,1)} %own_ref.1), channel_id=1, source_target_pairs={{1,0},{0,1},{3,2},{2,3},{5,4},{4,5},{7,6},{6,7},{9,8},{8,9},{11,10... | collective-permute-start | bytes 16515080 | tf_op jit(solution)/shard_map/ppermute | solution.py:20
  3.8 10.6 %copy-start.7 = (bf16[128]{0:T(256)(128)(2,1)S(1)}, bf16[128]{0:T(256)(128)(2,1)}, u32[]{:S(2)}) copy-start(bf16[128]{0:T(256)(128)(2,1)} %param.11) | copy-start | bytes 772
  3.8 22.1 %collective-permute-start.2 = (bf16[512,2560]{0,1:T(8,128)(2,1)S(1)}, bf16[512,2560]{0,1:T(8,128)(2,1)}, u32[]{:S(2)}, u32[]{:S(2)}) collective-permute-start(bf16[512,2560]{0,1:T(8,128)(2,1)S(1)} %copy.27), channel_id=1, source_target_pairs={{1,0},{0,1},{3,2},{2,3},{5,4},{4,5},{7,6},{6,7},{9,8},{8,9},{11,10... | collective-permute-start | bytes 7864328 | tf_op jit(solution)/shard_map/ppermute | solution.py:20
  9.6 16.3 %collective-permute-start = (bf16[32,7936]{1,0:T(8,128)(2,1)}, bf16[32,7936]{1,0:T(8,128)(2,1)}, u32[]{:S(2)}, u32[]{:S(2)}) collective-permute-start(bf16[32,7936]{1,0:T(8,128)(2,1)} %constant_dynamic-slice_fusion.2), channel_id=1, source_target_pairs={{4,0},{6,2},{0,4},{2,6},{5,1},{7,3},{1,5},{3,7},{12,8},{14,10},{8,... | collective-permute-start | bytes 1523720 | tf_op jit(solution)/shard_map/ppermute | solution.py:20
  11.9 56.6 %collective-permute-start.7 = (bf16[128,7936]{1,0:T(8,128)(2,1)}, bf16[128,7936]{1,0:T(8,128)(2,1)}, u32[]{:S(2)}, u32[]{:S(2)}) collective-permute-start(bf16[128,7936]{1,0:T(8,128)(2,1)} %constant_dynamic-update-slice_fusion.a_hbm), channel_id=1, source_target_pairs={{2,0},{4,2},{6,4},{0,6},{3,1},{5,3},{7,5},{1,7},{10,8},{12,10},{14... | collective-permute-start | bytes 6094856 | tf_op jit(solution)/shard_map/ppermute | solution.py:20
  14.3 25.0 %copy-start.5 = (f32[512,42]{1,0:T(8,128)}, f32[512,42]{1,0:T(8,128)S(1)}, u32[]{:S(2)}) copy-start(f32[512,42]{1,0:T(8,128)S(1)} %copy.28.own_scale_ref) | copy-start | bytes 258052
  14.3 1.8 collective-permute-start.3
  16.0 52.6 %collective-permute-start.8 = (bf16[128,7936]{1,0:T(8,128)(2,1)}, bf16[128,7936]{1,0:T(8,128)(2,1)}, u32[]{:S(2)}, u32[]{:S(2)}) collective-permute-start(bf16[128,7936]{1,0:T(8,128)(2,1)} %constant_dynamic-update-slice_fusion.a_hbm), channel_id=1, source_target_pairs={{6,0},{0,2},{2,4},{4,6},{7,1},{1,3},{3,5},{5,7},{14,8},{8,10},{10,... | collective-permute-start | bytes 6094856 | tf_op jit(solution)/shard_map/ppermute | solution.py:20
  25.9 55.2 %collective-permute-start.4 = (bf16[32,7936]{1,0:T(8,128)(2,1)}, bf16[32,7936]{1,0:T(8,128)(2,1)}, u32[]{:S(2)}, u32[]{:S(2)}) collective-permute-start(bf16[32,7936]{1,0:T(8,128)(2,1)} %collective-permute-done), channel_id=1, source_target_pairs={{64,0},{128,64},{192,128},{0,192},{65,1},{129,65},{193,129},{1,193... | collective-permute-start | bytes 1523720 | tf_op jit(solution)/shard_map/ppermute | solution.py:20
  28.6 53.6 %collective-permute-start.5 = (bf16[32,7936]{1,0:T(8,128)(2,1)}, bf16[32,7936]{1,0:T(8,128)(2,1)}, u32[]{:S(2)}, u32[]{:S(2)}) collective-permute-start(bf16[32,7936]{1,0:T(8,128)(2,1)} %collective-permute-done), channel_id=1, source_target_pairs={{128,0},{192,64},{0,128},{64,192},{129,1},{193,65},{1,129},{65,193... | collective-permute-start | bytes 1523720 | tf_op jit(solution)/shard_map/ppermute | solution.py:20
  29.4 53.8 %collective-permute-start.6 = (bf16[32,7936]{1,0:T(8,128)(2,1)}, bf16[32,7936]{1,0:T(8,128)(2,1)}, u32[]{:S(2)}, u32[]{:S(2)}) collective-permute-start(bf16[32,7936]{1,0:T(8,128)(2,1)} %collective-permute-done), channel_id=1, source_target_pairs={{192,0},{0,64},{64,128},{128,192},{193,1},{1,65},{65,129},{129,193... | collective-permute-start | bytes 1523720 | tf_op jit(solution)/shard_map/ppermute | solution.py:20
  60.1 21.1 %copy-start.4 = (bf16[7,32,7936]{2,1,0:T(8,128)(2,1)S(1)}, bf16[7,32,7936]{2,1,0:T(8,128)(2,1)}, u32[]{:S(2)}) copy-start(bf16[7,32,7936]{2,1,0:T(8,128)(2,1)} %bitcast_dynamic-update-slice_fusion.5) | copy-start | bytes 10665988
  89.0 13.2 %copy-start.6 = (f32[8,256]{1,0:T(8,128)S(1)}, f32[8,256]{1,0:T(8,128)}, u32[]{:S(2)}) copy-start(f32[8,256]{1,0:T(8,128)} %get-tuple-element.21) | copy-start | bytes 24580
  105.1 14.5 %all-to-all-start = ((f32[16,8,512]{2,1,0:T(8,128)}), f32[16,8,512]{2,1,0:T(8,128)S(1)}, u32[]{:S(2)}, u32[]{:S(2)}) async-start(f32[16,8,512]{2,1,0:T(8,128)} %broadcast_in_dim.17), calls=%async_computation | async-start | bytes 524288 | tf_op jit(solution)/shard_map/all_to_all | solution.py:220
  113.5 17.1 %copy-start.1 = (bf16[128,2560]{1,0:T(8,128)(2,1)}, bf16[128,2560]{1,0:T(8,128)(2,1)S(1)}, u32[]{:S(2)}) copy-start(bf16[128,2560]{1,0:T(8,128)(2,1)S(1)} %slice.120) | copy-start | bytes 1966084
  114.8 15.7 %copy-start.2 = (bf16[128,2560]{1,0:T(8,128)(2,1)}, bf16[128,2560]{1,0:T(8,128)(2,1)S(1)}, u32[]{:S(2)}) copy-start(bf16[128,2560]{1,0:T(8,128)(2,1)S(1)} %slice.121) | copy-start | bytes 1966084
  116.2 31.3 %copy-start.3 = (bf16[128,2560]{1,0:T(8,128)(2,1)}, bf16[128,2560]{1,0:T(8,128)(2,1)S(1)}, u32[]{:S(2)}) copy-start(bf16[128,2560]{1,0:T(8,128)(2,1)S(1)} %slice.119) | copy-start | bytes 1966084
  120.5 17.5 %all-to-all-start.1 = ((f32[8,5,512]{2,1,0:T(8,128)}), f32[8,5,512]{2,1,0:T(8,128)S(1)}, u32[]{:S(2)}, u32[]{:S(2)}) async-start(f32[8,5,512]{2,1,0:T(8,128)} %broadcast_in_dim.18), calls=%async_computation.1 | async-start | bytes 262144 | tf_op jit(solution)/shard_map/all_to_all | solution.py:220
  130.6 24.2 %collective-permute-start.10 = (bf16[512,2560]{1,0:T(8,128)(2,1)}, bf16[512,2560]{1,0:T(8,128)(2,1)}, u32[]{:S(2)}, u32[]{:S(2)}) collective-permute-start(bf16[512,2560]{1,0:T(8,128)(2,1)} %pad_maximum_fusion.1), channel_id=1, source_target_pairs={{1,0},{0,1},{3,2},{2,3},{5,4},{4,5},{7,6},{6,7},{9,8},{8,9},{11,10... | collective-permute-start | bytes 7864328 | tf_op jit(solution)/shard_map/ppermute | solution.py:20
  147.6 37.1 %all-to-all-start.2 = ((bf16[16,640,128]{2,1,0:T(8,128)(2,1)}), bf16[16,640,128]{2,1,0:T(8,128)(2,1)S(1)}, u32[]{:S(2)}, u32[]{:S(2)}) async-start(bf16[16,640,128]{2,1,0:T(8,128)(2,1)} %bitcast.98), calls=%async_computation.2 | async-start | bytes 5242880 | tf_op jit(solution)/shard_map/all_to_all | solution.py:296
  152.6 2.1 %collective-permute-start.9 = (bf16[512,512]{1,0:T(8,128)(2,1)}, bf16[512,512]{1,0:T(8,128)(2,1)S(1)}, u32[]{:S(2)}, u32[]{:S(2)}) collective-permute-start(bf16[512,512]{1,0:T(8,128)(2,1)} %get-tuple-element.28), channel_id=1, source_target_pairs={{1,0},{0,1},{3,2},{2,3},{5,4},{4,5},{7,6},{6,7},{9,8},{8,9},{11,10... | collective-permute-start | bytes 1572872 | tf_op jit(solution)/shard_map/ppermute | solution.py:20
  185.7 12.7 %all-to-all-start.3 = ((bf16[8,80,128]{2,1,0:T(8,128)(2,1)}), bf16[8,80,128]{2,1,0:T(8,128)(2,1)S(1)}, u32[]{:S(2)}, u32[]{:S(2)}) async-start(bf16[8,80,128]{2,1,0:T(8,128)(2,1)} %bitcast.24), calls=%async_computation.3 | async-start | bytes 327680 | tf_op jit(solution)/shard_map/all_to_all | solution.py:298

commit v3 on v2

--- a/solution.py
+++ b/solution.py
@@ -31,6 +31,10 @@
 LOGIT_ROWS = 256
 
 
+def two_sources(i, steps):
+    return (jnp.minimum(i, steps - 1), 0), (jnp.maximum(i - steps, 0), 0)
+
+
 def dequant_kernel(own_steps, own_ref, other_ref, own_scale_ref, other_scale_ref, out_ref):
     def write(codes_ref, scale_ref):
         for g in range(codes_ref.shape[1] // GROUP):
@@ -51,20 +55,17 @@
     rows, width = codes.shape
     steps = rows // DEQUANT_ROWS
 
-    def own(i):
-        return (jnp.minimum(i, steps - 1), 0)
-
-    def other(i):
-        return (jnp.maximum(i - steps, 0), 0)
+    def source(width, k):
+        return pl.BlockSpec((DEQUANT_ROWS, width), lambda i: two_sources(i, steps)[k])
 
     return pl.pallas_call(
         functools.partial(dequant_kernel, steps),
         grid=(2 * steps,),
         in_specs=[
-            pl.BlockSpec((DEQUANT_ROWS, width), own),
-            pl.BlockSpec((DEQUANT_ROWS, width), other),
-            pl.BlockSpec((DEQUANT_ROWS, scales.shape[1]), own),
-            pl.BlockSpec((DEQUANT_ROWS, scales.shape[1]), other),
+            source(width, 0),
+            source(width, 1),
+            source(scales.shape[1], 0),
+            source(scales.shape[1], 1),
         ],
         out_specs=pl.BlockSpec((DEQUANT_ROWS, width), lambda i: (i, 0)),
         out_shape=jax.ShapeDtypeStruct((2 * rows, width), BF16),
@@ -76,21 +77,39 @@
     )(codes, codes_p, scales, scales_p)
 
 
-def logits_kernel(width_t, a_hbm, b_hbm, table_ref, weight_ref, t_ref, s_ref, stat_ref, pair, sem):
+def turn_kernel(steps, own_ref, other_ref, out_ref):
+    @pl.when(pl.program_id(0) < steps)
+    def _():
+        out_ref[...] = own_ref[...].T
+
+    @pl.when(pl.program_id(0) >= steps)
+    def _():
+        out_ref[...] = other_ref[...].T
+
+
+def turned_over(own, other):
+    rows, width = own.shape
+    steps = rows // DEQUANT_ROWS
+    return pl.pallas_call(
+        functools.partial(turn_kernel, steps),
+        grid=(2 * steps,),
+        in_specs=[
+            pl.BlockSpec((DEQUANT_ROWS, width), lambda i: two_sources(i, steps)[0]),
+            pl.BlockSpec((DEQUANT_ROWS, width), lambda i: two_sources(i, steps)[1]),
+        ],
+        out_specs=pl.BlockSpec((width, DEQUANT_ROWS), lambda i: (0, i)),
+        out_shape=jax.ShapeDtypeStruct((width, 2 * rows), BF16),
+        compiler_params=pltpu.CompilerParams(vmem_limit_bytes=VMEM_LIMIT),
+        cost_estimate=pl.CostEstimate(
+            flops=0, transcendentals=0, bytes_accessed=8 * rows * width
+        ),
+        name="turn",
+    )(own, other)
+
+
+def logits_tile(pair, table_ref, weight_ref, t_ref, s_ref, stat_ref):
     step = pl.program_id(0)
-    tok = a_hbm.shape[0]
-
-    @pl.when(step == 0)
-    def _():
-        copies = [
-            pltpu.make_async_copy(a_hbm, pair.at[pl.ds(0, tok)], sem.at[0]),
-            pltpu.make_async_copy(b_hbm, pair.at[pl.ds(tok, tok)], sem.at[1]),
-        ]
-        for copy in copies:
-            copy.start()
-        for copy in copies:
-            copy.wait()
-
+    width_t = table_ref.shape[1]
     t = lax.dot_general(table_ref[...], pair[:, :width_t], NT, preferred_element_type=F32)
     s = lax.dot_general(weight_ref[...], pair[:, width_t:], NT, preferred_element_type=F32)
     t_ref[...] = t
@@ -126,38 +145,114 @@
         stat_ref[4:5] = stat_ref[4:5] * s_keep + s_total
 
 
-def logits_of(a, b, table, weight):
-    rows, width_t = table.shape
-    width_s = weight.shape[1]
-    tokens = 2 * a.shape[0]
-    tile = jax.ShapeDtypeStruct((rows, tokens), F32)
+def load_pair(x_ref, refs, pair, sem):
+    tok, part = refs[0].shape[0], refs[1].shape[0]
+    copies = [pltpu.make_async_copy(refs[0], pair.at[pl.ds(0, tok)], sem.at[0])]
+    for k, ref in enumerate(refs[1:]):
+        at = pl.multiple_of(tok + lax.rem(x_ref[1] + k, tok // part) * part, part)
+        copies.append(pltpu.make_async_copy(ref, pair.at[pl.ds(at, part)], sem.at[k + 1]))
+    for copy in copies:
+        copy.start()
+    for copy in copies:
+        copy.wait()
+
+
+def logits_kernel(steps, n_pieces, place_ref, *rest):
+    pieces_hbm, rest = rest[:n_pieces], rest[n_pieces:]
+    (table_ref, weight_ref, weight_p_ref), rest = rest[:3], rest[3:]
+    tok = pieces_hbm[0].shape[0]
+    spread = len(rest) > 5
+    first_stat_ref, scale_ref = rest[:2] if spread else (None, None)
+    rest = rest[2:] if spread else rest
+    t_ref, s_ref, stat_ref = rest[:3]
+    spread_ref = rest[3] if spread else None
+    pair, sem = rest[-2:]
+    step = pl.program_id(0)
+
+    @pl.when(step == 0)
+    def _():
+        load_pair(place_ref, pieces_hbm, pair, sem)
+
+    @pl.when(step < steps)
+    def _():
+        logits_tile(pair, table_ref, weight_ref, t_ref, s_ref, stat_ref)
+
+    @pl.when(step >= steps)
+    def _():
+        logits_tile(pair, table_ref, weight_p_ref, t_ref, s_ref, stat_ref)
+
+    if spread:
+
+        @pl.when(step == 2 * steps - 1)
+        def _():
+            copies, _, wide = spread_ref.shape
+            n_y = wide // tok
+            row = lax.broadcasted_iota(jnp.int32, (8, tok), 0)
+            scale = jnp.broadcast_to(scale_ref[...], (8, tok))
+            first, last = first_stat_ref[...], stat_ref[...]
+            pieces = (
+                jnp.where(row == 5, scale, first[:, :tok]),
+                last[:, :tok],
+                first[:, tok:],
+                last[:, tok:],
+            )
+            for r, piece in enumerate(pieces):
+                at = pl.multiple_of(lax.rem(place_ref[0] + r, n_y) * tok, tok)
+                for k in range(copies):
+                    spread_ref[k, :, pl.ds(at, tok)] = piece
+
+
+def logits_of(place, pieces, table, weight, weight_p, first_stats=None, scale=None, copies=0):
+    width_t = table.shape[1]
+    rows, width_s = weight.shape
+    tok = pieces[0].shape[0]
+    tokens = 2 * tok
+    steps = rows // LOGIT_ROWS
+    tile = jax.ShapeDtypeStruct((2 * rows, tokens), F32)
+
+    def source(width, k):
+        return pl.BlockSpec((LOGIT_ROWS, width), lambda i, y: two_sources(i, steps)[k])
+
+    in_specs = [
+        *[pl.BlockSpec(memory_space=pl.ANY) for _ in pieces],
+        pl.BlockSpec((LOGIT_ROWS, width_t), lambda i, y: (i, 0)),
+        source(width_s, 0),
+        source(width_s, 1),
+    ]
+    out_specs = [
+        pl.BlockSpec((LOGIT_ROWS, tokens), lambda i, y: (i, 0)),
+        pl.BlockSpec((LOGIT_ROWS, tokens), lambda i, y: (i, 0)),
+        pl.BlockSpec((8, tokens), lambda i, y: (0, 0)),
+    ]
+    out_shape = [tile, tile, jax.ShapeDtypeStruct((8, tokens), F32)]
+    operands = [place, *pieces, table, weight, weight_p]
+    if first_stats is not None:
+        in_specs.append(pl.BlockSpec((8, tokens), lambda i, y: (0, 0)))
+        in_specs.append(pl.BlockSpec((1, tok), lambda i, y: (0, 0)))
+        operands += [first_stats, scale]
+        out_specs.append(pl.BlockSpec((copies, 8, 2 * tokens), lambda i, y: (0, 0, 0)))
+        out_shape.append(jax.ShapeDtypeStruct((copies, 8, 2 * tokens), F32))
     return pl.pallas_call(
-        functools.partial(logits_kernel, width_t),
-        grid=(rows // LOGIT_ROWS,),
-        in_specs=[
-            pl.BlockSpec(memory_space=pl.ANY),
-            pl.BlockSpec(memory_space=pl.ANY),
-            pl.BlockSpec((LOGIT_ROWS, width_t), lambda i: (i, 0)),
-            pl.BlockSpec((LOGIT_ROWS, width_s), lambda i: (i, 0)),
-        ],
-        out_specs=[
-            pl.BlockSpec((LOGIT_ROWS, tokens), lambda i: (i, 0)),
-            pl.BlockSpec((LOGIT_ROWS, tokens), lambda i: (i, 0)),
-            pl.BlockSpec((8, tokens), lambda i: (0, 0)),
-        ],
-        out_shape=[tile, tile, jax.ShapeDtypeStruct((8, tokens), F32)],
-        scratch_shapes=[
-            pltpu.VMEM((tokens, width_t + width_s), BF16),
-            pltpu.SemaphoreType.DMA((2,)),
-        ],
+        functools.partial(logits_kernel, steps, len(pieces)),
+        grid_spec=pltpu.PrefetchScalarGridSpec(
+            num_scalar_prefetch=1,
+            grid=(2 * steps,),
+            in_specs=in_specs,
+            out_specs=out_specs,
+            scratch_shapes=[
+                pltpu.VMEM((tokens, width_t + width_s), BF16),
+                pltpu.SemaphoreType.DMA((len(pieces),)),
+            ],
+        ),
+        out_shape=out_shape,
         compiler_params=pltpu.CompilerParams(vmem_limit_bytes=VMEM_LIMIT),
         cost_estimate=pl.CostEstimate(
-            flops=2 * rows * tokens * (width_t + width_s),
-            transcendentals=2 * rows * tokens,
-            bytes_accessed=2 * (rows + tokens) * (width_t + width_s) + 8 * rows * tokens,
+            flops=4 * rows * tokens * (width_t + width_s),
+            transcendentals=4 * rows * tokens,
+            bytes_accessed=2 * (2 * rows + tokens) * (width_t + width_s) + 16 * rows * tokens,
         ),
         name="logits",
-    )(a, b, table, weight)
+    )(*operands)
 
 
 def grad_kernel(y_ref, rows_ref, t0, s0, t1, s1, turned_ref, own_ref, other_ref, out_ref):
@@ -245,8 +340,12 @@
     x, y = lax.axis_index("x"), lax.axis_index("y")
     part = tok // n_x
 
+    place = jnp.stack([y, x]).astype(jnp.int32)
+    piece = [
+        lax.dynamic_slice_in_dim(a, x * part, part, 0) for a in (teacher_hidden, student_hidden)
+    ]
+    quarter = shift(jnp.concatenate(piece, axis=1), "y", 2)
     hidden = jnp.concatenate([teacher_hidden, student_hidden], axis=1)
-    quarter = shift(lax.dynamic_slice_in_dim(hidden, x * part, part, 0), "y", 2)
     after, before = shift(hidden, "y", 1), shift(hidden, "y", 3)
     codes_p = shift(teacher_codes, "c", 1)
     weight_p = shift(student_weight, "c", 1)
@@ -254,21 +353,23 @@
     quarter, codes_p, weight_p, scales_p = lax.optimization_barrier(
         (quarter, codes_p, weight_p, scales_p)
     )
-    quarters = jnp.stack([quarter, *(shift(quarter, "x", k) for k in range(1, n_x))])
-    opposite = rolled(quarters, n_x - x).reshape(tok, -1)
-
+    quarters = [quarter, *(shift(quarter, "x", k) for k in range(1, n_x))]
     table = dequantize(teacher_codes, codes_p, teacher_scales, scales_p)
-    weight = jnp.concatenate([student_weight, weight_p])
-    turned = weight.T
-
-    t0, s0, stats0 = logits_of(hidden, opposite, table, weight)
-    t1, s1, stats1 = logits_of(after, before, table, weight)
-    pieces = [stats0[:, :tok], stats1[:, :tok], stats0[:, tok:], stats1[:, tok:]]
-    row = lax.broadcasted_iota(jnp.int32, (8, tok), 0)
-    pieces[0] = jnp.where(row == 5, loss_scale.astype(F32)[None], pieces[0])
-    twice = jnp.concatenate(pieces + pieces[:-1], axis=1)
-    mine = lax.dynamic_slice_in_dim(twice, lax.rem(n_y - y, n_y) * tok, n_y * tok, 1)
-    seen = to_all(mine, ("x", "y"))
+    turned = turned_over(student_weight, weight_p)
+
+    tables = (table, student_weight, weight_p)
+    t0, s0, stats0 = logits_of(place, [hidden, *quarters], *tables)
+    after, before, stats0, turned = lax.optimization_barrier((after, before, stats0, turned))
+    t1, s1, _, mine = logits_of(
+        place,
+        [after, before],
+        *tables,
+        first_stats=stats0,
+        scale=loss_scale.astype(F32)[None],
+        copies=n_x * n_y,
+    )
+    opposite_s = rolled(jnp.stack([q[:, width_t:] for q in quarters]), n_x - x).reshape(tok, -1)
+    seen = lax.all_to_all(mine, ("x", "y"), 0, 0, tiled=True)
     scales = jnp.sum(seen[:n_y, 5], axis=0)
     totals = combine(to_all(combine(seen), "z"))
     t_lse = totals[0] + jnp.log(totals[1])
@@ -281,7 +382,7 @@
     kl = found[3, :tok]
     order = [found[:, k * tok : (k + 1) * tok] for k in (0, 2, 1, 3)]
     own, other, blocks = gradients(
-        y.astype(jnp.int32)[None],
+        place,
         jnp.concatenate(order, axis=1),
         ((t0, s0), (t1, s1)),
         turned,
@@ -289,7 +390,9 @@
         n_y,
     )
     from_p = shift(other, "c", 1)
-    students = jnp.concatenate([p[:, width_t:] for p in (hidden, opposite, after, before)])
+    students = jnp.concatenate(
+        [student_hidden, opposite_s, after[:, width_t:], before[:, width_t:]]
+    )
     students_p = shift(students, "c", 1)
 
     blocks = blocks.reshape(n_x * n_y, width_s // n_x, tok)

time: 201 us -> 176 us (0.88)
  local copies, waits for them, and re-layouts: 34.2 us -> 18 us
  waiting for transfers between devices: 59.2 us -> 47.6 us
  Pallas kernels: 46.4 us -> 57.1 us
  other arithmetic: 12.9 us -> 6.36 us
    ppermute x11, waiting for transfers between devices: 21 us -> 10.2 us  [shift(): return lax.ppermute(a, axis, [((i + by) % n, i) for i in range(n)])]
    pallas_call x2 -> x3, Pallas kernels: 24.9 us -> 35 us  [the longest x2 27 us: logits_of(): pl.pallas_call(functools.partial(logits_kernel, steps, len(pieces)), grid...]
    concatenate x2 -> x0, local copies, waits for them, and re-layouts: 8.55 us -> none  [the longest x1 7.86 us: local(): weight = jnp.concatenate([student_weight, weight_p])]
    all_to_all x2 -> x1, starting transfers between devices: 15.7 us -> 8.47 us  [to_all(): lax.all_to_all(jnp.broadcast_to(a[None], (n, *a.shape)), axes, 0, 0, tile...]
    transpose x1 -> x0, other arithmetic: 7.06 us -> none  [local(): turned = weight.T]
    all_to_all x0 -> x1, starting transfers between devices: none -> 5.45 us  [local(): seen = lax.all_to_all(mine, ('x', 'y'), 0, 0, tiled=True)]
    unnamed x29 -> x34, local copies, waits for them, and re-layouts: 14.5 us -> 9.36 us
    all_to_all x2 -> x1, waiting for transfers between devices: 10.8 us -> 7.4 us  [to_all(): lax.all_to_all(jnp.broadcast_to(a[None], (n, *a.shape)), axes, 0, 0, tile...]
  transfers between devices with their start and end apart: 15 -> 15, of which waited for: 9 -> 6; matrix products, arithmetic and copies ran while one was open for 24% -> 17% of each run, Pallas kernels for 17% -> 25%
where the time goes in v3:
time: 176 us; the launch traced here: 175 us
  Pallas kernels  57.1 us (32%)
  waiting for transfers between devices  47.6 us (27%)
  starting transfers between devices  33.4 us (19%)
  local copies, waits for them, and re-layouts  18 us (10%)
  matrix products  11.9 us (7%)
  other arithmetic  6.36 us (4%)
    pallas_call x2, Pallas kernels, logits_of(): pl.pallas_call(functools.partial(logits_kernel, steps, len(pieces)), grid...  27 us
    all_to_all x1, waiting for transfers between devices, local(): got = lax.all_to_all(blocks, ('x', 'y'), 0, 0, tiled=True)  24.2 us
    pallas_call x1, Pallas kernels, dequantize(): pl.pallas_call(functools.partial(dequant_kernel, steps), grid=(2 * steps,...  12.9 us
    ppermute x11, starting transfers between devices, shift(): return lax.ppermute(a, axis, [((i + by) % n, i) for i in range(n)])  10.8 us
    ppermute x11, waiting for transfers between devices, shift(): return lax.ppermute(a, axis, [((i + by) % n, i) for i in range(n)])  10.2 us
    unnamed x34, local copies, waits for them, and re-layouts  9.36 us
    pallas_call x1, Pallas kernels, gradients(): pl.pallas_call(grad_kernel, grid_spec=pltpu.PrefetchScalarGridSpec(num_sc...  9.22 us
    all_to_all x1, starting transfers between devices, to_all(): lax.all_to_all(jnp.broadcast_to(a[None], (n, *a.shape)), axes, 0, 0, tile...  8.47 us
  transfers between devices with their start and end apart: 15, of which 6 were waited for; matrix products, arithmetic and copies ran while one was open for 17% of the time, Pallas kernels for 25%

profile of v3, /device:TPU:8, one launch (start us, length us, event | category | flops | bytes accessed | tf_op | source)
XLA Modules:
  0.0 175.2 jit_solution(12817386849576865128)
XLA Ops:
  5.3 2.3 %collective-permute-start.2 = (bf16[32,7936]{1,0:T(8,128)(2,1)}, bf16[32,7936]{1,0:T(8,128)(2,1)}, u32[]{:S(2)}, u32[]{:S(2)}) collective-permute-start(bf16[32,7936]{1,0:T(8,128)(2,1)} %pad_maximum_fusion.1), channel_id=1, source_target_pairs={{4,0},{6,2},{0,4},{2,6},{5,1},{7,3},{1,5},{3,7},{12,8},{14,10},{8,... | collective-permute-start | bytes 1523720 | tf_op jit(solution)/shard_map/ppermute | solution.py:20
  13.1 8.5 %collective-permute-done.2.rest_1_ = bf16[32,7936]{1,0:T(8,128)(2,1)} collective-permute-done((bf16[32,7936]{1,0:T(8,128)(2,1)}, bf16[32,7936]{1,0:T(8,128)(2,1)}, u32[]{:S(2)}, u32[]{:S(2)}) %collective-permute-start.2) | collective-permute-done | bytes 507936 | tf_op jit(solution)/shard_map/ppermute | solution.py:20
  21.6 1.6 collective-permute-start.8
  23.2 2.7 %collective-permute-start.7 = (bf16[32,7936]{1,0:T(8,128)(2,1)}, bf16[32,7936]{1,0:T(8,128)(2,1)S(1)}, u32[]{:S(2)}, u32[]{:S(2)}) collective-permute-start(bf16[32,7936]{1,0:T(8,128)(2,1)} %collective-permute-done.2.rest_1_), channel_id=1, source_target_pairs={{128,0},{192,64},{0,128},{64,192},{129,1},{193,65},{1,129},{65,193... | collective-permute-start | bytes 1523720 | tf_op jit(solution)/shard_map/ppermute | solution.py:20
  27.3 8.0 %turn.1.turned_ref = bf16[2560,1024]{1,0:T(8,128)(2,1)} custom-call(bf16[512,2560]{1,0:T(8,128)(2,1)} %rest_3_.1, bf16[512,2560]{1,0:T(8,128)(2,1)} %copy-done), custom_call_target="tpu_custom_call" | custom-call | bytes 10485760 | tf_op jit(solution)/shard_map/turn/pallas_call | solution.py:93
  35.4 12.9 %dequantize.1.rest_5_.rest_2_ = bf16[1024,5376]{1,0:T(8,128)(2,1)} custom-call(bf16[512,5376]{1,0:T(8,128)(2,1)} %own_ref.2, bf16[512,5376]{1,0:T(8,128)(2,1)} %collective-permute-done.3.other_ref, f32[512,42]{1,0:T(8,128)} %copy-done.9, f32[512,42]{1,0:T(8,128)} %collective-permute-done.5.other_scale_ref), custom_call_target="tpu_custom_call" | custom-call | flops 5505024 | bytes 22020096 | tf_op jit(solution)/shard_map/dequantize/pallas_call | solution.py:61
  51.0 13.4 %logits.2 = (f32[1024,256]{1,0:T(8,128)}, f32[1024,256]{1,0:T(8,128)}, f32[8,256]{1,0:T(8,128)}) custom-call(s32[2]{0:T(128)} %pad_add_fusion.place_ref.y_ref, bf16[128,7936]{1,0:T(8,128)(2,1)} %constant_dynamic-update-slice_fusion.rest_0_, bf16[32,7936]{1,0:T(8,128)(2,1)} %collective-permute-done.2.rest_1_, bf16[32,7936]{1,0:T(8,128)(2,1)} %copy-done.8, ...), custom_call_target="tpu_custom_call" | custom-call | flops 4160749568 | bytes 22413312 | tf_op jit(solution)/shard_map/logits/pallas_call | solution.py:235
  67.2 1.6 slice.97
  68.9 13.6 %logits.3 = (f32[1024,256]{1,0:T(8,128)}, f32[1024,256]{1,0:T(8,128)}, f32[8,256]{1,0:T(8,128)}, f32[16,8,512]{2,1,0:T(8,128)}) custom-call(s32[2]{0:T(128)} %pad_add_fusion.place_ref.y_ref, bf16[128,7936]{1,0:T(8,128)(2,1)} %copy-done.1, bf16[128,7936]{1,0:T(8,128)(2,1)} %collective-permute-done.1.rest_1_, bf16[1024,5376]{1,0:T(8,128)(2,1)} %dequantize.1.rest_5_.rest_2_, ...), custom_call_target="tpu_custom_call" | custom-call | flops 4160749568 | bytes 22413312 | tf_op jit(solution)/shard_map/logits/pallas_call | solution.py:235
  82.5 5.4 %all-to-all-start = ((f32[16,8,512]{2,1,0:T(8,128)}), f32[16,8,512]{2,1,0:T(8,128)S(1)}, u32[]{:S(2)}, u32[]{:S(2)}) async-start(f32[16,8,512]{2,1,0:T(8,128)} %get-tuple-element.28), calls=%async_computation | async-start | bytes 524288 | tf_op jit(solution)/shard_map/all_to_all | solution.py:372
  88.0 1.6 fusion.2
  89.6 1.6 fusion.4
  92.3 2.7 %all-to-all-done = f32[16,8,512]{2,1,0:T(8,128)S(1)} async-done(((f32[16,8,512]{2,1,0:T(8,128)}), f32[16,8,512]{2,1,0:T(8,128)S(1)}, u32[]{:S(2)}, u32[]{:S(2)}) %all-to-all-start) | async-done | bytes 262176 | tf_op jit(solution)/shard_map/all_to_all | solution.py:372
  95.9 8.5 %all-to-all-start.1 = ((f32[8,5,512]{2,1,0:T(8,128)}), f32[8,5,512]{2,1,0:T(8,128)S(1)}, u32[]{:S(2)}, u32[]{:S(2)}) async-start(f32[8,5,512]{2,1,0:T(8,128)} %broadcast_in_dim.20), calls=%async_computation.1 | async-start | bytes 262144 | tf_op jit(solution)/shard_map/all_to_all | solution.py:315
  104.3 1.6 pad_maximum_fusion
  106.0 7.4 %all-to-all-done.1 = f32[8,5,512]{2,1,0:T(8,128)S(1)} async-done(((f32[8,5,512]{2,1,0:T(8,128)}), f32[8,5,512]{2,1,0:T(8,128)S(1)}, u32[]{:S(2)}, u32[]{:S(2)}) %all-to-all-start.1) | async-done | bytes 81952 | tf_op jit(solution)/shard_map/all_to_all | solution.py:315
  114.3 9.2 %gradients.1 = (bf16[512,512]{1,0:T(8,128)(2,1)}, bf16[512,512]{1,0:T(8,128)(2,1)}, bf16[4,4,640,128]{3,2,1,0:T(8,128)(2,1)}) custom-call(s32[2]{0:T(128)} %pad_add_fusion.place_ref.y_ref, f32[8,512]{1,0:T(8,128)} %pad_maximum_fusion.2.rows_ref, f32[1024,256]{1,0:T(8,128)} %get-tuple-element.29.t0, f32[1024,256]{1,0:T(8,128)} %get-tuple-element.30.s0, ...), custom_call_target="tpu_custom_call" | custom-call | flops 2684354560 | bytes 13107200 | tf_op jit(solution)/shard_map/gradients/pallas_call | solution.py:287
  123.5 5.2 %all-to-all-start.2 = ((bf16[16,640,128]{2,1,0:T(8,128)(2,1)}), bf16[16,640,128]{2,1,0:T(8,128)(2,1)S(1)}, u32[]{:S(2)}, u32[]{:S(2)}) async-start(bf16[16,640,128]{2,1,0:T(8,128)(2,1)} %bitcast.108), calls=%async_computation.2 | async-start | bytes 5242880 | tf_op jit(solution)/shard_map/all_to_all | solution.py:399
  129.2 1.6 collective-permute-done.9
  130.8 5.6 %fusion.26 = f32[512,2560]{1,0:T(8,128)} fusion(bf16[512,512]{1,0:T(8,128)(2,1)S(1)} %collective-permute-done.9, bf16[512,2560]{1,0:T(8,128)(2,1)} %collective-permute-done.10), kind=kOutput, calls=%fused_computation.61 | convolution fusion | flops 1342177280 | bytes 8388608 | tf_op jit(solution)/shard_map/dot_general | solution.py:405
  136.4 24.2 %all-to-all-done.2 = bf16[16,640,128]{2,1,0:T(8,128)(2,1)S(1)} async-done(((bf16[16,640,128]{2,1,0:T(8,128)(2,1)}), bf16[16,640,128]{2,1,0:T(8,128)(2,1)S(1)}, u32[]{:S(2)}, u32[]{:S(2)}) %all-to-all-start.2) | async-done | bytes 2621472 | tf_op jit(solution)/shard_map/all_to_all | solution.py:399
  161.6 3.5 %all-to-all-start.3 = ((bf16[8,80,128]{2,1,0:T(8,128)(2,1)}), bf16[8,80,128]{2,1,0:T(8,128)(2,1)S(1)}, u32[]{:S(2)}, u32[]{:S(2)}) async-start(bf16[8,80,128]{2,1,0:T(8,128)(2,1)} %bitcast.20), calls=%async_computation.3 | async-start | bytes 327680 | tf_op jit(solution)/shard_map/all_to_all | solution.py:401
  165.2 6.3 %add_convert_fusion = bf16[512,2560]{1,0:T(8,128)(2,1)} fusion(f32[512,2560]{1,0:T(8,128)} %fusion.26, bf16[512,512]{1,0:T(8,128)(2,1)} %get-tuple-element.35, bf16[128,2560]{1,0:T(8,128)(2,1)} %copy-done.3, bf16[128,2560]{1,0:T(8,128)(2,1)} %copy-done.4, bf16[128,2560]{1,0:T(8,128)(2,1)} %bitcast.107, bf16[128,2560]{1,0:T(8,128)(2,1)S(1)} %copy-done.2), kind=kOutput, calls=%fused_computation | convolution fusion | flops 1355284480 | bytes 11010048 | tf_op jit(solution)/shard_map/dot_general | solution.py:404
  171.4 3.1 %all-to-all-done.3 = bf16[8,80,128]{2,1,0:T(8,128)(2,1)S(1)} async-done(((bf16[8,80,128]{2,1,0:T(8,128)(2,1)}), bf16[8,80,128]{2,1,0:T(8,128)(2,1)S(1)}, u32[]{:S(2)}, u32[]{:S(2)}) %all-to-all-start.3) | async-done | bytes 163872 | tf_op jit(solution)/shard_map/all_to_all | solution.py:401
  (78 shorter events, 22.1 us)
Async XLA Ops:
  0.6 8.2 %copy-start.2 = (bf16[128,2560]{1,0:T(8,128)(2,1)S(1)}, bf16[128,2560]{1,0:T(8,128)(2,1)}, u32[]{:S(2)}) copy-start(bf16[128,2560]{1,0:T(8,128)(2,1)} %param.7) | copy-start | bytes 1966084
  0.6 21.0 %collective-permute-start.3 = (bf16[512,5376]{1,0:T(8,128)(2,1)}, bf16[512,5376]{1,0:T(8,128)(2,1)}, u32[]{:S(2)}, u32[]{:S(2)}) collective-permute-start(bf16[512,5376]{1,0:T(8,128)(2,1)} %own_ref.2), channel_id=1, source_target_pairs={{1,0},{0,1},{3,2},{2,3},{5,4},{4,5},{7,6},{6,7},{9,8},{8,9},{11,10... | collective-permute-start | bytes 16515080 | tf_op jit(solution)/shard_map/ppermute | solution.py:20
  1.8 7.9 %copy-start.9 = (f32[512,42]{1,0:T(8,128)}, f32[512,42]{1,0:T(8,128)S(1)}, u32[]{:S(2)}) copy-start(f32[512,42]{1,0:T(8,128)S(1)} %copy.22.own_scale_ref) | copy-start | bytes 258052
  1.8 10.5 %collective-permute-start.5 = (f32[512,42]{1,0:T(8,128)S(1)}, f32[512,42]{1,0:T(8,128)}, u32[]{:S(2)}, u32[]{:S(2)}) collective-permute-start(f32[512,42]{1,0:T(8,128)S(1)} %copy.22.own_scale_ref), channel_id=1, source_target_pairs={{1,0},{0,1},{3,2},{2,3},{5,4},{4,5},{7,6},{6,7},{9,8},{8,9},{11,10... | collective-permute-start | bytes 258056 | tf_op jit(solution)/shard_map/ppermute | solution.py:20
  2.4 19.2 %collective-permute-start.4 = (bf16[512,2560]{1,0:T(8,128)(2,1)}, bf16[512,2560]{1,0:T(8,128)(2,1)S(1)}, u32[]{:S(2)}, u32[]{:S(2)}) collective-permute-start(bf16[512,2560]{1,0:T(8,128)(2,1)} %rest_3_.1), channel_id=1, source_target_pairs={{1,0},{0,1},{3,2},{2,3},{5,4},{4,5},{7,6},{6,7},{9,8},{8,9},{11,10... | collective-permute-start | bytes 7864328 | tf_op jit(solution)/shard_map/ppermute | solution.py:20
  2.5 5.2 %copy-start.6 = (bf16[128,5376]{1,0:T(8,128)(2,1)S(1)}, bf16[128,5376]{1,0:T(8,128)(2,1)}, u32[]{:S(2)}) copy-start(bf16[128,5376]{1,0:T(8,128)(2,1)} %param.6) | copy-start | bytes 4128772
  4.5 6.6 %copy-start.12 = (bf16[128]{0:T(256)(128)(2,1)S(1)}, bf16[128]{0:T(256)(128)(2,1)}, u32[]{:S(2)}) copy-start(bf16[128]{0:T(256)(128)(2,1)} %param.11) | copy-start | bytes 772
  5.3 16.2 %collective-permute-start.2 = (bf16[32,7936]{1,0:T(8,128)(2,1)}, bf16[32,7936]{1,0:T(8,128)(2,1)}, u32[]{:S(2)}, u32[]{:S(2)}) collective-permute-start(bf16[32,7936]{1,0:T(8,128)(2,1)} %pad_maximum_fusion.1), channel_id=1, source_target_pairs={{4,0},{6,2},{0,4},{2,6},{5,1},{7,3},{1,5},{3,7},{12,8},{14,10},{8,... | collective-permute-start | bytes 1523720 | tf_op jit(solution)/shard_map/ppermute | solution.py:20
  9.8 57.4 %collective-permute-start.1 = (bf16[128,7936]{1,0:T(8,128)(2,1)}, bf16[128,7936]{1,0:T(8,128)(2,1)}, u32[]{:S(2)}, u32[]{:S(2)}) collective-permute-start(bf16[128,7936]{1,0:T(8,128)(2,1)} %constant_dynamic-update-slice_fusion.rest_0_), channel_id=1, source_target_pairs={{6,0},{0,2},{2,4},{4,6},{7,1},{1,3},{3,5},{5,7},{14,8},{8,10},{10,... | collective-permute-start | bytes 6094856 | tf_op jit(solution)/shard_map/ppermute | solution.py:20
  12.4 54.8 %collective-permute-start = (bf16[128,7936]{1,0:T(8,128)(2,1)}, bf16[128,7936]{1,0:T(8,128)(2,1)S(1)}, u32[]{:S(2)}, u32[]{:S(2)}) collective-permute-start(bf16[128,7936]{1,0:T(8,128)(2,1)} %constant_dynamic-update-slice_fusion.rest_0_), channel_id=1, source_target_pairs={{2,0},{4,2},{6,4},{0,6},{3,1},{5,3},{7,5},{1,7},{10,8},{12,10},{14... | collective-permute-start | bytes 6094856 | tf_op jit(solution)/shard_map/ppermute | solution.py:20
  21.6 5.7 %copy-start = (bf16[512,2560]{1,0:T(8,128)(2,1)}, bf16[512,2560]{1,0:T(8,128)(2,1)S(1)}, u32[]{:S(2)}) copy-start(bf16[512,2560]{1,0:T(8,128)(2,1)S(1)} %collective-permute-done.4.rest_7_.other_ref.rest_4_) | copy-start | bytes 7864324
  21.6 27.6 %collective-permute-start.8 = (bf16[32,7936]{1,0:T(8,128)(2,1)}, bf16[32,7936]{1,0:T(8,128)(2,1)S(1)}, u32[]{:S(2)}, u32[]{:S(2)}) collective-permute-start(bf16[32,7936]{1,0:T(8,128)(2,1)} %collective-permute-done.2.rest_1_), channel_id=1, source_target_pairs={{192,0},{0,64},{64,128},{128,192},{193,1},{1,65},{65,129},{129,193... | collective-permute-start | bytes 1523720 | tf_op jit(solution)/shard_map/ppermute | solution.py:20
  23.2 26.1 %collective-permute-start.7 = (bf16[32,7936]{1,0:T(8,128)(2,1)}, bf16[32,7936]{1,0:T(8,128)(2,1)S(1)}, u32[]{:S(2)}, u32[]{:S(2)}) collective-permute-start(bf16[32,7936]{1,0:T(8,128)(2,1)} %collective-permute-done.2.rest_1_), channel_id=1, source_target_pairs={{128,0},{192,64},{0,128},{64,192},{129,1},{193,65},{1,129},{65,193... | collective-permute-start | bytes 1523720 | tf_op jit(solution)/shard_map/ppermute | solution.py:20
  25.9 23.3 %collective-permute-start.6 = (bf16[32,7936]{1,0:T(8,128)(2,1)}, bf16[32,7936]{1,0:T(8,128)(2,1)S(1)}, u32[]{:S(2)}, u32[]{:S(2)}) collective-permute-start(bf16[32,7936]{1,0:T(8,128)(2,1)} %collective-permute-done.2.rest_1_), channel_id=1, source_target_pairs={{64,0},{128,64},{192,128},{0,192},{65,1},{129,65},{193,129},{1,193... | collective-permute-start | bytes 1523720 | tf_op jit(solution)/shard_map/ppermute | solution.py:20
  67.2 15.4 %copy-start.11 = (bf16[7,32,2560]{2,1,0:T(8,128)(2,1)}, bf16[7,32,2560]{2,1,0:T(8,128)(2,1)S(1)}, u32[]{:S(2)}) copy-start(bf16[7,32,2560]{2,1,0:T(8,128)(2,1)S(1)} %bitcast_dynamic-update-slice_fusion.1) | copy-start | bytes 3440644
  68.8 35.5 %copy-start.3 = (bf16[128,2560]{1,0:T(8,128)(2,1)}, bf16[128,2560]{1,0:T(8,128)(2,1)S(1)}, u32[]{:S(2)}) copy-start(bf16[128,2560]{1,0:T(8,128)(2,1)S(1)} %slice.97) | copy-start | bytes 1966084
  68.9 35.5 %copy-start.4 = (bf16[128,2560]{1,0:T(8,128)(2,1)}, bf16[128,2560]{1,0:T(8,128)(2,1)S(1)}, u32[]{:S(2)}) copy-start(bf16[128,2560]{1,0:T(8,128)(2,1)S(1)} %slice.96) | copy-start | bytes 1966084
  82.5 12.4 %all-to-all-start = ((f32[16,8,512]{2,1,0:T(8,128)}), f32[16,8,512]{2,1,0:T(8,128)S(1)}, u32[]{:S(2)}, u32[]{:S(2)}) async-start(f32[16,8,512]{2,1,0:T(8,128)} %get-tuple-element.28), calls=%async_computation | async-start | bytes 524288 | tf_op jit(solution)/shard_map/all_to_all | solution.py:372
  92.3 13.7 %copy-start.5 = (bf16[4,32,2560]{2,1,0:T(8,128)(2,1)}, bf16[4,32,2560]{2,1,0:T(8,128)(2,1)S(1)}, u32[]{:S(2)}) copy-start(bf16[4,32,2560]{2,1,0:T(8,128)(2,1)S(1)} %constant_dynamic-slice_fusion) | copy-start | bytes 1966084
  95.9 17.6 %all-to-all-start.1 = ((f32[8,5,512]{2,1,0:T(8,128)}), f32[8,5,512]{2,1,0:T(8,128)S(1)}, u32[]{:S(2)}, u32[]{:S(2)}) async-start(f32[8,5,512]{2,1,0:T(8,128)} %broadcast_in_dim.20), calls=%async_computation.1 | async-start | bytes 262144 | tf_op jit(solution)/shard_map/all_to_all | solution.py:315
  106.0 24.8 %collective-permute-start.10 = (bf16[512,2560]{1,0:T(8,128)(2,1)}, bf16[512,2560]{1,0:T(8,128)(2,1)}, u32[]{:S(2)}, u32[]{:S(2)}) collective-permute-start(bf16[512,2560]{1,0:T(8,128)(2,1)} %pad_maximum_fusion), channel_id=1, source_target_pairs={{1,0},{0,1},{3,2},{2,3},{5,4},{4,5},{7,6},{6,7},{9,8},{8,9},{11,10... | collective-permute-start | bytes 7864328 | tf_op jit(solution)/shard_map/ppermute | solution.py:20
  123.5 37.1 %all-to-all-start.2 = ((bf16[16,640,128]{2,1,0:T(8,128)(2,1)}), bf16[16,640,128]{2,1,0:T(8,128)(2,1)S(1)}, u32[]{:S(2)}, u32[]{:S(2)}) async-start(bf16[16,640,128]{2,1,0:T(8,128)(2,1)} %bitcast.108), calls=%async_computation.2 | async-start | bytes 5242880 | tf_op jit(solution)/shard_map/all_to_all | solution.py:399
  128.7 2.1 %collective-permute-start.9 = (bf16[512,512]{1,0:T(8,128)(2,1)}, bf16[512,512]{1,0:T(8,128)(2,1)S(1)}, u32[]{:S(2)}, u32[]{:S(2)}) collective-permute-start(bf16[512,512]{1,0:T(8,128)(2,1)} %get-tuple-element.36), channel_id=1, source_target_pairs={{1,0},{0,1},{3,2},{2,3},{5,4},{4,5},{7,6},{6,7},{9,8},{8,9},{11,10... | collective-permute-start | bytes 1572872 | tf_op jit(solution)/shard_map/ppermute | solution.py:20
  161.6 12.9 %all-to-all-start.3 = ((bf16[8,80,128]{2,1,0:T(8,128)(2,1)}), bf16[8,80,128]{2,1,0:T(8,128)(2,1)S(1)}, u32[]{:S(2)}, u32[]{:S(2)}) async-start(bf16[8,80,128]{2,1,0:T(8,128)(2,1)} %bitcast.20), calls=%async_computation.3 | async-start | bytes 327680 | tf_op jit(solution)/shard_map/all_to_all | solution.py:401
  (4 other events, 4.2 us)

commit v4 on v3

--- a/solution.py
+++ b/solution.py
@@ -26,7 +26,7 @@
 
 
 NT = (((1,), (1,)), ((), ()))
-VMEM_LIMIT = 56 * 1024 * 1024
+MIB = 1024 * 1024
 DEQUANT_ROWS = 128
 LOGIT_ROWS = 256
 
@@ -69,7 +69,7 @@
         ],
         out_specs=pl.BlockSpec((DEQUANT_ROWS, width), lambda i: (i, 0)),
         out_shape=jax.ShapeDtypeStruct((2 * rows, width), BF16),
-        compiler_params=pltpu.CompilerParams(vmem_limit_bytes=VMEM_LIMIT),
+        compiler_params=pltpu.CompilerParams(vmem_limit_bytes=12 * MIB),
         cost_estimate=pl.CostEstimate(
             flops=2 * rows * width, transcendentals=0, bytes_accessed=8 * rows * width
         ),
@@ -99,7 +99,7 @@
         ],
         out_specs=pl.BlockSpec((width, DEQUANT_ROWS), lambda i: (0, i)),
         out_shape=jax.ShapeDtypeStruct((width, 2 * rows), BF16),
-        compiler_params=pltpu.CompilerParams(vmem_limit_bytes=VMEM_LIMIT),
+        compiler_params=pltpu.CompilerParams(vmem_limit_bytes=8 * MIB),
         cost_estimate=pl.CostEstimate(
             flops=0, transcendentals=0, bytes_accessed=8 * rows * width
         ),
@@ -245,7 +245,7 @@
             ],
         ),
         out_shape=out_shape,
-        compiler_params=pltpu.CompilerParams(vmem_limit_bytes=VMEM_LIMIT),
+        compiler_params=pltpu.CompilerParams(vmem_limit_bytes=22 * MIB),
         cost_estimate=pl.CostEstimate(
             flops=4 * rows * tokens * (width_t + width_s),
             transcendentals=4 * rows * tokens,
@@ -300,7 +300,7 @@
             out_specs=[lg_spec, lg_spec, pl.BlockSpec((1, n_y, *cut), lambda i, y: (i, 0, 0, 0))],
         ),
         out_shape=[lg, lg, jax.ShapeDtypeStruct((n_x, n_y, *cut), BF16)],
-        compiler_params=pltpu.CompilerParams(vmem_limit_bytes=VMEM_LIMIT),
+        compiler_params=pltpu.CompilerParams(vmem_limit_bytes=22 * MIB),
         cost_estimate=pl.CostEstimate(
             flops=4 * vocab * tokens * width,
             transcendentals=4 * vocab * tokens,
@@ -368,6 +368,7 @@
         scale=loss_scale.astype(F32)[None],
         copies=n_x * n_y,
     )
+    mine, after, before, quarters = lax.optimization_barrier((mine, after, before, quarters))
     opposite_s = rolled(jnp.stack([q[:, width_t:] for q in quarters]), n_x - x).reshape(tok, -1)
     seen = lax.all_to_all(mine, ("x", "y"), 0, 0, tiled=True)
     scales = jnp.sum(seen[:n_y, 5], axis=0)

time: 176 us -> 222 us (1.26)
  waiting for transfers between devices: 47.6 us -> 94.3 us
  Pallas kernels: 57.1 us -> 41.1 us
  local copies, waits for them, and re-layouts: 18 us -> 28.9 us
  starting transfers between devices: 33.4 us -> 37.6 us
    ppermute x11, waiting for transfers between devices: 10.2 us -> 54.4 us  [shift(): return lax.ppermute(a, axis, [((i + by) % n, i) for i in range(n)])]
    unnamed x34 -> x50, local copies, waits for them, and re-layouts: 9.36 us -> 18 us
    pallas_call x2, Pallas kernels: 27 us -> 20.4 us  [logits_of(): pl.pallas_call(functools.partial(logits_kernel, steps, len(pieces)), grid...]
    all_to_all x1, waiting for transfers between devices: 2.66 us -> 6.5 us  [local(): seen = lax.all_to_all(mine, ('x', 'y'), 0, 0, tiled=True)]
    pallas_call x1, Pallas kernels: 12.9 us -> 9.22 us  [dequantize(): pl.pallas_call(functools.partial(dequant_kernel, steps), grid=(2 * steps,...]
    pallas_call x1, Pallas kernels: 9.22 us -> 5.56 us  [gradients(): pl.pallas_call(grad_kernel, grid_spec=pltpu.PrefetchScalarGridSpec(num_sc...]
    ppermute x11, starting transfers between devices: 10.8 us -> 13.3 us  [shift(): return lax.ppermute(a, axis, [((i + by) % n, i) for i in range(n)])]
  transfers between devices with their start and end apart: 15 -> 15, of which waited for: 6 -> 9; matrix products, arithmetic and copies ran while one was open for 17% -> 11% of each run, Pallas kernels for 25% -> 14%
where the time goes in v4:
time: 222 us; the launch traced here: 220 us
  waiting for transfers between devices  94.3 us (42%)
  Pallas kernels  41.1 us (19%)
  starting transfers between devices  37.6 us (17%)
  local copies, waits for them, and re-layouts  28.9 us (13%)
  matrix products  11.9 us (5%)
  other arithmetic  5.23 us (2%)
    ppermute x11, waiting for transfers between devices, shift(): return lax.ppermute(a, axis, [((i + by) % n, i) for i in range(n)])  54.4 us
    all_to_all x1, waiting for transfers between devices, local(): got = lax.all_to_all(blocks, ('x', 'y'), 0, 0, tiled=True)  24.4 us
    pallas_call x2, Pallas kernels, logits_of(): pl.pallas_call(functools.partial(logits_kernel, steps, len(pieces)), grid...  20.4 us
    unnamed x50, local copies, waits for them, and re-layouts  18 us
    ppermute x11, starting transfers between devices, shift(): return lax.ppermute(a, axis, [((i + by) % n, i) for i in range(n)])  13.3 us
    pallas_call x1, Pallas kernels, dequantize(): pl.pallas_call(functools.partial(dequant_kernel, steps), grid=(2 * steps,...  9.22 us
    all_to_all x1, starting transfers between devices, to_all(): lax.all_to_all(jnp.broadcast_to(a[None], (n, *a.shape)), axes, 0, 0, tile...  8.47 us
    all_to_all x1, waiting for transfers between devices, local(): seen = lax.all_to_all(mine, ('x', 'y'), 0, 0, tiled=True)  6.5 us
  transfers between devices with their start and end apart: 15, of which 9 were waited for; matrix products, arithmetic and copies ran while one was open for 11% of the time, Pallas kernels for 14%

profile of v4, /device:TPU:8, one launch (start us, length us, event | category | flops | bytes accessed | tf_op | source)
XLA Modules:
  0.0 220.1 jit_solution(9467179608834514795)
XLA Ops:
  1.3 2.6 %constant_dynamic-update-slice_fusion.1 = bf16[128,7936]{1,0:T(8,128)(2,1)} fusion(bf16[128,5376]{1,0:T(8,128)(2,1)} %param.6), kind=kLoop, calls=%fused_computation.26 | loop fusion | bytes 2752512
  5.8 2.2 collective-permute-start
  11.2 5.7 %collective-permute-start.2 = (bf16[32,7936]{1,0:T(8,128)(2,1)S(1)}, bf16[32,7936]{1,0:T(8,128)(2,1)S(1)}, u32[]{:S(2)}, u32[]{:S(2)}) collective-permute-start(bf16[32,7936]{1,0:T(8,128)(2,1)S(1)} %pad_maximum_fusion.1), channel_id=1, source_target_pairs={{4,0},{6,2},{0,4},{2,6},{5,1},{7,3},{1,5},{3,7},{12,8},{14,10},{8,... | collective-permute-start | bytes 1523720 | tf_op jit(solution)/shard_map/ppermute | solution.py:20
  16.9 47.2 %collective-permute-done.2.rest_1_ = bf16[32,7936]{1,0:T(8,128)(2,1)S(1)} collective-permute-done((bf16[32,7936]{1,0:T(8,128)(2,1)S(1)}, bf16[32,7936]{1,0:T(8,128)(2,1)S(1)}, u32[]{:S(2)}, u32[]{:S(2)}) %collective-permute-start.2) | collective-permute-done | bytes 507936 | tf_op jit(solution)/shard_map/ppermute | solution.py:20
  64.1 2.8 %collective-permute-start.6 = (bf16[32,7936]{1,0:T(8,128)(2,1)S(1)}, bf16[32,7936]{1,0:T(8,128)(2,1)}, u32[]{:S(2)}, u32[]{:S(2)}) collective-permute-start(bf16[32,7936]{1,0:T(8,128)(2,1)S(1)} %collective-permute-done.2.rest_1_), channel_id=1, source_target_pairs={{64,0},{128,64},{192,128},{0,192},{65,1},{129,65},{193,129},{1,193... | collective-permute-start | bytes 1523720 | tf_op jit(solution)/shard_map/ppermute | solution.py:20
  68.6 6.0 %turn.1.turned_ref = bf16[2560,1024]{1,0:T(8,128)(2,1)S(1)} custom-call(bf16[512,2560]{1,0:T(8,128)(2,1)S(1)} %copy-done, bf16[512,2560]{1,0:T(8,128)(2,1)} %collective-permute-done.4.rest_7_.other_ref.rest_4_), custom_call_target="tpu_custom_call" | custom-call | bytes 10485760 | tf_op jit(solution)/shard_map/turn/pallas_call | solution.py:93
  74.6 2.4 %copy-done.1 = bf16[2560,1024]{1,0:T(8,128)(2,1)} copy-done((bf16[2560,1024]{1,0:T(8,128)(2,1)}, bf16[2560,1024]{1,0:T(8,128)(2,1)S(1)}, u32[]{:S(2)}) %copy-start.1) | copy-done | bytes 5242904
  77.0 9.2 %dequantize.1.rest_5_.rest_2_ = bf16[1024,5376]{1,0:T(8,128)(2,1)S(1)} custom-call(bf16[512,5376]{1,0:T(8,128)(2,1)S(1)} %bitcast.99, bf16[512,5376]{1,0:T(8,128)(2,1)} %collective-permute-done.3.other_ref, f32[512,42]{1,0:T(8,128)S(1)} %copy.22.own_scale_ref, f32[512,42]{1,0:T(8,128)S(1)} %copy-done.4), custom_call_target="tpu_custom_call" | custom-call | flops 5505024 | bytes 22020096 | tf_op jit(solution)/shard_map/dequantize/pallas_call | solution.py:61
  88.0 3.8 %collective-permute-done.8.rest_4_ = bf16[32,7936]{1,0:T(8,128)(2,1)} collective-permute-done((bf16[32,7936]{1,0:T(8,128)(2,1)S(1)}, bf16[32,7936]{1,0:T(8,128)(2,1)}, u32[]{:S(2)}, u32[]{:S(2)}) %collective-permute-start.8) | collective-permute-done | bytes 507936 | tf_op jit(solution)/shard_map/ppermute | solution.py:20
  91.7 9.7 %logits.2 = (f32[1024,256]{1,0:T(8,128)S(1)}, f32[1024,256]{1,0:T(8,128)S(1)}, f32[8,256]{1,0:T(8,128)S(1)}) custom-call(s32[2]{0:T(128)S(1)} %pad_add_fusion.place_ref.y_ref, bf16[128,7936]{1,0:T(8,128)(2,1)} %constant_dynamic-update-slice_fusion.rest_0_, bf16[32,7936]{1,0:T(8,128)(2,1)S(1)} %collective-permute-done.2.rest_1_, ...), custom_call_target="tpu_custom_call" | custom-call | flops 4160749568 | bytes 22413312 | tf_op jit(solution)/shard_map/logits/pallas_call | solution.py:235
  103.5 10.6 %logits.3 = (f32[1024,256]{1,0:T(8,128)S(1)}, f32[1024,256]{1,0:T(8,128)S(1)}, f32[8,256]{1,0:T(8,128)}, f32[16,8,512]{2,1,0:T(8,128)}) custom-call(s32[2]{0:T(128)S(1)} %pad_add_fusion.place_ref.y_ref, bf16[128,7936]{1,0:T(8,128)(2,1)} %collective-permute-done.rest_0_, bf16[128,7936]{1,0:T(8,128)(2,1)} %collective-permute-done.1.rest_1_, ...), custom_call_target="tpu_custom_call" | custom-call | flops 4160749568 | bytes 22413312 | tf_op jit(solution)/shard_map/logits/pallas_call | solution.py:235
  123.9 5.5 %all-to-all-start = ((f32[16,8,512]{2,1,0:T(8,128)}), f32[16,8,512]{2,1,0:T(8,128)S(1)}, u32[]{:S(2)}, u32[]{:S(2)}) async-start(f32[16,8,512]{2,1,0:T(8,128)} %get-tuple-element.36), calls=%async_computation | async-start | bytes 524288 | tf_op jit(solution)/shard_map/all_to_all | solution.py:373
  130.3 6.5 %all-to-all-done = f32[16,8,512]{2,1,0:T(8,128)S(1)} async-done(((f32[16,8,512]{2,1,0:T(8,128)}), f32[16,8,512]{2,1,0:T(8,128)S(1)}, u32[]{:S(2)}, u32[]{:S(2)}) %all-to-all-start) | async-done | bytes 262176 | tf_op jit(solution)/shard_map/all_to_all | solution.py:373
  137.7 8.5 %all-to-all-start.1 = ((f32[8,5,512]{2,1,0:T(8,128)}), f32[8,5,512]{2,1,0:T(8,128)S(1)}, u32[]{:S(2)}, u32[]{:S(2)}) async-start(f32[8,5,512]{2,1,0:T(8,128)} %broadcast_in_dim.20), calls=%async_computation.1 | async-start | bytes 262144 | tf_op jit(solution)/shard_map/all_to_all | solution.py:315
  146.2 3.0 %pad_maximum_fusion = bf16[512,2560]{1,0:T(8,128)(2,1)} fusion(bf16[128,2560]{1,0:T(8,128)(2,1)} %slice.97, bf16[128,2560]{1,0:T(8,128)(2,1)} %slice.96, bf16[128,2560]{1,0:T(8,128)(2,1)} %bitcast.100, bf16[128,2560]{1,0:T(8,128)(2,1)} %param.7), kind=kLoop, calls=%fused_computation.1 | loop fusion | flops 10485760 | bytes 5242880 | tf_op jit(solution)/shard_map/concatenate | solution.py:394
  149.3 6.0 %all-to-all-done.1 = f32[8,5,512]{2,1,0:T(8,128)S(1)} async-done(((f32[8,5,512]{2,1,0:T(8,128)}), f32[8,5,512]{2,1,0:T(8,128)S(1)}, u32[]{:S(2)}, u32[]{:S(2)}) %all-to-all-start.1) | async-done | bytes 81952 | tf_op jit(solution)/shard_map/all_to_all | solution.py:315
  155.6 2.5 %copy-done.2 = bf16[2560,1024]{1,0:T(8,128)(2,1)S(1)} copy-done((bf16[2560,1024]{1,0:T(8,128)(2,1)S(1)}, bf16[2560,1024]{1,0:T(8,128)(2,1)}, u32[]{:S(2)}) %copy-start.2) | copy-done | bytes 5242904
  159.3 5.6 %gradients.1 = (bf16[512,512]{1,0:T(8,128)(2,1)S(1)}, bf16[512,512]{1,0:T(8,128)(2,1)S(1)}, bf16[4,4,640,128]{3,2,1,0:T(8,128)(2,1)}) custom-call(s32[2]{0:T(128)S(1)} %pad_add_fusion.place_ref.y_ref, f32[8,512]{1,0:T(8,128)S(1)} %pad_maximum_fusion.2.rows_ref, f32[1024,256]{1,0:T(8,128)S(1)} %copy-done.6, f32[1024,256]{1,0:T(8,128)S(1)} %copy-done.8, ...), custom_call_target="tpu_custom_call" | custom-call | flops 2684354560 | bytes 13107200 | tf_op jit(solution)/shard_map/gradients/pallas_call | solution.py:287
  166.5 5.3 %all-to-all-start.2 = ((bf16[16,640,128]{2,1,0:T(8,128)(2,1)}), bf16[16,640,128]{2,1,0:T(8,128)(2,1)S(1)}, u32[]{:S(2)}, u32[]{:S(2)}) async-start(bf16[16,640,128]{2,1,0:T(8,128)(2,1)} %bitcast.19), calls=%async_computation.2 | async-start | bytes 5242880 | tf_op jit(solution)/shard_map/all_to_all | solution.py:400
  174.0 5.6 %fusion.21 = f32[512,2560]{1,0:T(8,128)} fusion(bf16[512,512]{1,0:T(8,128)(2,1)S(1)} %collective-permute-done.9, bf16[512,2560]{1,0:T(8,128)(2,1)} %collective-permute-done.10), kind=kOutput, calls=%fused_computation.58 | convolution fusion | flops 1342177280 | bytes 8388608 | tf_op jit(solution)/shard_map/dot_general | solution.py:406
  179.6 24.4 %all-to-all-done.2 = bf16[16,640,128]{2,1,0:T(8,128)(2,1)S(1)} async-done(((bf16[16,640,128]{2,1,0:T(8,128)(2,1)}), bf16[16,640,128]{2,1,0:T(8,128)(2,1)S(1)}, u32[]{:S(2)}, u32[]{:S(2)}) %all-to-all-start.2) | async-done | bytes 2621472 | tf_op jit(solution)/shard_map/all_to_all | solution.py:400
  205.0 5.0 %all-to-all-start.3 = ((bf16[8,80,128]{2,1,0:T(8,128)(2,1)}), bf16[8,80,128]{2,1,0:T(8,128)(2,1)S(1)}, u32[]{:S(2)}, u32[]{:S(2)}) async-start(bf16[8,80,128]{2,1,0:T(8,128)(2,1)} %bitcast.20), calls=%async_computation.3 | async-start | bytes 327680 | tf_op jit(solution)/shard_map/all_to_all | solution.py:402
  210.1 6.4 %add_convert_fusion = bf16[512,2560]{1,0:T(8,128)(2,1)} fusion(f32[512,2560]{1,0:T(8,128)} %fusion.21, bf16[512,512]{1,0:T(8,128)(2,1)S(1)} %copy-done.16, bf16[128,2560]{1,0:T(8,128)(2,1)} %slice.97, bf16[128,2560]{1,0:T(8,128)(2,1)} %slice.96, bf16[128,2560]{1,0:T(8,128)(2,1)} %bitcast.101, bf16[128,2560]{1,0:T(8,128)(2,1)} %param.7), kind=kOutput, calls=%fused_computation | convolution fusion | flops 1355284480 | bytes 11010048 | tf_op jit(solution)/shard_map/dot_general | solution.py:405
  216.4 3.1 %all-to-all-done.3 = bf16[8,80,128]{2,1,0:T(8,128)(2,1)S(1)} async-done(((bf16[8,80,128]{2,1,0:T(8,128)(2,1)}), bf16[8,80,128]{2,1,0:T(8,128)(2,1)S(1)}, u32[]{:S(2)}, u32[]{:S(2)}) %all-to-all-start.3) | async-done | bytes 163872 | tf_op jit(solution)/shard_map/all_to_all | solution.py:402
  (95 shorter events, 29.8 us)
Async XLA Ops:
  0.6 68.0 %copy-start = (bf16[512,2560]{1,0:T(8,128)(2,1)S(1)}, bf16[512,2560]{1,0:T(8,128)(2,1)}, u32[]{:S(2)}) copy-start(bf16[512,2560]{1,0:T(8,128)(2,1)} %rest_3_.1) | copy-start | bytes 7864324
  0.7 68.0 %copy-start.18 = (bf16[128]{0:T(256)(128)(2,1)S(1)}, bf16[128]{0:T(256)(128)(2,1)}, u32[]{:S(2)}) copy-start(bf16[128]{0:T(256)(128)(2,1)} %param.11) | copy-start | bytes 772
  0.7 63.4 %collective-permute-start.3 = (bf16[512,5376]{1,0:T(8,128)(2,1)}, bf16[512,5376]{1,0:T(8,128)(2,1)}, u32[]{:S(2)}, u32[]{:S(2)}) collective-permute-start(bf16[512,5376]{1,0:T(8,128)(2,1)} %own_ref.2), channel_id=1, source_target_pairs={{1,0},{0,1},{3,2},{2,3},{5,4},{4,5},{7,6},{6,7},{9,8},{8,9},{11,10... | collective-permute-start | bytes 16515080 | tf_op jit(solution)/shard_map/ppermute | solution.py:20
  0.8 63.3 %collective-permute-start.4 = (bf16[512,2560]{1,0:T(8,128)(2,1)}, bf16[512,2560]{1,0:T(8,128)(2,1)}, u32[]{:S(2)}, u32[]{:S(2)}) collective-permute-start(bf16[512,2560]{1,0:T(8,128)(2,1)} %rest_3_.1), channel_id=1, source_target_pairs={{1,0},{0,1},{3,2},{2,3},{5,4},{4,5},{7,6},{6,7},{9,8},{8,9},{11,10... | collective-permute-start | bytes 7864328 | tf_op jit(solution)/shard_map/ppermute | solution.py:20
  5.8 97.7 %collective-permute-start = (bf16[128,7936]{1,0:T(8,128)(2,1)}, bf16[128,7936]{1,0:T(8,128)(2,1)}, u32[]{:S(2)}, u32[]{:S(2)}) collective-permute-start(bf16[128,7936]{1,0:T(8,128)(2,1)} %constant_dynamic-update-slice_fusion.rest_0_), channel_id=1, source_target_pairs={{2,0},{4,2},{6,4},{0,6},{3,1},{5,3},{7,5},{1,7},{10,8},{12,10},{14... | collective-permute-start | bytes 6094856 | tf_op jit(solution)/shard_map/ppermute | solution.py:20
  8.0 95.5 %collective-permute-start.1 = (bf16[128,7936]{1,0:T(8,128)(2,1)}, bf16[128,7936]{1,0:T(8,128)(2,1)}, u32[]{:S(2)}, u32[]{:S(2)}) collective-permute-start(bf16[128,7936]{1,0:T(8,128)(2,1)} %constant_dynamic-update-slice_fusion.rest_0_), channel_id=1, source_target_pairs={{6,0},{0,2},{2,4},{4,6},{7,1},{1,3},{3,5},{5,7},{14,8},{8,10},{10,... | collective-permute-start | bytes 6094856 | tf_op jit(solution)/shard_map/ppermute | solution.py:20
  8.1 2.4 %collective-permute-start.5 = (f32[512,42]{1,0:T(8,128)S(1)}, f32[512,42]{1,0:T(8,128)S(1)}, u32[]{:S(2)}, u32[]{:S(2)}) collective-permute-start(f32[512,42]{1,0:T(8,128)S(1)} %copy.22.own_scale_ref), channel_id=1, source_target_pairs={{1,0},{0,1},{3,2},{2,3},{5,4},{4,5},{7,6},{6,7},{9,8},{8,9},{11,10... | collective-permute-start | bytes 258056 | tf_op jit(solution)/shard_map/ppermute | solution.py:20
  11.2 52.8 %collective-permute-start.2 = (bf16[32,7936]{1,0:T(8,128)(2,1)S(1)}, bf16[32,7936]{1,0:T(8,128)(2,1)S(1)}, u32[]{:S(2)}, u32[]{:S(2)}) collective-permute-start(bf16[32,7936]{1,0:T(8,128)(2,1)S(1)} %pad_maximum_fusion.1), channel_id=1, source_target_pairs={{4,0},{6,2},{0,4},{2,6},{5,1},{7,3},{1,5},{3,7},{12,8},{14,10},{8,... | collective-permute-start | bytes 1523720 | tf_op jit(solution)/shard_map/ppermute | solution.py:20
  64.1 23.9 %collective-permute-start.6 = (bf16[32,7936]{1,0:T(8,128)(2,1)S(1)}, bf16[32,7936]{1,0:T(8,128)(2,1)}, u32[]{:S(2)}, u32[]{:S(2)}) collective-permute-start(bf16[32,7936]{1,0:T(8,128)(2,1)S(1)} %collective-permute-done.2.rest_1_), channel_id=1, source_target_pairs={{64,0},{128,64},{192,128},{0,192},{65,1},{129,65},{193,129},{1,193... | collective-permute-start | bytes 1523720 | tf_op jit(solution)/shard_map/ppermute | solution.py:20
  66.8 21.1 %collective-permute-start.7 = (bf16[32,7936]{1,0:T(8,128)(2,1)S(1)}, bf16[32,7936]{1,0:T(8,128)(2,1)}, u32[]{:S(2)}, u32[]{:S(2)}) collective-permute-start(bf16[32,7936]{1,0:T(8,128)(2,1)S(1)} %collective-permute-done.2.rest_1_), channel_id=1, source_target_pairs={{128,0},{192,64},{0,128},{64,192},{129,1},{193,65},{1,129},{65,193... | collective-permute-start | bytes 1523720 | tf_op jit(solution)/shard_map/ppermute | solution.py:20
  67.6 24.1 %collective-permute-start.8 = (bf16[32,7936]{1,0:T(8,128)(2,1)S(1)}, bf16[32,7936]{1,0:T(8,128)(2,1)}, u32[]{:S(2)}, u32[]{:S(2)}) collective-permute-start(bf16[32,7936]{1,0:T(8,128)(2,1)S(1)} %collective-permute-done.2.rest_1_), channel_id=1, source_target_pairs={{192,0},{0,64},{64,128},{128,192},{193,1},{1,65},{65,129},{129,193... | collective-permute-start | bytes 1523720 | tf_op jit(solution)/shard_map/ppermute | solution.py:20
  68.6 8.4 %slice-start = ((s8[5505024]{0:T(1024)(128)(4,1)}), s8[4194304]{0:T(1024)(128)(4,1)S(1)}, s32[]{:S(2)}) async-start(s8[5505024]{0:T(1024)(128)(4,1)} %bitcast.98), calls=%async_computation.4 | async-start | bytes 8388608
  68.6 8.4 %slice-start.1 = ((s8[5505024]{0:T(1024)(128)(4,1)}), s8[1310720]{0:T(1024)(128)(4,1)S(1)}, s32[]{:S(2)}) async-start(s8[5505024]{0:T(1024)(128)(4,1)} %bitcast.98), calls=%async_computation.5 | async-start | bytes 2621440
  68.6 8.4 %copy-start.4 = (f32[512,42]{1,0:T(8,128)S(1)}, f32[512,42]{1,0:T(8,128)}, u32[]{:S(2)}) copy-start(f32[512,42]{1,0:T(8,128)} %copy-done.3) | copy-start | bytes 258052
  123.9 12.9 %all-to-all-start = ((f32[16,8,512]{2,1,0:T(8,128)}), f32[16,8,512]{2,1,0:T(8,128)S(1)}, u32[]{:S(2)}, u32[]{:S(2)}) async-start(f32[16,8,512]{2,1,0:T(8,128)} %get-tuple-element.36), calls=%async_computation | async-start | bytes 524288 | tf_op jit(solution)/shard_map/all_to_all | solution.py:373
  137.7 17.5 %all-to-all-start.1 = ((f32[8,5,512]{2,1,0:T(8,128)}), f32[8,5,512]{2,1,0:T(8,128)S(1)}, u32[]{:S(2)}, u32[]{:S(2)}) async-start(f32[8,5,512]{2,1,0:T(8,128)} %broadcast_in_dim.20), calls=%async_computation.1 | async-start | bytes 262144 | tf_op jit(solution)/shard_map/all_to_all | solution.py:315
  146.2 9.4 %copy-start.6 = (f32[1024,256]{1,0:T(8,128)S(1)}, f32[1024,256]{1,0:T(8,128)}, u32[]{:S(2)}) copy-start(f32[1024,256]{1,0:T(8,128)} %copy-done.5) | copy-start | bytes 3145732
  146.2 9.4 %copy-start.8 = (f32[1024,256]{1,0:T(8,128)S(1)}, f32[1024,256]{1,0:T(8,128)}, u32[]{:S(2)}) copy-start(f32[1024,256]{1,0:T(8,128)} %copy-done.7) | copy-start | bytes 3145732
  146.2 9.4 %copy-start.10 = (f32[1024,256]{1,0:T(8,128)S(1)}, f32[1024,256]{1,0:T(8,128)}, u32[]{:S(2)}) copy-start(f32[1024,256]{1,0:T(8,128)} %copy-done.9) | copy-start | bytes 3145732
  149.3 24.7 %collective-permute-start.10 = (bf16[512,2560]{1,0:T(8,128)(2,1)}, bf16[512,2560]{1,0:T(8,128)(2,1)}, u32[]{:S(2)}, u32[]{:S(2)}) collective-permute-start(bf16[512,2560]{1,0:T(8,128)(2,1)} %pad_maximum_fusion), channel_id=1, source_target_pairs={{1,0},{0,1},{3,2},{2,3},{5,4},{4,5},{7,6},{6,7},{9,8},{8,9},{11,10... | collective-permute-start | bytes 7864328 | tf_op jit(solution)/shard_map/ppermute | solution.py:20
  166.5 37.5 %all-to-all-start.2 = ((bf16[16,640,128]{2,1,0:T(8,128)(2,1)}), bf16[16,640,128]{2,1,0:T(8,128)(2,1)S(1)}, u32[]{:S(2)}, u32[]{:S(2)}) async-start(bf16[16,640,128]{2,1,0:T(8,128)(2,1)} %bitcast.19), calls=%async_computation.2 | async-start | bytes 5242880 | tf_op jit(solution)/shard_map/all_to_all | solution.py:400
  171.8 2.2 %collective-permute-start.9 = (bf16[512,512]{1,0:T(8,128)(2,1)S(1)}, bf16[512,512]{1,0:T(8,128)(2,1)S(1)}, u32[]{:S(2)}, u32[]{:S(2)}) collective-permute-start(bf16[512,512]{1,0:T(8,128)(2,1)S(1)} %copy-done.14), channel_id=1, source_target_pairs={{1,0},{0,1},{3,2},{2,3},{5,4},{4,5},{7,6},{6,7},{9,8},{8,9},{11,10... | collective-permute-start | bytes 1572872 | tf_op jit(solution)/shard_map/ppermute | solution.py:20
  179.6 30.5 %copy-start.16 = (bf16[512,512]{1,0:T(8,128)(2,1)S(1)}, bf16[512,512]{1,0:T(8,128)(2,1)}, u32[]{:S(2)}) copy-start(bf16[512,512]{1,0:T(8,128)(2,1)} %copy-done.15) | copy-start | bytes 1572868
  205.0 14.4 %all-to-all-start.3 = ((bf16[8,80,128]{2,1,0:T(8,128)(2,1)}), bf16[8,80,128]{2,1,0:T(8,128)(2,1)S(1)}, u32[]{:S(2)}, u32[]{:S(2)}) async-start(bf16[8,80,128]{2,1,0:T(8,128)(2,1)} %bitcast.20), calls=%async_computation.3 | async-start | bytes 327680 | tf_op jit(solution)/shard_map/all_to_all | solution.py:402
  (12 other events, 27.0 us)

commit v5 on v4

--- a/solution.py
+++ b/solution.py
@@ -29,6 +29,7 @@
 MIB = 1024 * 1024
 DEQUANT_ROWS = 128
 LOGIT_ROWS = 256
+WEIGHT_COLUMNS = 512
 
 
 def two_sources(i, steps):
@@ -161,17 +162,18 @@
     pieces_hbm, rest = rest[:n_pieces], rest[n_pieces:]
     (table_ref, weight_ref, weight_p_ref), rest = rest[:3], rest[3:]
     tok = pieces_hbm[0].shape[0]
-    spread = len(rest) > 5
+    spread = len(rest) > 6
     first_stat_ref, scale_ref = rest[:2] if spread else (None, None)
     rest = rest[2:] if spread else rest
-    t_ref, s_ref, stat_ref = rest[:3]
-    spread_ref = rest[3] if spread else None
+    t_ref, s_ref, stat_ref, student_ref = rest[:4]
+    spread_ref = rest[4] if spread else None
     pair, sem = rest[-2:]
     step = pl.program_id(0)
 
     @pl.when(step == 0)
     def _():
         load_pair(place_ref, pieces_hbm, pair, sem)
+        student_ref[...] = pair[:, table_ref.shape[1] :]
 
     @pl.when(step < steps)
     def _():
@@ -223,8 +225,14 @@
         pl.BlockSpec((LOGIT_ROWS, tokens), lambda i, y: (i, 0)),
         pl.BlockSpec((LOGIT_ROWS, tokens), lambda i, y: (i, 0)),
         pl.BlockSpec((8, tokens), lambda i, y: (0, 0)),
+        pl.BlockSpec((tokens, width_s), lambda i, y: (0, 0)),
     ]
-    out_shape = [tile, tile, jax.ShapeDtypeStruct((8, tokens), F32)]
+    out_shape = [
+        tile,
+        tile,
+        jax.ShapeDtypeStruct((8, tokens), F32),
+        jax.ShapeDtypeStruct((tokens, width_s), BF16),
+    ]
     operands = [place, *pieces, table, weight, weight_p]
     if first_stats is not None:
         in_specs.append(pl.BlockSpec((8, tokens), lambda i, y: (0, 0)))
@@ -331,6 +339,35 @@
     )
 
 
+def weight_kernel(own_ref, from_ref, s0_ref, s1_ref, s0_p_ref, s1_p_ref, out_ref):
+    half = s0_ref.shape[0]
+    total = jnp.dot(own_ref[:, :half], s0_ref[...], preferred_element_type=F32)
+    total += jnp.dot(own_ref[:, half:], s1_ref[...], preferred_element_type=F32)
+    total += jnp.dot(from_ref[:, :half], s0_p_ref[...], preferred_element_type=F32)
+    total += jnp.dot(from_ref[:, half:], s1_p_ref[...], preferred_element_type=F32)
+    out_ref[...] = total.astype(BF16)
+
+
+def weight_gradient(own, from_p, *students):
+    rows, tokens = own.shape
+    half, width = students[0].shape
+    whole = pl.BlockSpec((rows, tokens), lambda i: (0, 0))
+    return pl.pallas_call(
+        weight_kernel,
+        grid=(width // WEIGHT_COLUMNS,),
+        in_specs=[whole, whole] + [pl.BlockSpec((half, WEIGHT_COLUMNS), lambda i: (0, i))] * 4,
+        out_specs=pl.BlockSpec((rows, WEIGHT_COLUMNS), lambda i: (0, i)),
+        out_shape=jax.ShapeDtypeStruct((rows, width), BF16),
+        compiler_params=pltpu.CompilerParams(vmem_limit_bytes=14 * MIB),
+        cost_estimate=pl.CostEstimate(
+            flops=4 * rows * tokens * width,
+            transcendentals=0,
+            bytes_accessed=2 * width * (rows + 4 * half) + 4 * rows * tokens,
+        ),
+        name="weight_gradient",
+    )(own, from_p, *students)
+
+
 def local(
     teacher_hidden, student_hidden, teacher_codes, teacher_scales, student_weight, loss_scale
 ):
@@ -346,7 +383,8 @@
     ]
     quarter = shift(jnp.concatenate(piece, axis=1), "y", 2)
     hidden = jnp.concatenate([teacher_hidden, student_hidden], axis=1)
-    after, before = shift(hidden, "y", 1), shift(hidden, "y", 3)
+    quarter, whole = lax.optimization_barrier((quarter, hidden))
+    after, before = shift(whole, "y", 1), shift(whole, "y", 3)
     codes_p = shift(teacher_codes, "c", 1)
     weight_p = shift(student_weight, "c", 1)
     scales_p = shift(teacher_scales, "c", 1)
@@ -358,9 +396,10 @@
     turned = turned_over(student_weight, weight_p)
 
     tables = (table, student_weight, weight_p)
-    t0, s0, stats0 = logits_of(place, [hidden, *quarters], *tables)
+    t0, s0, stats0, students0 = logits_of(place, [hidden, *quarters], *tables)
     after, before, stats0, turned = lax.optimization_barrier((after, before, stats0, turned))
-    t1, s1, _, mine = logits_of(
+    students0_p = shift(students0, "c", 1)
+    t1, s1, _, students1, mine = logits_of(
         place,
         [after, before],
         *tables,
@@ -368,8 +407,6 @@
         scale=loss_scale.astype(F32)[None],
         copies=n_x * n_y,
     )
-    mine, after, before, quarters = lax.optimization_barrier((mine, after, before, quarters))
-    opposite_s = rolled(jnp.stack([q[:, width_t:] for q in quarters]), n_x - x).reshape(tok, -1)
     seen = lax.all_to_all(mine, ("x", "y"), 0, 0, tiled=True)
     scales = jnp.sum(seen[:n_y, 5], axis=0)
     totals = combine(to_all(combine(seen), "z"))
@@ -391,10 +428,8 @@
         n_y,
     )
     from_p = shift(other, "c", 1)
-    students = jnp.concatenate(
-        [student_hidden, opposite_s, after[:, width_t:], before[:, width_t:]]
-    )
-    students_p = shift(students, "c", 1)
+    students1_p = shift(students1, "c", 1)
+    grad_weight = weight_gradient(own, from_p, students0, students1, students0_p, students1_p)
 
     blocks = blocks.reshape(n_x * n_y, width_s // n_x, tok)
     got = lax.all_to_all(blocks, ("x", "y"), 0, 0, tiled=True)
@@ -402,9 +437,7 @@
     got = lax.all_to_all(got, "z", 0, 0, tiled=True)
     grad_hidden = jnp.sum(got.astype(F32), axis=0).astype(BF16).T
 
-    grad_weight = jnp.dot(own, students, preferred_element_type=F32)
-    grad_weight += jnp.dot(from_p, students_p, preferred_element_type=F32)
-    return kl, grad_hidden, grad_weight.astype(BF16)
+    return kl, grad_hidden, grad_weight
 
 
 def solution(mesh):

time: 222 us -> 181 us (0.82)
  waiting for transfers between devices: 94.3 us -> 57.8 us
  blocking collectives: 0 us -> 13.6 us
  matrix products: 11.9 us -> 0 us
  starting transfers between devices: 37.6 us -> 28.1 us
  Pallas kernels: 41.1 us -> 47.8 us
  local copies, waits for them, and re-layouts: 28.9 us -> 26.4 us
    ppermute x11 -> x12, waiting for transfers between devices: 54.4 us -> 17.9 us  [shift(): return lax.ppermute(a, axis, [((i + by) % n, i) for i in range(n)])]
    all_to_all x0 -> x1, blocking collectives: none -> 13.6 us  [local(): seen = lax.all_to_all(mine, ('x', 'y'), 0, 0, tiled=True)]
    dot_general x2 -> x0, matrix products: 11.9 us -> none  [the longest x1 6.36 us: local(): grad_weight = jnp.dot(own, students, preferred_element_type=F32)]
    pallas_call x0 -> x1, Pallas kernels: none -> 6.66 us  [weight_gradient(): pl.pallas_call(weight_kernel, grid=(width // WEIGHT_COLUMNS,), in_specs=[...]
    all_to_all x1 -> x0, waiting for transfers between devices: 6.5 us -> none  [local(): seen = lax.all_to_all(mine, ('x', 'y'), 0, 0, tiled=True)]
    all_to_all x1 -> x0, starting transfers between devices: 5.51 us -> none  [local(): seen = lax.all_to_all(mine, ('x', 'y'), 0, 0, tiled=True)]
    all_to_all x1, waiting for transfers between devices: 24.4 us -> 29.7 us  [local(): got = lax.all_to_all(blocks, ('x', 'y'), 0, 0, tiled=True)]
    unnamed x50, local copies, waits for them, and re-layouts: 18 us -> 22.2 us
  transfers between devices with their start and end apart: 15 -> 15, of which waited for: 9 -> 8; matrix products, arithmetic and copies ran while one was open for 11% -> 4% of each run, Pallas kernels for 14% -> 18%
where the time goes in v5:
time: 181 us; the launch traced here: 179 us
  waiting for transfers between devices  57.8 us (32%)
  Pallas kernels  47.8 us (26%)
  starting transfers between devices  28.1 us (16%)
  local copies, waits for them, and re-layouts  26.4 us (15%)
  blocking collectives  13.6 us (8%)
  other arithmetic  3.93 us (2%)
    all_to_all x1, waiting for transfers between devices, local(): got = lax.all_to_all(blocks, ('x', 'y'), 0, 0, tiled=True)  29.7 us
    unnamed x50, local copies, waits for them, and re-layouts  22.2 us
    pallas_call x2, Pallas kernels, logits_of(): pl.pallas_call(functools.partial(logits_kernel, steps, len(pieces)), grid...  20.4 us
    ppermute x12, waiting for transfers between devices, shift(): return lax.ppermute(a, axis, [((i + by) % n, i) for i in range(n)])  17.9 us
    all_to_all x1, blocking collectives, local(): seen = lax.all_to_all(mine, ('x', 'y'), 0, 0, tiled=True)  13.6 us
    ppermute x12, starting transfers between devices, shift(): return lax.ppermute(a, axis, [((i + by) % n, i) for i in range(n)])  10.2 us
    pallas_call x1, Pallas kernels, dequantize(): pl.pallas_call(functools.partial(dequant_kernel, steps), grid=(2 * steps,...  9.21 us
    all_to_all x1, waiting for transfers between devices, to_all(): lax.all_to_all(jnp.broadcast_to(a[None], (n, *a.shape)), axes, 0, 0, tile...  9.05 us
  transfers between devices with their start and end apart: 15, of which 8 were waited for; matrix products, arithmetic and copies ran while one was open for 4% of the time, Pallas kernels for 18%

profile of v5, /device:TPU:8, one launch (start us, length us, event | category | flops | bytes accessed | tf_op | source)
XLA Modules:
  0.0 178.5 jit_solution(16463373273337424346)
XLA Ops:
  3.4 2.4 %collective-permute-start = (bf16[32,7936]{1,0:T(8,128)(2,1)S(1)}, bf16[32,7936]{1,0:T(8,128)(2,1)S(1)}, u32[]{:S(2)}, u32[]{:S(2)}) collective-permute-start(bf16[32,7936]{1,0:T(8,128)(2,1)S(1)} %pad_maximum_fusion), channel_id=1, source_target_pairs={{4,0},{6,2},{0,4},{2,6},{5,1},{7,3},{1,5},{3,7},{12,8},{14,10},{8,... | collective-permute-start | bytes 1523720 | tf_op jit(solution)/shard_map/ppermute | solution.py:20
  7.8 10.7 %collective-permute-done.rest_1_ = bf16[32,7936]{1,0:T(8,128)(2,1)S(1)} collective-permute-done((bf16[32,7936]{1,0:T(8,128)(2,1)S(1)}, bf16[32,7936]{1,0:T(8,128)(2,1)S(1)}, u32[]{:S(2)}, u32[]{:S(2)}) %collective-permute-start) | collective-permute-done | bytes 507936 | tf_op jit(solution)/shard_map/ppermute | solution.py:20
  18.5 2.2 %collective-permute-start.1 = (bf16[128,7936]{1,0:T(8,128)(2,1)}, bf16[128,7936]{1,0:T(8,128)(2,1)}, u32[]{:S(2)}, u32[]{:S(2)}) collective-permute-start(bf16[128,7936]{1,0:T(8,128)(2,1)} %constant_dynamic-update-slice_fusion.rest_0_), channel_id=1, source_target_pairs={{2,0},{4,2},{6,4},{0,6},{3,1},{5,3},{7,5},{1,7},{10,8},{12,10},{14... | collective-permute-start | bytes 6094856 | tf_op jit(solution)/shard_map/ppermute | solution.py:20
  21.0 1.5 collective-permute-done.5.other_scale_ref
  23.2 2.6 %collective-permute-start.6 = (bf16[32,7936]{1,0:T(8,128)(2,1)S(1)}, bf16[32,7936]{1,0:T(8,128)(2,1)}, u32[]{:S(2)}, u32[]{:S(2)}) collective-permute-start(bf16[32,7936]{1,0:T(8,128)(2,1)S(1)} %collective-permute-done.rest_1_), channel_id=1, source_target_pairs={{64,0},{128,64},{192,128},{0,192},{65,1},{129,65},{193,129},{1,193... | collective-permute-start | bytes 1523720 | tf_op jit(solution)/shard_map/ppermute | solution.py:20
  27.6 5.9 %turn.1.turned_ref = bf16[2560,1024]{1,0:T(8,128)(2,1)S(1)} custom-call(bf16[512,2560]{1,0:T(8,128)(2,1)S(1)} %copy-done, bf16[512,2560]{1,0:T(8,128)(2,1)} %collective-permute-done.4.rest_7_.other_ref.rest_4_), custom_call_target="tpu_custom_call" | custom-call | bytes 10485760 | tf_op jit(solution)/shard_map/turn/pallas_call | solution.py:94
  33.5 2.4 %copy-done.2 = bf16[2560,1024]{1,0:T(8,128)(2,1)} copy-done((bf16[2560,1024]{1,0:T(8,128)(2,1)}, bf16[2560,1024]{1,0:T(8,128)(2,1)S(1)}, u32[]{:S(2)}) %copy-start.2) | copy-done | bytes 5242904
  35.9 2.6 %copy-done.1 = bf16[512,5376]{1,0:T(8,128)(2,1)S(1)} copy-done((bf16[512,5376]{1,0:T(8,128)(2,1)S(1)}, bf16[512,5376]{1,0:T(8,128)(2,1)}, u32[]{:S(2)}) %copy-start.1) | copy-done | bytes 5505048
  38.4 9.2 %dequantize.1.rest_5_.rest_2_ = bf16[1024,5376]{1,0:T(8,128)(2,1)S(1)} custom-call(bf16[512,5376]{1,0:T(8,128)(2,1)S(1)} %copy-done.1, bf16[512,5376]{1,0:T(8,128)(2,1)} %collective-permute-done.3.other_ref, f32[512,42]{1,0:T(8,128)S(1)} %copy.22.own_scale_ref, f32[512,42]{1,0:T(8,128)S(1)} %copy-done.5), custom_call_target="tpu_custom_call" | custom-call | flops 5505024 | bytes 22020096 | tf_op jit(solution)/shard_map/dequantize/pallas_call | solution.py:62
  47.9 3.8 %collective-permute-done.8.rest_4_ = bf16[32,7936]{1,0:T(8,128)(2,1)} collective-permute-done((bf16[32,7936]{1,0:T(8,128)(2,1)S(1)}, bf16[32,7936]{1,0:T(8,128)(2,1)}, u32[]{:S(2)}, u32[]{:S(2)}) %collective-permute-start.8) | collective-permute-done | bytes 507936 | tf_op jit(solution)/shard_map/ppermute | solution.py:20
  51.6 9.8 %logits.2 = (f32[1024,256]{1,0:T(8,128)S(1)}, f32[1024,256]{1,0:T(8,128)S(1)}, f32[8,256]{1,0:T(8,128)S(1)}, bf16[256,2560]{1,0:T(8,128)(2,1)S(1)}) custom-call(s32[2]{0:T(128)S(1)} %pad_add_fusion.place_ref.y_ref, bf16[128,7936]{1,0:T(8,128)(2,1)} %constant_dynamic-update-slice_fusion.rest_0_, bf16[32,7936]{1,0:T(8,128)(2,1)S(1)} %collective-permute-done.rest_1_, ...), custom_call_target="tpu_custom_call" | custom-call | flops 4160749568 | bytes 22413312 | tf_op jit(solution)/shard_map/logits/pallas_call | solution.py:243
  64.5 1.6 collective-permute-done.2.rest_1_
  66.2 10.6 %logits.3 = (f32[1024,256]{1,0:T(8,128)S(1)}, f32[1024,256]{1,0:T(8,128)S(1)}, f32[8,256]{1,0:T(8,128)}, bf16[256,2560]{1,0:T(8,128)(2,1)S(1)}, f32[16,8,512]{2,1,0:T(8,128)S(1)}) custom-call(s32[2]{0:T(128)S(1)} %pad_add_fusion.place_ref.y_ref, bf16[128,7936]{1,0:T(8,128)(2,1)} %collective-permute-done.1.rest_0_, ...), custom_call_target="tpu_custom_call" | custom-call | flops 4160749568 | bytes 22413312 | tf_op jit(solution)/shard_map/logits/pallas_call | solution.py:243
  79.8 13.6 %all_to_all.20 = f32[16,8,512]{2,1,0:T(8,128)S(1)} all-to-all(f32[16,8,512]{2,1,0:T(8,128)S(1)} %get-tuple-element.34), channel_id=1, replica_groups=mesh['x'=4,'z'=8,'y'=4,'c'=2] {'x','y'}, dimensions={0} | all-to-all | bytes 524288 | tf_op jit(solution)/shard_map/all_to_all | solution.py:410
  94.2 8.5 %all-to-all-start.1 = ((f32[8,5,512]{2,1,0:T(8,128)}), f32[8,5,512]{2,1,0:T(8,128)S(1)}, u32[]{:S(2)}, u32[]{:S(2)}) async-start(f32[8,5,512]{2,1,0:T(8,128)} %broadcast_in_dim.20), calls=%async_computation.1 | async-start | bytes 262144 | tf_op jit(solution)/shard_map/all_to_all | solution.py:323
  102.7 9.1 %all-to-all-done.1 = f32[8,5,512]{2,1,0:T(8,128)S(1)} async-done(((f32[8,5,512]{2,1,0:T(8,128)}), f32[8,5,512]{2,1,0:T(8,128)S(1)}, u32[]{:S(2)}, u32[]{:S(2)}) %all-to-all-start.1) | async-done | bytes 81952 | tf_op jit(solution)/shard_map/all_to_all | solution.py:323
  112.0 2.5 %copy-done.3 = bf16[2560,1024]{1,0:T(8,128)(2,1)S(1)} copy-done((bf16[2560,1024]{1,0:T(8,128)(2,1)S(1)}, bf16[2560,1024]{1,0:T(8,128)(2,1)}, u32[]{:S(2)}) %copy-start.3) | copy-done | bytes 5242904
  117.0 1.2 copy-done.15
  119.4 5.6 %gradients.1 = (bf16[512,512]{1,0:T(8,128)(2,1)S(1)}, bf16[512,512]{1,0:T(8,128)(2,1)S(1)}, bf16[4,4,640,128]{3,2,1,0:T(8,128)(2,1)}) custom-call(s32[2]{0:T(128)S(1)} %pad_add_fusion.place_ref.y_ref, f32[8,512]{1,0:T(8,128)S(1)} %pad_maximum_fusion.1.rows_ref, f32[1024,256]{1,0:T(8,128)S(1)} %copy-done.11, f32[1024,256]{1,0:T(8,128)S(1)} %copy-done.13, ...), custom_call_target="tpu_custom_call" | custom-call | flops 2684354560 | bytes 13107200 | tf_op jit(solution)/shard_map/gradients/pallas_call | solution.py:295
  125.8 6.1 %all-to-all-start.2 = ((bf16[16,640,128]{2,1,0:T(8,128)(2,1)}), bf16[16,640,128]{2,1,0:T(8,128)(2,1)}, u32[]{:S(2)}, u32[]{:S(2)}) async-start(bf16[16,640,128]{2,1,0:T(8,128)(2,1)} %bitcast.19), calls=%async_computation.2 | async-start | bytes 5242880 | tf_op jit(solution)/shard_map/all_to_all | solution.py:435
  132.6 29.7 %all-to-all-done.2 = bf16[16,640,128]{2,1,0:T(8,128)(2,1)} async-done(((bf16[16,640,128]{2,1,0:T(8,128)(2,1)}), bf16[16,640,128]{2,1,0:T(8,128)(2,1)}, u32[]{:S(2)}, u32[]{:S(2)}) %all-to-all-start.2) | async-done | bytes 2621472 | tf_op jit(solution)/shard_map/all_to_all | solution.py:435
  162.4 2.8 %reduce_sum.94 = bf16[640,128]{1,0:T(8,128)(2,1)} reduce(bf16[16,640,128]{2,1,0:T(8,128)(2,1)} %all-to-all-done.2, bf16[]{:T(256)} %constant.25.clone.1), dimensions={0}, to_apply=%region_11.0 | reduce | flops 1228800 | bytes 2785282 | tf_op jit(solution)/shard_map/reduce_sum | solution.py:436
  165.1 3.4 %all-to-all-start.3 = ((bf16[8,80,128]{2,1,0:T(8,128)(2,1)}), bf16[8,80,128]{2,1,0:T(8,128)(2,1)S(1)}, u32[]{:S(2)}, u32[]{:S(2)}) async-start(bf16[8,80,128]{2,1,0:T(8,128)(2,1)} %bitcast.20), calls=%async_computation.3 | async-start | bytes 327680 | tf_op jit(solution)/shard_map/all_to_all | solution.py:437
  170.1 6.7 %weight_gradient.1 = bf16[512,2560]{1,0:T(8,128)(2,1)} custom-call(bf16[512,512]{1,0:T(8,128)(2,1)S(1)} %copy-done.19, bf16[512,512]{1,0:T(8,128)(2,1)} %collective-permute-done.9.from_ref, bf16[256,2560]{1,0:T(8,128)(2,1)S(1)} %copy-done.7, bf16[256,2560]{1,0:T(8,128)(2,1)S(1)} %copy-done.9, bf16[256,2560]{1,0:T(8,128)(2,1)} %collective-permute-done.10.s0_p_ref, ...), custom_call_target="tpu_custom_call" | custom-call | flops 2684354560 | bytes 8912896 | tf_op jit(solution)/shard_map/weight_gradient/pallas_call | solution.py:355
  (89 shorter events, 23.3 us)
Async XLA Ops:
  0.6 22.6 %collective-permute-start.3 = (bf16[512,5376]{1,0:T(8,128)(2,1)}, bf16[512,5376]{1,0:T(8,128)(2,1)}, u32[]{:S(2)}, u32[]{:S(2)}) collective-permute-start(bf16[512,5376]{1,0:T(8,128)(2,1)} %own_ref.2), channel_id=1, source_target_pairs={{1,0},{0,1},{3,2},{2,3},{5,4},{4,5},{7,6},{6,7},{9,8},{8,9},{11,10... | collective-permute-start | bytes 16515080 | tf_op jit(solution)/shard_map/ppermute | solution.py:20
  0.7 22.5 %collective-permute-start.4 = (bf16[512,2560]{1,0:T(8,128)(2,1)}, bf16[512,2560]{1,0:T(8,128)(2,1)}, u32[]{:S(2)}, u32[]{:S(2)}) collective-permute-start(bf16[512,2560]{1,0:T(8,128)(2,1)} %rest_3_.1), channel_id=1, source_target_pairs={{1,0},{0,1},{3,2},{2,3},{5,4},{4,5},{7,6},{6,7},{9,8},{8,9},{11,10... | collective-permute-start | bytes 7864328 | tf_op jit(solution)/shard_map/ppermute | solution.py:20
  1.2 4.5 %copy-start.20 = (bf16[128,5376]{1,0:T(8,128)(2,1)S(1)}, bf16[128,5376]{1,0:T(8,128)(2,1)}, u32[]{:S(2)}) copy-start(bf16[128,5376]{1,0:T(8,128)(2,1)} %param.6) | copy-start | bytes 4128772
  3.3 3.6 %copy-start.21 = (bf16[128,2560]{1,0:T(8,128)(2,1)S(1)}, bf16[128,2560]{1,0:T(8,128)(2,1)}, u32[]{:S(2)}) copy-start(bf16[128,2560]{1,0:T(8,128)(2,1)} %param.7) | copy-start | bytes 1966084
  3.3 17.4 %copy-start.22 = (f32[512,42]{0,1:T(8,128)S(1)}, f32[512,42]{0,1:T(8,128)}, u32[]{:S(2)}) copy-start(f32[512,42]{0,1:T(8,128)} %param.9) | copy-start | bytes 258052
  3.3 24.2 %copy-start.23 = (bf16[128]{0:T(256)(128)(2,1)S(1)}, bf16[128]{0:T(256)(128)(2,1)}, u32[]{:S(2)}) copy-start(bf16[128]{0:T(256)(128)(2,1)} %param.11) | copy-start | bytes 772
  3.4 24.2 %copy-start = (bf16[512,2560]{1,0:T(8,128)(2,1)S(1)}, bf16[512,2560]{1,0:T(8,128)(2,1)}, u32[]{:S(2)}) copy-start(bf16[512,2560]{1,0:T(8,128)(2,1)} %rest_3_.1) | copy-start | bytes 7864324
  3.4 15.2 %collective-permute-start = (bf16[32,7936]{1,0:T(8,128)(2,1)S(1)}, bf16[32,7936]{1,0:T(8,128)(2,1)S(1)}, u32[]{:S(2)}, u32[]{:S(2)}) collective-permute-start(bf16[32,7936]{1,0:T(8,128)(2,1)S(1)} %pad_maximum_fusion), channel_id=1, source_target_pairs={{4,0},{6,2},{0,4},{2,6},{5,1},{7,3},{1,5},{3,7},{12,8},{14,10},{8,... | collective-permute-start | bytes 1523720 | tf_op jit(solution)/shard_map/ppermute | solution.py:20
  18.5 46.0 %collective-permute-start.1 = (bf16[128,7936]{1,0:T(8,128)(2,1)}, bf16[128,7936]{1,0:T(8,128)(2,1)}, u32[]{:S(2)}, u32[]{:S(2)}) collective-permute-start(bf16[128,7936]{1,0:T(8,128)(2,1)} %constant_dynamic-update-slice_fusion.rest_0_), channel_id=1, source_target_pairs={{2,0},{4,2},{6,4},{0,6},{3,1},{5,3},{7,5},{1,7},{10,8},{12,10},{14... | collective-permute-start | bytes 6094856 | tf_op jit(solution)/shard_map/ppermute | solution.py:20
  20.7 45.4 %collective-permute-start.2 = (bf16[128,7936]{1,0:T(8,128)(2,1)}, bf16[128,7936]{1,0:T(8,128)(2,1)}, u32[]{:S(2)}, u32[]{:S(2)}) collective-permute-start(bf16[128,7936]{1,0:T(8,128)(2,1)} %constant_dynamic-update-slice_fusion.rest_0_), channel_id=1, source_target_pairs={{6,0},{0,2},{2,4},{4,6},{7,1},{1,3},{3,5},{5,7},{14,8},{8,10},{10,... | collective-permute-start | bytes 6094856 | tf_op jit(solution)/shard_map/ppermute | solution.py:20
  20.9 1.6 collective-permute-start.5
  23.2 24.6 %collective-permute-start.6 = (bf16[32,7936]{1,0:T(8,128)(2,1)S(1)}, bf16[32,7936]{1,0:T(8,128)(2,1)}, u32[]{:S(2)}, u32[]{:S(2)}) collective-permute-start(bf16[32,7936]{1,0:T(8,128)(2,1)S(1)} %collective-permute-done.rest_1_), channel_id=1, source_target_pairs={{64,0},{128,64},{192,128},{0,192},{65,1},{129,65},{193,129},{1,193... | collective-permute-start | bytes 1523720 | tf_op jit(solution)/shard_map/ppermute | solution.py:20
  25.8 22.1 %collective-permute-start.7 = (bf16[32,7936]{1,0:T(8,128)(2,1)S(1)}, bf16[32,7936]{1,0:T(8,128)(2,1)}, u32[]{:S(2)}, u32[]{:S(2)}) collective-permute-start(bf16[32,7936]{1,0:T(8,128)(2,1)S(1)} %collective-permute-done.rest_1_), channel_id=1, source_target_pairs={{128,0},{192,64},{0,128},{64,192},{129,1},{193,65},{1,129},{65,193... | collective-permute-start | bytes 1523720 | tf_op jit(solution)/shard_map/ppermute | solution.py:20
  26.6 25.0 %collective-permute-start.8 = (bf16[32,7936]{1,0:T(8,128)(2,1)S(1)}, bf16[32,7936]{1,0:T(8,128)(2,1)}, u32[]{:S(2)}, u32[]{:S(2)}) collective-permute-start(bf16[32,7936]{1,0:T(8,128)(2,1)S(1)} %collective-permute-done.rest_1_), channel_id=1, source_target_pairs={{192,0},{0,64},{64,128},{128,192},{193,1},{1,65},{65,129},{129,193... | collective-permute-start | bytes 1523720 | tf_op jit(solution)/shard_map/ppermute | solution.py:20
  27.6 8.3 %copy-start.5 = (f32[512,42]{1,0:T(8,128)S(1)}, f32[512,42]{1,0:T(8,128)}, u32[]{:S(2)}) copy-start(f32[512,42]{1,0:T(8,128)} %copy-done.4) | copy-start | bytes 258052
  35.8 2.6 %copy-start.1 = (bf16[512,5376]{1,0:T(8,128)(2,1)S(1)}, bf16[512,5376]{1,0:T(8,128)(2,1)}, u32[]{:S(2)}) copy-start(bf16[512,5376]{1,0:T(8,128)(2,1)} %own_ref.2) | copy-start | bytes 16515076
  94.2 17.5 %all-to-all-start.1 = ((f32[8,5,512]{2,1,0:T(8,128)}), f32[8,5,512]{2,1,0:T(8,128)S(1)}, u32[]{:S(2)}, u32[]{:S(2)}) async-start(f32[8,5,512]{2,1,0:T(8,128)} %broadcast_in_dim.20), calls=%async_computation.1 | async-start | bytes 262144 | tf_op jit(solution)/shard_map/all_to_all | solution.py:323
  125.8 6.1 %copy-start.9 = (bf16[256,2560]{1,0:T(8,128)(2,1)S(1)}, bf16[256,2560]{1,0:T(8,128)(2,1)}, u32[]{:S(2)}) copy-start(bf16[256,2560]{1,0:T(8,128)(2,1)} %copy-done.8) | copy-start | bytes 3932164
  125.8 6.2 %copy-start.7 = (bf16[256,2560]{1,0:T(8,128)(2,1)S(1)}, bf16[256,2560]{1,0:T(8,128)(2,1)}, u32[]{:S(2)}) copy-start(bf16[256,2560]{1,0:T(8,128)(2,1)} %copy-done.6) | copy-start | bytes 3932164
  125.8 36.5 %all-to-all-start.2 = ((bf16[16,640,128]{2,1,0:T(8,128)(2,1)}), bf16[16,640,128]{2,1,0:T(8,128)(2,1)}, u32[]{:S(2)}, u32[]{:S(2)}) async-start(bf16[16,640,128]{2,1,0:T(8,128)(2,1)} %bitcast.19), calls=%async_computation.2 | async-start | bytes 5242880 | tf_op jit(solution)/shard_map/all_to_all | solution.py:435
  131.9 37.2 %collective-permute-start.11 = (bf16[256,2560]{1,0:T(8,128)(2,1)S(1)}, bf16[256,2560]{1,0:T(8,128)(2,1)}, u32[]{:S(2)}, u32[]{:S(2)}) collective-permute-start(bf16[256,2560]{1,0:T(8,128)(2,1)S(1)} %copy-done.9), channel_id=1, source_target_pairs={{1,0},{0,1},{3,2},{2,3},{5,4},{4,5},{7,6},{6,7},{9,8},{8,9},{11,10... | collective-permute-start | bytes 3932168 | tf_op jit(solution)/shard_map/ppermute | solution.py:20
  132.0 37.0 %collective-permute-start.10 = (bf16[256,2560]{1,0:T(8,128)(2,1)S(1)}, bf16[256,2560]{1,0:T(8,128)(2,1)}, u32[]{:S(2)}, u32[]{:S(2)}) collective-permute-start(bf16[256,2560]{1,0:T(8,128)(2,1)S(1)} %copy-done.7), channel_id=1, source_target_pairs={{1,0},{0,1},{3,2},{2,3},{5,4},{4,5},{7,6},{6,7},{9,8},{8,9},{11,10... | collective-permute-start | bytes 3932168 | tf_op jit(solution)/shard_map/ppermute | solution.py:20
  132.5 36.6 %collective-permute-start.9 = (bf16[512,512]{1,0:T(8,128)(2,1)S(1)}, bf16[512,512]{1,0:T(8,128)(2,1)}, u32[]{:S(2)}, u32[]{:S(2)}) collective-permute-start(bf16[512,512]{1,0:T(8,128)(2,1)S(1)} %get-tuple-element.42), channel_id=1, source_target_pairs={{1,0},{0,1},{3,2},{2,3},{5,4},{4,5},{7,6},{6,7},{9,8},{8,9},{11,10... | collective-permute-start | bytes 1572872 | tf_op jit(solution)/shard_map/ppermute | solution.py:20
  165.1 12.7 %all-to-all-start.3 = ((bf16[8,80,128]{2,1,0:T(8,128)(2,1)}), bf16[8,80,128]{2,1,0:T(8,128)(2,1)S(1)}, u32[]{:S(2)}, u32[]{:S(2)}) async-start(bf16[8,80,128]{2,1,0:T(8,128)(2,1)} %bitcast.20), calls=%async_computation.3 | async-start | bytes 327680 | tf_op jit(solution)/shard_map/all_to_all | solution.py:437
  (15 other events, 18.4 us)

commit v6 on v5

--- a/solution.py
+++ b/solution.py
@@ -99,7 +99,7 @@
             pl.BlockSpec((DEQUANT_ROWS, width), lambda i: two_sources(i, steps)[1]),
         ],
         out_specs=pl.BlockSpec((width, DEQUANT_ROWS), lambda i: (0, i)),
-        out_shape=jax.ShapeDtypeStruct((width, 2 * rows), BF16),
+        out_shape=pltpu.HBM((width, 2 * rows), BF16),
         compiler_params=pltpu.CompilerParams(vmem_limit_bytes=8 * MIB),
         cost_estimate=pl.CostEstimate(
             flops=0, transcendentals=0, bytes_accessed=8 * rows * width
@@ -210,7 +210,7 @@
     tok = pieces[0].shape[0]
     tokens = 2 * tok
     steps = rows // LOGIT_ROWS
-    tile = jax.ShapeDtypeStruct((2 * rows, tokens), F32)
+    tile = pltpu.HBM((2 * rows, tokens), F32)
 
     def source(width, k):
         return pl.BlockSpec((LOGIT_ROWS, width), lambda i, y: two_sources(i, steps)[k])
@@ -231,7 +231,7 @@
         tile,
         tile,
         jax.ShapeDtypeStruct((8, tokens), F32),
-        jax.ShapeDtypeStruct((tokens, width_s), BF16),
+        pltpu.HBM((tokens, width_s), BF16),
     ]
     operands = [place, *pieces, table, weight, weight_p]
     if first_stats is not None:
@@ -288,7 +288,7 @@
     (t0, s0), (t1, s1) = logits
     vocab, tokens = t0.shape
     width = turned.shape[0]
-    lg = jax.ShapeDtypeStruct((vocab // 2, 2 * tokens), BF16)
+    lg = pltpu.HBM((vocab // 2, 2 * tokens), BF16)
     whole = pl.BlockSpec((vocab, tokens), lambda i, y: (0, 0))
     lg_spec = pl.BlockSpec((vocab // 2, 2 * tokens), lambda i, y: (0, 0))
     cut = (width // n_x, 2 * tokens // n_y)
@@ -307,8 +307,8 @@
             ],
             out_specs=[lg_spec, lg_spec, pl.BlockSpec((1, n_y, *cut), lambda i, y: (i, 0, 0, 0))],
         ),
-        out_shape=[lg, lg, jax.ShapeDtypeStruct((n_x, n_y, *cut), BF16)],
-        compiler_params=pltpu.CompilerParams(vmem_limit_bytes=22 * MIB),
+        out_shape=[lg, lg, pltpu.HBM((n_x, n_y, *cut), BF16)],
+        compiler_params=pltpu.CompilerParams(vmem_limit_bytes=56 * MIB),
         cost_estimate=pl.CostEstimate(
             flops=4 * vocab * tokens * width,
             transcendentals=4 * vocab * tokens,
@@ -358,7 +358,7 @@
         in_specs=[whole, whole] + [pl.BlockSpec((half, WEIGHT_COLUMNS), lambda i: (0, i))] * 4,
         out_specs=pl.BlockSpec((rows, WEIGHT_COLUMNS), lambda i: (0, i)),
         out_shape=jax.ShapeDtypeStruct((rows, width), BF16),
-        compiler_params=pltpu.CompilerParams(vmem_limit_bytes=14 * MIB),
+        compiler_params=pltpu.CompilerParams(vmem_limit_bytes=56 * MIB),
         cost_estimate=pl.CostEstimate(
             flops=4 * rows * tokens * width,
             transcendentals=0,

time: 181 us -> 172 us (0.950)
  local copies, waits for them, and re-layouts: 26.4 us -> 8.78 us
  Pallas kernels: 47.8 us -> 55.5 us
  waiting for transfers between devices: 57.8 us -> 60.8 us
    unnamed x50 -> x22, local copies, waits for them, and re-layouts: 22.2 us -> 4.6 us
    pallas_call x1, Pallas kernels: 5.58 us -> 9.22 us  [gradients(): pl.pallas_call(grad_kernel, grid_spec=pltpu.PrefetchScalarGridSpec(num_sc...]
    ppermute x12, waiting for transfers between devices: 17.9 us -> 20.6 us  [shift(): return lax.ppermute(a, axis, [((i + by) % n, i) for i in range(n)])]
    pallas_call x2, Pallas kernels: 20.4 us -> 22.4 us  [logits_of(): pl.pallas_call(functools.partial(logits_kernel, steps, len(pieces)), grid...]
  transfers between devices with their start and end apart: 15 -> 15, of which waited for: 8 -> 9; matrix products, arithmetic and copies ran while one was open for 4% -> 3% of each run, Pallas kernels for 18% -> 21%
where the time goes in v6:
time: 172 us; the launch traced here: 170 us
  waiting for transfers between devices  60.8 us (35%)
  Pallas kernels  55.5 us (32%)
  starting transfers between devices  27.3 us (16%)
  blocking collectives  13.6 us (8%)
  local copies, waits for them, and re-layouts  8.78 us (5%)
  other arithmetic  2.79 us (2%)
    all_to_all x1, waiting for transfers between devices, local(): got = lax.all_to_all(blocks, ('x', 'y'), 0, 0, tiled=True)  29.7 us
    pallas_call x2, Pallas kernels, logits_of(): pl.pallas_call(functools.partial(logits_kernel, steps, len(pieces)), grid...  22.4 us
    ppermute x12, waiting for transfers between devices, shift(): return lax.ppermute(a, axis, [((i + by) % n, i) for i in range(n)])  20.6 us
    all_to_all x1, blocking collectives, local(): seen = lax.all_to_all(mine, ('x', 'y'), 0, 0, tiled=True)  13.6 us
    ppermute x12, starting transfers between devices, shift(): return lax.ppermute(a, axis, [((i + by) % n, i) for i in range(n)])  10.1 us
    pallas_call x1, Pallas kernels, dequantize(): pl.pallas_call(functools.partial(dequant_kernel, steps), grid=(2 * steps,...  9.24 us
    pallas_call x1, Pallas kernels, gradients(): pl.pallas_call(grad_kernel, grid_spec=pltpu.PrefetchScalarGridSpec(num_sc...  9.22 us
    all_to_all x1, waiting for transfers between devices, to_all(): lax.all_to_all(jnp.broadcast_to(a[None], (n, *a.shape)), axes, 0, 0, tile...  9.05 us
  transfers between devices with their start and end apart: 15, of which 9 were waited for; matrix products, arithmetic and copies ran while one was open for 3% of the time, Pallas kernels for 21%

profile of v6, /device:TPU:8, one launch (start us, length us, event | category | flops | bytes accessed | tf_op | source)
XLA Modules:
  0.0 169.6 jit_solution(17152930646905989134)
XLA Ops:
  3.4 2.4 %collective-permute-start = (bf16[32,7936]{1,0:T(8,128)(2,1)S(1)}, bf16[32,7936]{1,0:T(8,128)(2,1)S(1)}, u32[]{:S(2)}, u32[]{:S(2)}) collective-permute-start(bf16[32,7936]{1,0:T(8,128)(2,1)S(1)} %pad_maximum_fusion), channel_id=1, source_target_pairs={{4,0},{6,2},{0,4},{2,6},{5,1},{7,3},{1,5},{3,7},{12,8},{14,10},{8,... | collective-permute-start | bytes 1523720 | tf_op jit(solution)/shard_map/ppermute | solution.py:20
  5.8 1.2 constant_dynamic-update-slice_fusion.1
  7.8 10.7 %collective-permute-done.rest_1_ = bf16[32,7936]{1,0:T(8,128)(2,1)S(1)} collective-permute-done((bf16[32,7936]{1,0:T(8,128)(2,1)S(1)}, bf16[32,7936]{1,0:T(8,128)(2,1)S(1)}, u32[]{:S(2)}, u32[]{:S(2)}) %collective-permute-start) | collective-permute-done | bytes 507936 | tf_op jit(solution)/shard_map/ppermute | solution.py:20
  18.5 2.2 %collective-permute-start.1 = (bf16[128,7936]{1,0:T(8,128)(2,1)}, bf16[128,7936]{1,0:T(8,128)(2,1)}, u32[]{:S(2)}, u32[]{:S(2)}) collective-permute-start(bf16[128,7936]{1,0:T(8,128)(2,1)} %constant_dynamic-update-slice_fusion.rest_0_), channel_id=1, source_target_pairs={{2,0},{4,2},{6,4},{0,6},{3,1},{5,3},{7,5},{1,7},{10,8},{12,10},{14... | collective-permute-start | bytes 6094856 | tf_op jit(solution)/shard_map/ppermute | solution.py:20
  21.0 1.5 collective-permute-done.5.other_scale_ref
  23.2 2.6 %collective-permute-start.6 = (bf16[32,7936]{1,0:T(8,128)(2,1)S(1)}, bf16[32,7936]{1,0:T(8,128)(2,1)}, u32[]{:S(2)}, u32[]{:S(2)}) collective-permute-start(bf16[32,7936]{1,0:T(8,128)(2,1)S(1)} %collective-permute-done.rest_1_), channel_id=1, source_target_pairs={{64,0},{128,64},{192,128},{0,192},{65,1},{129,65},{193,129},{1,193... | collective-permute-start | bytes 1523720 | tf_op jit(solution)/shard_map/ppermute | solution.py:20
  27.6 7.3 %turn.1.turned_ref = bf16[2560,1024]{1,0:T(8,128)(2,1)} custom-call(bf16[512,2560]{1,0:T(8,128)(2,1)S(1)} %copy-done, bf16[512,2560]{1,0:T(8,128)(2,1)} %collective-permute-done.4.rest_7_.other_ref.rest_4_), custom_call_target="tpu_custom_call" | custom-call | bytes 10485760 | tf_op jit(solution)/shard_map/turn/pallas_call | solution.py:94
  34.9 2.6 %copy-done.1 = bf16[512,5376]{1,0:T(8,128)(2,1)S(1)} copy-done((bf16[512,5376]{1,0:T(8,128)(2,1)S(1)}, bf16[512,5376]{1,0:T(8,128)(2,1)}, u32[]{:S(2)}) %copy-start.1) | copy-done | bytes 5505048
  37.4 9.2 %dequantize.1.rest_5_.rest_2_ = bf16[1024,5376]{1,0:T(8,128)(2,1)S(1)} custom-call(bf16[512,5376]{1,0:T(8,128)(2,1)S(1)} %copy-done.1, bf16[512,5376]{1,0:T(8,128)(2,1)} %collective-permute-done.3.other_ref, f32[512,42]{1,0:T(8,128)S(1)} %copy.22.own_scale_ref, f32[512,42]{1,0:T(8,128)S(1)} %copy-done.3), custom_call_target="tpu_custom_call" | custom-call | flops 5505024 | bytes 22020096 | tf_op jit(solution)/shard_map/dequantize/pallas_call | solution.py:62
  46.7 1.2 collective-permute-done.6.rest_2_
  47.9 3.8 %collective-permute-done.8.rest_4_ = bf16[32,7936]{1,0:T(8,128)(2,1)} collective-permute-done((bf16[32,7936]{1,0:T(8,128)(2,1)S(1)}, bf16[32,7936]{1,0:T(8,128)(2,1)}, u32[]{:S(2)}, u32[]{:S(2)}) %collective-permute-start.8) | collective-permute-done | bytes 507936 | tf_op jit(solution)/shard_map/ppermute | solution.py:20
  51.6 11.1 %logits.2 = (f32[1024,256]{1,0:T(8,128)}, f32[1024,256]{1,0:T(8,128)}, f32[8,256]{1,0:T(8,128)S(1)}, bf16[256,2560]{1,0:T(8,128)(2,1)}) custom-call(s32[2]{0:T(128)S(1)} %pad_add_fusion.place_ref.y_ref, bf16[128,7936]{1,0:T(8,128)(2,1)} %constant_dynamic-update-slice_fusion.rest_0_, bf16[32,7936]{1,0:T(8,128)(2,1)S(1)} %collective-permute-done.rest_1_, ...), custom_call_target="tpu_custom_call" | custom-call | flops 4160749568 | bytes 22413312 | tf_op jit(solution)/shard_map/logits/pallas_call | solution.py:243
  62.8 1.5 collective-permute-done.1.rest_0_
  64.3 1.9 %collective-permute-done.2.rest_1_ = bf16[128,7936]{1,0:T(8,128)(2,1)} collective-permute-done((bf16[128,7936]{1,0:T(8,128)(2,1)}, bf16[128,7936]{1,0:T(8,128)(2,1)}, u32[]{:S(2)}, u32[]{:S(2)}) %collective-permute-start.2) | collective-permute-done | bytes 2031648 | tf_op jit(solution)/shard_map/ppermute | solution.py:20
  66.2 11.3 %logits.3 = (f32[1024,256]{1,0:T(8,128)}, f32[1024,256]{1,0:T(8,128)}, f32[8,256]{1,0:T(8,128)}, bf16[256,2560]{1,0:T(8,128)(2,1)}, f32[16,8,512]{2,1,0:T(8,128)S(1)}) custom-call(s32[2]{0:T(128)S(1)} %pad_add_fusion.place_ref.y_ref, bf16[128,7936]{1,0:T(8,128)(2,1)} %collective-permute-done.1.rest_0_, bf16[128,7936]{1,0:T(8,128)(2,1)} %collective-permute-done.2.rest_1_, ...), custom_call_target="tpu_custom_call" | custom-call | flops 4160749568 | bytes 22413312 | tf_op jit(solution)/shard_map/logits/pallas_call | solution.py:243
  77.5 13.6 %all_to_all.20 = f32[16,8,512]{2,1,0:T(8,128)S(1)} all-to-all(f32[16,8,512]{2,1,0:T(8,128)S(1)} %get-tuple-element.34), channel_id=1, replica_groups=mesh['x'=4,'z'=8,'y'=4,'c'=2] {'x','y'}, dimensions={0} | all-to-all | bytes 524288 | tf_op jit(solution)/shard_map/all_to_all | solution.py:410
  91.9 8.5 %all-to-all-start.1 = ((f32[8,5,512]{2,1,0:T(8,128)}), f32[8,5,512]{2,1,0:T(8,128)S(1)}, u32[]{:S(2)}, u32[]{:S(2)}) async-start(f32[8,5,512]{2,1,0:T(8,128)} %broadcast_in_dim.20), calls=%async_computation.1 | async-start | bytes 262144 | tf_op jit(solution)/shard_map/all_to_all | solution.py:323
  100.4 9.1 %all-to-all-done.1 = f32[8,5,512]{2,1,0:T(8,128)S(1)} async-done(((f32[8,5,512]{2,1,0:T(8,128)}), f32[8,5,512]{2,1,0:T(8,128)S(1)}, u32[]{:S(2)}, u32[]{:S(2)}) %all-to-all-start.1) | async-done | bytes 81952 | tf_op jit(solution)/shard_map/all_to_all | solution.py:323
  110.4 9.2 %gradients.1 = (bf16[512,512]{1,0:T(8,128)(2,1)}, bf16[512,512]{1,0:T(8,128)(2,1)}, bf16[4,4,640,128]{3,2,1,0:T(8,128)(2,1)}) custom-call(s32[2]{0:T(128)} %copy-done.4, f32[8,512]{1,0:T(8,128)} %pad_maximum_fusion.1.rows_ref, f32[1024,256]{1,0:T(8,128)} %get-tuple-element.35.t0, f32[1024,256]{1,0:T(8,128)} %get-tuple-element.36.s0, ...), custom_call_target="tpu_custom_call" | custom-call | flops 2684354560 | bytes 13107200 | tf_op jit(solution)/shard_map/gradients/pallas_call | solution.py:295
  119.6 5.3 %all-to-all-start.2 = ((bf16[16,640,128]{2,1,0:T(8,128)(2,1)}), bf16[16,640,128]{2,1,0:T(8,128)(2,1)S(1)}, u32[]{:S(2)}, u32[]{:S(2)}) async-start(bf16[16,640,128]{2,1,0:T(8,128)(2,1)} %bitcast.83), calls=%async_computation.2 | async-start | bytes 5242880 | tf_op jit(solution)/shard_map/all_to_all | solution.py:435
  125.5 29.7 %all-to-all-done.2 = bf16[16,640,128]{2,1,0:T(8,128)(2,1)S(1)} async-done(((bf16[16,640,128]{2,1,0:T(8,128)(2,1)}), bf16[16,640,128]{2,1,0:T(8,128)(2,1)S(1)}, u32[]{:S(2)}, u32[]{:S(2)}) %all-to-all-start.2) | async-done | bytes 2621472 | tf_op jit(solution)/shard_map/all_to_all | solution.py:435
  156.2 3.4 %all-to-all-start.3 = ((bf16[8,80,128]{2,1,0:T(8,128)(2,1)}), bf16[8,80,128]{2,1,0:T(8,128)(2,1)S(1)}, u32[]{:S(2)}, u32[]{:S(2)}) async-start(bf16[8,80,128]{2,1,0:T(8,128)(2,1)} %bitcast.20), calls=%async_computation.3 | async-start | bytes 327680 | tf_op jit(solution)/shard_map/all_to_all | solution.py:437
  160.2 7.4 %weight_gradient.1 = bf16[512,2560]{1,0:T(8,128)(2,1)} custom-call(bf16[512,512]{1,0:T(8,128)(2,1)} %get-tuple-element.41.own_ref, bf16[512,512]{1,0:T(8,128)(2,1)} %collective-permute-done.9.from_ref, bf16[256,2560]{1,0:T(8,128)(2,1)} %get-tuple-element.43.s0_ref, bf16[256,2560]{1,0:T(8,128)(2,1)} %get-tuple-element.44.s1_ref, ...), custom_call_target="tpu_custom_call" | custom-call | flops 2684354560 | bytes 8912896 | tf_op jit(solution)/shard_map/weight_gradient/pallas_call | solution.py:355
  167.5 1.5 all-to-all-done.3
  (61 shorter events, 10.8 us)
Async XLA Ops:
  0.6 22.6 %collective-permute-start.3 = (bf16[512,5376]{1,0:T(8,128)(2,1)}, bf16[512,5376]{1,0:T(8,128)(2,1)}, u32[]{:S(2)}, u32[]{:S(2)}) collective-permute-start(bf16[512,5376]{1,0:T(8,128)(2,1)} %own_ref.2), channel_id=1, source_target_pairs={{1,0},{0,1},{3,2},{2,3},{5,4},{4,5},{7,6},{6,7},{9,8},{8,9},{11,10... | collective-permute-start | bytes 16515080 | tf_op jit(solution)/shard_map/ppermute | solution.py:20
  0.7 22.5 %collective-permute-start.4 = (bf16[512,2560]{1,0:T(8,128)(2,1)}, bf16[512,2560]{1,0:T(8,128)(2,1)}, u32[]{:S(2)}, u32[]{:S(2)}) collective-permute-start(bf16[512,2560]{1,0:T(8,128)(2,1)} %rest_3_.1), channel_id=1, source_target_pairs={{1,0},{0,1},{3,2},{2,3},{5,4},{4,5},{7,6},{6,7},{9,8},{8,9},{11,10... | collective-permute-start | bytes 7864328 | tf_op jit(solution)/shard_map/ppermute | solution.py:20
  1.2 4.5 %copy-start.5 = (bf16[128,5376]{1,0:T(8,128)(2,1)S(1)}, bf16[128,5376]{1,0:T(8,128)(2,1)}, u32[]{:S(2)}) copy-start(bf16[128,5376]{1,0:T(8,128)(2,1)} %param.6) | copy-start | bytes 4128772
  3.3 3.6 %copy-start.6 = (bf16[128,2560]{1,0:T(8,128)(2,1)S(1)}, bf16[128,2560]{1,0:T(8,128)(2,1)}, u32[]{:S(2)}) copy-start(bf16[128,2560]{1,0:T(8,128)(2,1)} %param.7) | copy-start | bytes 1966084
  3.3 17.4 %copy-start.7 = (f32[512,42]{0,1:T(8,128)S(1)}, f32[512,42]{0,1:T(8,128)}, u32[]{:S(2)}) copy-start(f32[512,42]{0,1:T(8,128)} %param.9) | copy-start | bytes 258052
  3.3 24.2 %copy-start.9 = (bf16[128]{0:T(256)(128)(2,1)S(1)}, bf16[128]{0:T(256)(128)(2,1)}, u32[]{:S(2)}) copy-start(bf16[128]{0:T(256)(128)(2,1)} %param.11) | copy-start | bytes 772
  3.4 24.2 %copy-start = (bf16[512,2560]{1,0:T(8,128)(2,1)S(1)}, bf16[512,2560]{1,0:T(8,128)(2,1)}, u32[]{:S(2)}) copy-start(bf16[512,2560]{1,0:T(8,128)(2,1)} %rest_3_.1) | copy-start | bytes 7864324
  3.4 15.2 %collective-permute-start = (bf16[32,7936]{1,0:T(8,128)(2,1)S(1)}, bf16[32,7936]{1,0:T(8,128)(2,1)S(1)}, u32[]{:S(2)}, u32[]{:S(2)}) collective-permute-start(bf16[32,7936]{1,0:T(8,128)(2,1)S(1)} %pad_maximum_fusion), channel_id=1, source_target_pairs={{4,0},{6,2},{0,4},{2,6},{5,1},{7,3},{1,5},{3,7},{12,8},{14,10},{8,... | collective-permute-start | bytes 1523720 | tf_op jit(solution)/shard_map/ppermute | solution.py:20
  18.5 45.7 %collective-permute-start.1 = (bf16[128,7936]{1,0:T(8,128)(2,1)}, bf16[128,7936]{1,0:T(8,128)(2,1)}, u32[]{:S(2)}, u32[]{:S(2)}) collective-permute-start(bf16[128,7936]{1,0:T(8,128)(2,1)} %constant_dynamic-update-slice_fusion.rest_0_), channel_id=1, source_target_pairs={{2,0},{4,2},{6,4},{0,6},{3,1},{5,3},{7,5},{1,7},{10,8},{12,10},{14... | collective-permute-start | bytes 6094856 | tf_op jit(solution)/shard_map/ppermute | solution.py:20
  20.7 45.4 %collective-permute-start.2 = (bf16[128,7936]{1,0:T(8,128)(2,1)}, bf16[128,7936]{1,0:T(8,128)(2,1)}, u32[]{:S(2)}, u32[]{:S(2)}) collective-permute-start(bf16[128,7936]{1,0:T(8,128)(2,1)} %constant_dynamic-update-slice_fusion.rest_0_), channel_id=1, source_target_pairs={{6,0},{0,2},{2,4},{4,6},{7,1},{1,3},{3,5},{5,7},{14,8},{8,10},{10,... | collective-permute-start | bytes 6094856 | tf_op jit(solution)/shard_map/ppermute | solution.py:20
  20.9 1.6 collective-permute-start.5
  23.2 24.6 %collective-permute-start.6 = (bf16[32,7936]{1,0:T(8,128)(2,1)S(1)}, bf16[32,7936]{1,0:T(8,128)(2,1)}, u32[]{:S(2)}, u32[]{:S(2)}) collective-permute-start(bf16[32,7936]{1,0:T(8,128)(2,1)S(1)} %collective-permute-done.rest_1_), channel_id=1, source_target_pairs={{64,0},{128,64},{192,128},{0,192},{65,1},{129,65},{193,129},{1,193... | collective-permute-start | bytes 1523720 | tf_op jit(solution)/shard_map/ppermute | solution.py:20
  25.8 22.1 %collective-permute-start.7 = (bf16[32,7936]{1,0:T(8,128)(2,1)S(1)}, bf16[32,7936]{1,0:T(8,128)(2,1)}, u32[]{:S(2)}, u32[]{:S(2)}) collective-permute-start(bf16[32,7936]{1,0:T(8,128)(2,1)S(1)} %collective-permute-done.rest_1_), channel_id=1, source_target_pairs={{128,0},{192,64},{0,128},{64,192},{129,1},{193,65},{1,129},{65,193... | collective-permute-start | bytes 1523720 | tf_op jit(solution)/shard_map/ppermute | solution.py:20
  26.6 25.0 %collective-permute-start.8 = (bf16[32,7936]{1,0:T(8,128)(2,1)S(1)}, bf16[32,7936]{1,0:T(8,128)(2,1)}, u32[]{:S(2)}, u32[]{:S(2)}) collective-permute-start(bf16[32,7936]{1,0:T(8,128)(2,1)S(1)} %collective-permute-done.rest_1_), channel_id=1, source_target_pairs={{192,0},{0,64},{64,128},{128,192},{193,1},{1,65},{65,129},{129,193... | collective-permute-start | bytes 1523720 | tf_op jit(solution)/shard_map/ppermute | solution.py:20
  27.6 38.6 %copy-start.4 = (s32[2]{0:T(128)}, s32[2]{0:T(128)S(1)}, u32[]{:S(2)}) copy-start(s32[2]{0:T(128)S(1)} %pad_add_fusion.place_ref.y_ref) | copy-start | bytes 28
  27.6 7.3 %copy-start.3 = (f32[512,42]{1,0:T(8,128)S(1)}, f32[512,42]{1,0:T(8,128)}, u32[]{:S(2)}) copy-start(f32[512,42]{1,0:T(8,128)} %copy-done.2) | copy-start | bytes 258052
  34.9 2.6 %copy-start.1 = (bf16[512,5376]{1,0:T(8,128)(2,1)S(1)}, bf16[512,5376]{1,0:T(8,128)(2,1)}, u32[]{:S(2)}) copy-start(bf16[512,5376]{1,0:T(8,128)(2,1)} %own_ref.2) | copy-start | bytes 16515076
  91.9 17.6 %all-to-all-start.1 = ((f32[8,5,512]{2,1,0:T(8,128)}), f32[8,5,512]{2,1,0:T(8,128)S(1)}, u32[]{:S(2)}, u32[]{:S(2)}) async-start(f32[8,5,512]{2,1,0:T(8,128)} %broadcast_in_dim.20), calls=%async_computation.1 | async-start | bytes 262144 | tf_op jit(solution)/shard_map/all_to_all | solution.py:323
  119.6 5.8 %copy-start.8 = (bf16[512,512]{1,0:T(8,128)(2,1)S(1)}, bf16[512,512]{1,0:T(8,128)(2,1)}, u32[]{:S(2)}) copy-start(bf16[512,512]{1,0:T(8,128)(2,1)} %get-tuple-element.42) | copy-start | bytes 1572868
  119.6 35.6 %all-to-all-start.2 = ((bf16[16,640,128]{2,1,0:T(8,128)(2,1)}), bf16[16,640,128]{2,1,0:T(8,128)(2,1)S(1)}, u32[]{:S(2)}, u32[]{:S(2)}) async-start(bf16[16,640,128]{2,1,0:T(8,128)(2,1)} %bitcast.83), calls=%async_computation.2 | async-start | bytes 5242880 | tf_op jit(solution)/shard_map/all_to_all | solution.py:435
  124.9 35.2 %collective-permute-start.11 = (bf16[256,2560]{1,0:T(8,128)(2,1)}, bf16[256,2560]{1,0:T(8,128)(2,1)}, u32[]{:S(2)}, u32[]{:S(2)}) collective-permute-start(bf16[256,2560]{1,0:T(8,128)(2,1)} %get-tuple-element.44.s1_ref), channel_id=1, source_target_pairs={{1,0},{0,1},{3,2},{2,3},{5,4},{4,5},{7,6},{6,7},{9,8},{8,9},{11,10... | collective-permute-start | bytes 3932168 | tf_op jit(solution)/shard_map/ppermute | solution.py:20
  124.9 35.2 %collective-permute-start.10 = (bf16[256,2560]{1,0:T(8,128)(2,1)}, bf16[256,2560]{1,0:T(8,128)(2,1)}, u32[]{:S(2)}, u32[]{:S(2)}) collective-permute-start(bf16[256,2560]{1,0:T(8,128)(2,1)} %get-tuple-element.43.s0_ref), channel_id=1, source_target_pairs={{1,0},{0,1},{3,2},{2,3},{5,4},{4,5},{7,6},{6,7},{9,8},{8,9},{11,10... | collective-permute-start | bytes 3932168 | tf_op jit(solution)/shard_map/ppermute | solution.py:20
  125.4 34.7 %collective-permute-start.9 = (bf16[512,512]{1,0:T(8,128)(2,1)S(1)}, bf16[512,512]{1,0:T(8,128)(2,1)}, u32[]{:S(2)}, u32[]{:S(2)}) collective-permute-start(bf16[512,512]{1,0:T(8,128)(2,1)S(1)} %copy-done.8), channel_id=1, source_target_pairs={{1,0},{0,1},{3,2},{2,3},{5,4},{4,5},{7,6},{6,7},{9,8},{8,9},{11,10... | collective-permute-start | bytes 1572872 | tf_op jit(solution)/shard_map/ppermute | solution.py:20
  156.2 12.7 %all-to-all-start.3 = ((bf16[8,80,128]{2,1,0:T(8,128)(2,1)}), bf16[8,80,128]{2,1,0:T(8,128)(2,1)S(1)}, u32[]{:S(2)}, u32[]{:S(2)}) async-start(bf16[8,80,128]{2,1,0:T(8,128)(2,1)} %bitcast.20), calls=%async_computation.3 | async-start | bytes 327680 | tf_op jit(solution)/shard_map/all_to_all | solution.py:437
  (1 other events, 0.7 us)

commit v7 on v6

--- a/solution.py
+++ b/solution.py
@@ -375,15 +375,21 @@
     width_s = student_hidden.shape[1]
     n_x, n_z, n_y = (lax.axis_size(a) for a in ("x", "z", "y"))
     x, y = lax.axis_index("x"), lax.axis_index("y")
-    part = tok // n_x
 
     place = jnp.stack([y, x]).astype(jnp.int32)
+    eighth = tok // (2 * n_x)
+    odd = lax.rem(lax.axis_index("z"), 2)
     piece = [
-        lax.dynamic_slice_in_dim(a, x * part, part, 0) for a in (teacher_hidden, student_hidden)
+        lax.dynamic_slice_in_dim(a, (2 * x + odd) * eighth, eighth, 0)
+        for a in (teacher_hidden, student_hidden)
     ]
-    quarter = shift(jnp.concatenate(piece, axis=1), "y", 2)
+    piece = shift(jnp.concatenate(piece, axis=1), "y", 2)
     hidden = jnp.concatenate([teacher_hidden, student_hidden], axis=1)
-    quarter, whole = lax.optimization_barrier((quarter, hidden))
+    piece, whole = lax.optimization_barrier((piece, hidden))
+    swapped = lax.ppermute(piece, "z", [(i, i ^ 1) for i in range(n_z)])
+    quarter = jnp.where(
+        odd == 0, jnp.concatenate([piece, swapped]), jnp.concatenate([swapped, piece])
+    )
     after, before = shift(whole, "y", 1), shift(whole, "y", 3)
     codes_p = shift(teacher_codes, "c", 1)
     weight_p = shift(student_weight, "c", 1)

time: 172 us -> 168 us (0.977)
  waiting for transfers between devices: 60.8 us -> 55 us
  local copies, waits for them, and re-layouts: 8.78 us -> 10.6 us
    ppermute x12, waiting for transfers between devices: 20.6 us -> 9.42 us  [shift(): return lax.ppermute(a, axis, [((i + by) % n, i) for i in range(n)])]
    ppermute x0 -> x1, waiting for transfers between devices: none -> 3.6 us  [local(): swapped = lax.ppermute(piece, 'z', [(i, i ^ 1) for i in range(n_z)])]
    unnamed x22, local copies, waits for them, and re-layouts: 4.6 us -> 6.64 us
    ppermute x0 -> x1, starting transfers between devices: none -> 1.92 us  [local(): swapped = lax.ppermute(piece, 'z', [(i, i ^ 1) for i in range(n_z)])]
    all_to_all x1, waiting for transfers between devices: 29.7 us -> 31.5 us  [local(): got = lax.all_to_all(blocks, ('x', 'y'), 0, 0, tiled=True)]
  transfers between devices with their start and end apart: 15 -> 16, of which waited for: 9 -> 8; matrix products, arithmetic and copies ran while one was open for 3% -> 5% of each run, Pallas kernels for 21% -> 21%
where the time goes in v7:
time: 168 us; the launch traced here: 167 us
  Pallas kernels  55.5 us (33%)
  waiting for transfers between devices  55 us (33%)
  starting transfers between devices  28.8 us (17%)
  blocking collectives  12.2 us (7%)
  local copies, waits for them, and re-layouts  10.6 us (6%)
  other arithmetic  4.22 us (3%)
    all_to_all x1, waiting for transfers between devices, local(): got = lax.all_to_all(blocks, ('x', 'y'), 0, 0, tiled=True)  31.5 us
    pallas_call x2, Pallas kernels, logits_of(): pl.pallas_call(functools.partial(logits_kernel, steps, len(pieces)), grid...  22.4 us
    all_to_all x1, blocking collectives, local(): seen = lax.all_to_all(mine, ('x', 'y'), 0, 0, tiled=True)  12.2 us
    ppermute x12, starting transfers between devices, shift(): return lax.ppermute(a, axis, [((i + by) % n, i) for i in range(n)])  10 us
    ppermute x12, waiting for transfers between devices, shift(): return lax.ppermute(a, axis, [((i + by) % n, i) for i in range(n)])  9.42 us
    pallas_call x1, Pallas kernels, dequantize(): pl.pallas_call(functools.partial(dequant_kernel, steps), grid=(2 * steps,...  9.24 us
    pallas_call x1, Pallas kernels, gradients(): pl.pallas_call(grad_kernel, grid_spec=pltpu.PrefetchScalarGridSpec(num_sc...  9.22 us
    all_to_all x1, waiting for transfers between devices, to_all(): lax.all_to_all(jnp.broadcast_to(a[None], (n, *a.shape)), axes, 0, 0, tile...  9.05 us
  transfers between devices with their start and end apart: 16, of which 8 were waited for; matrix products, arithmetic and copies ran while one was open for 5% of the time, Pallas kernels for 21%

profile of v7, /device:TPU:8, one launch (start us, length us, event | category | flops | bytes accessed | tf_op | source)
XLA Modules:
  0.0 167.2 jit_solution(16529089764848621612)
XLA Ops:
  3.1 2.4 %collective-permute-start = (bf16[16,7936]{1,0:T(8,128)(2,1)S(1)}, bf16[16,7936]{1,0:T(8,128)(2,1)}, u32[]{:S(2)}, u32[]{:S(2)}) collective-permute-start(bf16[16,7936]{1,0:T(8,128)(2,1)S(1)} %pad_maximum_fusion), channel_id=1, source_target_pairs={{4,0},{6,2},{0,4},{2,6},{5,1},{7,3},{1,5},{3,7},{12,8},{14,10},{8,... | collective-permute-start | bytes 761864 | tf_op jit(solution)/shard_map/ppermute | solution.py:20
  5.5 2.5 %constant_dynamic-update-slice_fusion.1 = bf16[128,7936]{1,0:T(8,128)(2,1)} fusion(bf16[128,5376]{1,0:T(8,128)(2,1)} %param.6), kind=kLoop, calls=%fused_computation.34 | loop fusion | bytes 2752512
  8.9 4.1 %collective-permute-done = bf16[16,7936]{1,0:T(8,128)(2,1)} collective-permute-done((bf16[16,7936]{1,0:T(8,128)(2,1)S(1)}, bf16[16,7936]{1,0:T(8,128)(2,1)}, u32[]{:S(2)}, u32[]{:S(2)}) %collective-permute-start) | collective-permute-done | bytes 253984 | tf_op jit(solution)/shard_map/ppermute | solution.py:20
  12.9 1.9 %collective-permute-start.3 = (bf16[16,7936]{1,0:T(8,128)(2,1)}, bf16[16,7936]{1,0:T(8,128)(2,1)S(1)}, u32[]{:S(2)}, u32[]{:S(2)}) collective-permute-start(bf16[16,7936]{1,0:T(8,128)(2,1)} %collective-permute-done), channel_id=1, source_target_pairs={{0,8},{8,0},{16,24},{24,16},{32,40},{40,32},{48,56},{56,48},{1,9},... | collective-permute-start | bytes 761864 | tf_op jit(solution)/shard_map/ppermute | solution.py:389
  15.3 1.6 collective-permute-start.2
  17.0 3.6 %collective-permute-done.3 = bf16[16,7936]{1,0:T(8,128)(2,1)S(1)} collective-permute-done((bf16[16,7936]{1,0:T(8,128)(2,1)}, bf16[16,7936]{1,0:T(8,128)(2,1)S(1)}, u32[]{:S(2)}, u32[]{:S(2)}) %collective-permute-start.3) | collective-permute-done | bytes 253984 | tf_op jit(solution)/shard_map/ppermute | solution.py:389
  21.3 1.4 maximum_select_fusion.rest_1_
  23.6 2.8 %collective-permute-start.7 = (bf16[32,7936]{1,0:T(8,128)(2,1)S(1)}, bf16[32,7936]{1,0:T(8,128)(2,1)}, u32[]{:S(2)}, u32[]{:S(2)}) collective-permute-start(bf16[32,7936]{1,0:T(8,128)(2,1)S(1)} %maximum_select_fusion.rest_1_), channel_id=1, source_target_pairs={{64,0},{128,64},{192,128},{0,192},{65,1},{129,65},{193,129},{1,193... | collective-permute-start | bytes 1523720 | tf_op jit(solution)/shard_map/ppermute | solution.py:20
  28.1 7.3 %turn.1.turned_ref = bf16[2560,1024]{1,0:T(8,128)(2,1)} custom-call(bf16[512,2560]{1,0:T(8,128)(2,1)S(1)} %copy-done, bf16[512,2560]{1,0:T(8,128)(2,1)} %collective-permute-done.5.rest_7_.other_ref.rest_4_), custom_call_target="tpu_custom_call" | custom-call | bytes 10485760 | tf_op jit(solution)/shard_map/turn/pallas_call | solution.py:94
  35.4 2.6 %copy-done.1 = bf16[512,5376]{1,0:T(8,128)(2,1)S(1)} copy-done((bf16[512,5376]{1,0:T(8,128)(2,1)S(1)}, bf16[512,5376]{1,0:T(8,128)(2,1)}, u32[]{:S(2)}) %copy-start.1) | copy-done | bytes 5505048
  38.0 9.2 %dequantize.1.rest_5_.rest_2_ = bf16[1024,5376]{1,0:T(8,128)(2,1)S(1)} custom-call(bf16[512,5376]{1,0:T(8,128)(2,1)S(1)} %copy-done.1, bf16[512,5376]{1,0:T(8,128)(2,1)} %collective-permute-done.4.other_ref, f32[512,42]{1,0:T(8,128)S(1)} %copy.22.own_scale_ref, f32[512,42]{1,0:T(8,128)S(1)} %copy-done.3), custom_call_target="tpu_custom_call" | custom-call | flops 5505024 | bytes 22020096 | tf_op jit(solution)/shard_map/dequantize/pallas_call | solution.py:62
  47.2 1.5 collective-permute-done.7.rest_2_
  48.7 3.8 %collective-permute-done.9.rest_4_ = bf16[32,7936]{1,0:T(8,128)(2,1)} collective-permute-done((bf16[32,7936]{1,0:T(8,128)(2,1)S(1)}, bf16[32,7936]{1,0:T(8,128)(2,1)}, u32[]{:S(2)}, u32[]{:S(2)}) %collective-permute-start.9) | collective-permute-done | bytes 507936 | tf_op jit(solution)/shard_map/ppermute | solution.py:20
  52.5 11.1 %logits.2 = (f32[1024,256]{1,0:T(8,128)}, f32[1024,256]{1,0:T(8,128)}, f32[8,256]{1,0:T(8,128)S(1)}, bf16[256,2560]{1,0:T(8,128)(2,1)}) custom-call(s32[2]{0:T(128)S(1)} %pad_add_fusion.place_ref.y_ref, bf16[128,7936]{1,0:T(8,128)(2,1)} %constant_dynamic-update-slice_fusion.rest_0_, bf16[32,7936]{1,0:T(8,128)(2,1)S(1)} %maximum_select_fusion.rest_1_, ...), custom_call_target="tpu_custom_call" | custom-call | flops 4160749568 | bytes 22413312 | tf_op jit(solution)/shard_map/logits/pallas_call | solution.py:243
  63.6 11.3 %logits.3 = (f32[1024,256]{1,0:T(8,128)}, f32[1024,256]{1,0:T(8,128)}, f32[8,256]{1,0:T(8,128)}, bf16[256,2560]{1,0:T(8,128)(2,1)}, f32[16,8,512]{2,1,0:T(8,128)S(1)}) custom-call(s32[2]{0:T(128)S(1)} %pad_add_fusion.place_ref.y_ref, bf16[128,7936]{1,0:T(8,128)(2,1)} %collective-permute-done.1.rest_0_, bf16[128,7936]{1,0:T(8,128)(2,1)} %collective-permute-done.2.rest_1_, ...), custom_call_target="tpu_custom_call" | custom-call | flops 4160749568 | bytes 22413312 | tf_op jit(solution)/shard_map/logits/pallas_call | solution.py:243
  75.0 12.2 %all_to_all.20 = f32[16,8,512]{2,1,0:T(8,128)S(1)} all-to-all(f32[16,8,512]{2,1,0:T(8,128)S(1)} %get-tuple-element.34), channel_id=1, replica_groups=mesh['x'=4,'z'=8,'y'=4,'c'=2] {'x','y'}, dimensions={0} | all-to-all | bytes 524288 | tf_op jit(solution)/shard_map/all_to_all | solution.py:416
  88.1 8.3 %all-to-all-start.1 = ((f32[8,5,512]{2,1,0:T(8,128)}), f32[8,5,512]{2,1,0:T(8,128)S(1)}, u32[]{:S(2)}, u32[]{:S(2)}) async-start(f32[8,5,512]{2,1,0:T(8,128)} %broadcast_in_dim.20), calls=%async_computation.1 | async-start | bytes 262144 | tf_op jit(solution)/shard_map/all_to_all | solution.py:323
  96.4 9.1 %all-to-all-done.1 = f32[8,5,512]{2,1,0:T(8,128)S(1)} async-done(((f32[8,5,512]{2,1,0:T(8,128)}), f32[8,5,512]{2,1,0:T(8,128)S(1)}, u32[]{:S(2)}, u32[]{:S(2)}) %all-to-all-start.1) | async-done | bytes 81952 | tf_op jit(solution)/shard_map/all_to_all | solution.py:323
  106.3 9.2 %gradients.1 = (bf16[512,512]{1,0:T(8,128)(2,1)}, bf16[512,512]{1,0:T(8,128)(2,1)}, bf16[4,4,640,128]{3,2,1,0:T(8,128)(2,1)}) custom-call(s32[2]{0:T(128)} %copy-done.4, f32[8,512]{1,0:T(8,128)} %pad_maximum_fusion.1.rows_ref, f32[1024,256]{1,0:T(8,128)} %get-tuple-element.35.t0, f32[1024,256]{1,0:T(8,128)} %get-tuple-element.36.s0, ...), custom_call_target="tpu_custom_call" | custom-call | flops 2684354560 | bytes 13107200 | tf_op jit(solution)/shard_map/gradients/pallas_call | solution.py:295
  115.6 5.2 %all-to-all-start.2 = ((bf16[16,640,128]{2,1,0:T(8,128)(2,1)}), bf16[16,640,128]{2,1,0:T(8,128)(2,1)S(1)}, u32[]{:S(2)}, u32[]{:S(2)}) async-start(bf16[16,640,128]{2,1,0:T(8,128)(2,1)} %bitcast.83), calls=%async_computation.2 | async-start | bytes 5242880 | tf_op jit(solution)/shard_map/all_to_all | solution.py:441
  121.4 31.5 %all-to-all-done.2 = bf16[16,640,128]{2,1,0:T(8,128)(2,1)S(1)} async-done(((bf16[16,640,128]{2,1,0:T(8,128)(2,1)}), bf16[16,640,128]{2,1,0:T(8,128)(2,1)S(1)}, u32[]{:S(2)}, u32[]{:S(2)}) %all-to-all-start.2) | async-done | bytes 2621472 | tf_op jit(solution)/shard_map/all_to_all | solution.py:441
  153.9 3.4 %all-to-all-start.3 = ((bf16[8,80,128]{2,1,0:T(8,128)(2,1)}), bf16[8,80,128]{2,1,0:T(8,128)(2,1)S(1)}, u32[]{:S(2)}, u32[]{:S(2)}) async-start(bf16[8,80,128]{2,1,0:T(8,128)(2,1)} %bitcast.20), calls=%async_computation.3 | async-start | bytes 327680 | tf_op jit(solution)/shard_map/all_to_all | solution.py:443
  157.8 7.4 %weight_gradient.1 = bf16[512,2560]{1,0:T(8,128)(2,1)} custom-call(bf16[512,512]{1,0:T(8,128)(2,1)} %get-tuple-element.41.own_ref, bf16[512,512]{1,0:T(8,128)(2,1)} %collective-permute-done.10.from_ref, bf16[256,2560]{1,0:T(8,128)(2,1)} %get-tuple-element.43.s0_ref, bf16[256,2560]{1,0:T(8,128)(2,1)} %get-tuple-element.44.s1_ref, ...), custom_call_target="tpu_custom_call" | custom-call | flops 2684354560 | bytes 8912896 | tf_op jit(solution)/shard_map/weight_gradient/pallas_call | solution.py:355
  165.1 1.5 all-to-all-done.3
  (64 shorter events, 11.7 us)
Async XLA Ops:
  0.6 7.4 %copy-start.5 = (bf16[128,2560]{1,0:T(8,128)(2,1)S(1)}, bf16[128,2560]{1,0:T(8,128)(2,1)}, u32[]{:S(2)}) copy-start(bf16[128,2560]{1,0:T(8,128)(2,1)} %param.7) | copy-start | bytes 1966084
  0.6 22.9 %collective-permute-start.4 = (bf16[512,5376]{1,0:T(8,128)(2,1)}, bf16[512,5376]{1,0:T(8,128)(2,1)}, u32[]{:S(2)}, u32[]{:S(2)}) collective-permute-start(bf16[512,5376]{1,0:T(8,128)(2,1)} %own_ref.2), channel_id=1, source_target_pairs={{1,0},{0,1},{3,2},{2,3},{5,4},{4,5},{7,6},{6,7},{9,8},{8,9},{11,10... | collective-permute-start | bytes 16515080 | tf_op jit(solution)/shard_map/ppermute | solution.py:20
  0.7 22.8 %collective-permute-start.5 = (bf16[512,2560]{1,0:T(8,128)(2,1)}, bf16[512,2560]{1,0:T(8,128)(2,1)}, u32[]{:S(2)}, u32[]{:S(2)}) collective-permute-start(bf16[512,2560]{1,0:T(8,128)(2,1)} %rest_3_.1), channel_id=1, source_target_pairs={{1,0},{0,1},{3,2},{2,3},{5,4},{4,5},{7,6},{6,7},{9,8},{8,9},{11,10... | collective-permute-start | bytes 7864328 | tf_op jit(solution)/shard_map/ppermute | solution.py:20
  3.1 13.8 %copy-start.7 = (f32[512,42]{0,1:T(8,128)S(1)}, f32[512,42]{0,1:T(8,128)}, u32[]{:S(2)}) copy-start(f32[512,42]{0,1:T(8,128)} %param.9) | copy-start | bytes 258052
  3.1 9.8 %collective-permute-start = (bf16[16,7936]{1,0:T(8,128)(2,1)S(1)}, bf16[16,7936]{1,0:T(8,128)(2,1)}, u32[]{:S(2)}, u32[]{:S(2)}) collective-permute-start(bf16[16,7936]{1,0:T(8,128)(2,1)S(1)} %pad_maximum_fusion), channel_id=1, source_target_pairs={{4,0},{6,2},{0,4},{2,6},{5,1},{7,3},{1,5},{3,7},{12,8},{14,10},{8,... | collective-permute-start | bytes 761864 | tf_op jit(solution)/shard_map/ppermute | solution.py:20
  8.0 20.1 %copy-start.9 = (bf16[128]{0:T(256)(128)(2,1)S(1)}, bf16[128]{0:T(256)(128)(2,1)}, u32[]{:S(2)}) copy-start(bf16[128]{0:T(256)(128)(2,1)} %param.11) | copy-start | bytes 772
  8.0 20.1 %copy-start = (bf16[512,2560]{1,0:T(8,128)(2,1)S(1)}, bf16[512,2560]{1,0:T(8,128)(2,1)}, u32[]{:S(2)}) copy-start(bf16[512,2560]{1,0:T(8,128)(2,1)} %rest_3_.1) | copy-start | bytes 7864324
  12.9 7.7 %collective-permute-start.3 = (bf16[16,7936]{1,0:T(8,128)(2,1)}, bf16[16,7936]{1,0:T(8,128)(2,1)S(1)}, u32[]{:S(2)}, u32[]{:S(2)}) collective-permute-start(bf16[16,7936]{1,0:T(8,128)(2,1)} %collective-permute-done), channel_id=1, source_target_pairs={{0,8},{8,0},{16,24},{24,16},{32,40},{40,32},{48,56},{56,48},{1,9},... | collective-permute-start | bytes 761864 | tf_op jit(solution)/shard_map/ppermute | solution.py:389
  14.9 48.8 %collective-permute-start.1 = (bf16[128,7936]{1,0:T(8,128)(2,1)}, bf16[128,7936]{1,0:T(8,128)(2,1)}, u32[]{:S(2)}, u32[]{:S(2)}) collective-permute-start(bf16[128,7936]{1,0:T(8,128)(2,1)} %constant_dynamic-update-slice_fusion.rest_0_), channel_id=1, source_target_pairs={{2,0},{4,2},{6,4},{0,6},{3,1},{5,3},{7,5},{1,7},{10,8},{12,10},{14... | collective-permute-start | bytes 6094856 | tf_op jit(solution)/shard_map/ppermute | solution.py:20
  15.3 48.3 %collective-permute-start.2 = (bf16[128,7936]{1,0:T(8,128)(2,1)}, bf16[128,7936]{1,0:T(8,128)(2,1)}, u32[]{:S(2)}, u32[]{:S(2)}) collective-permute-start(bf16[128,7936]{1,0:T(8,128)(2,1)} %constant_dynamic-update-slice_fusion.rest_0_), channel_id=1, source_target_pairs={{6,0},{0,2},{2,4},{4,6},{7,1},{1,3},{3,5},{5,7},{14,8},{8,10},{10,... | collective-permute-start | bytes 6094856 | tf_op jit(solution)/shard_map/ppermute | solution.py:20
  21.3 1.5 collective-permute-start.6
  23.6 25.1 %collective-permute-start.7 = (bf16[32,7936]{1,0:T(8,128)(2,1)S(1)}, bf16[32,7936]{1,0:T(8,128)(2,1)}, u32[]{:S(2)}, u32[]{:S(2)}) collective-permute-start(bf16[32,7936]{1,0:T(8,128)(2,1)S(1)} %maximum_select_fusion.rest_1_), channel_id=1, source_target_pairs={{64,0},{128,64},{192,128},{0,192},{65,1},{129,65},{193,129},{1,193... | collective-permute-start | bytes 1523720 | tf_op jit(solution)/shard_map/ppermute | solution.py:20
  26.3 22.4 %collective-permute-start.8 = (bf16[32,7936]{1,0:T(8,128)(2,1)S(1)}, bf16[32,7936]{1,0:T(8,128)(2,1)}, u32[]{:S(2)}, u32[]{:S(2)}) collective-permute-start(bf16[32,7936]{1,0:T(8,128)(2,1)S(1)} %maximum_select_fusion.rest_1_), channel_id=1, source_target_pairs={{128,0},{192,64},{0,128},{64,192},{129,1},{193,65},{1,129},{65,193... | collective-permute-start | bytes 1523720 | tf_op jit(solution)/shard_map/ppermute | solution.py:20
  27.1 25.3 %collective-permute-start.9 = (bf16[32,7936]{1,0:T(8,128)(2,1)S(1)}, bf16[32,7936]{1,0:T(8,128)(2,1)}, u32[]{:S(2)}, u32[]{:S(2)}) collective-permute-start(bf16[32,7936]{1,0:T(8,128)(2,1)S(1)} %maximum_select_fusion.rest_1_), channel_id=1, source_target_pairs={{192,0},{0,64},{64,128},{128,192},{193,1},{1,65},{65,129},{129,193... | collective-permute-start | bytes 1523720 | tf_op jit(solution)/shard_map/ppermute | solution.py:20
  28.1 35.5 %copy-start.4 = (s32[2]{0:T(128)}, s32[2]{0:T(128)S(1)}, u32[]{:S(2)}) copy-start(s32[2]{0:T(128)S(1)} %pad_add_fusion.place_ref.y_ref) | copy-start | bytes 28
  28.1 7.3 %copy-start.3 = (f32[512,42]{1,0:T(8,128)S(1)}, f32[512,42]{1,0:T(8,128)}, u32[]{:S(2)}) copy-start(f32[512,42]{1,0:T(8,128)} %copy-done.2) | copy-start | bytes 258052
  35.4 2.6 %copy-start.1 = (bf16[512,5376]{1,0:T(8,128)(2,1)S(1)}, bf16[512,5376]{1,0:T(8,128)(2,1)}, u32[]{:S(2)}) copy-start(bf16[512,5376]{1,0:T(8,128)(2,1)} %own_ref.2) | copy-start | bytes 16515076
  88.1 17.4 %all-to-all-start.1 = ((f32[8,5,512]{2,1,0:T(8,128)}), f32[8,5,512]{2,1,0:T(8,128)S(1)}, u32[]{:S(2)}, u32[]{:S(2)}) async-start(f32[8,5,512]{2,1,0:T(8,128)} %broadcast_in_dim.20), calls=%async_computation.1 | async-start | bytes 262144 | tf_op jit(solution)/shard_map/all_to_all | solution.py:323
  115.6 5.7 %copy-start.8 = (bf16[512,512]{1,0:T(8,128)(2,1)S(1)}, bf16[512,512]{1,0:T(8,128)(2,1)}, u32[]{:S(2)}) copy-start(bf16[512,512]{1,0:T(8,128)(2,1)} %get-tuple-element.42) | copy-start | bytes 1572868
  115.6 37.3 %all-to-all-start.2 = ((bf16[16,640,128]{2,1,0:T(8,128)(2,1)}), bf16[16,640,128]{2,1,0:T(8,128)(2,1)S(1)}, u32[]{:S(2)}, u32[]{:S(2)}) async-start(bf16[16,640,128]{2,1,0:T(8,128)(2,1)} %bitcast.83), calls=%async_computation.2 | async-start | bytes 5242880 | tf_op jit(solution)/shard_map/all_to_all | solution.py:441
  120.7 37.0 %collective-permute-start.12 = (bf16[256,2560]{1,0:T(8,128)(2,1)}, bf16[256,2560]{1,0:T(8,128)(2,1)}, u32[]{:S(2)}, u32[]{:S(2)}) collective-permute-start(bf16[256,2560]{1,0:T(8,128)(2,1)} %get-tuple-element.44.s1_ref), channel_id=1, source_target_pairs={{1,0},{0,1},{3,2},{2,3},{5,4},{4,5},{7,6},{6,7},{9,8},{8,9},{11,10... | collective-permute-start | bytes 3932168 | tf_op jit(solution)/shard_map/ppermute | solution.py:20
  120.8 37.0 %collective-permute-start.11 = (bf16[256,2560]{1,0:T(8,128)(2,1)}, bf16[256,2560]{1,0:T(8,128)(2,1)}, u32[]{:S(2)}, u32[]{:S(2)}) collective-permute-start(bf16[256,2560]{1,0:T(8,128)(2,1)} %get-tuple-element.43.s0_ref), channel_id=1, source_target_pairs={{1,0},{0,1},{3,2},{2,3},{5,4},{4,5},{7,6},{6,7},{9,8},{8,9},{11,10... | collective-permute-start | bytes 3932168 | tf_op jit(solution)/shard_map/ppermute | solution.py:20
  121.3 36.5 %collective-permute-start.10 = (bf16[512,512]{1,0:T(8,128)(2,1)S(1)}, bf16[512,512]{1,0:T(8,128)(2,1)}, u32[]{:S(2)}, u32[]{:S(2)}) collective-permute-start(bf16[512,512]{1,0:T(8,128)(2,1)S(1)} %copy-done.8), channel_id=1, source_target_pairs={{1,0},{0,1},{3,2},{2,3},{5,4},{4,5},{7,6},{6,7},{9,8},{8,9},{11,10... | collective-permute-start | bytes 1572872 | tf_op jit(solution)/shard_map/ppermute | solution.py:20
  153.9 12.7 %all-to-all-start.3 = ((bf16[8,80,128]{2,1,0:T(8,128)(2,1)}), bf16[8,80,128]{2,1,0:T(8,128)(2,1)S(1)}, u32[]{:S(2)}, u32[]{:S(2)}) async-start(bf16[8,80,128]{2,1,0:T(8,128)(2,1)} %bitcast.20), calls=%async_computation.3 | async-start | bytes 327680 | tf_op jit(solution)/shard_map/all_to_all | solution.py:443
  (2 other events, 1.4 us)

commit v8 on v7

--- a/solution.py
+++ b/solution.py
@@ -20,15 +20,11 @@
     return lax.ppermute(a, axis, [((i + by) % n, i) for i in range(n)])
 
 
-def rolled(blocks, start):
-    n = blocks.shape[0]
-    return lax.dynamic_slice_in_dim(jnp.concatenate([blocks, blocks[:-1]]), start % n, n, 0)
-
-
 NT = (((1,), (1,)), ((), ()))
 MIB = 1024 * 1024
 DEQUANT_ROWS = 128
 LOGIT_ROWS = 256
+ROW_STEP = 16
 WEIGHT_COLUMNS = 512
 
 
@@ -70,7 +66,7 @@
         ],
         out_specs=pl.BlockSpec((DEQUANT_ROWS, width), lambda i: (i, 0)),
         out_shape=jax.ShapeDtypeStruct((2 * rows, width), BF16),
-        compiler_params=pltpu.CompilerParams(vmem_limit_bytes=12 * MIB),
+        compiler_params=pltpu.CompilerParams(vmem_limit_bytes=56 * MIB),
         cost_estimate=pl.CostEstimate(
             flops=2 * rows * width, transcendentals=0, bytes_accessed=8 * rows * width
         ),
@@ -146,12 +142,11 @@
         stat_ref[4:5] = stat_ref[4:5] * s_keep + s_total
 
 
-def load_pair(x_ref, refs, pair, sem):
-    tok, part = refs[0].shape[0], refs[1].shape[0]
-    copies = [pltpu.make_async_copy(refs[0], pair.at[pl.ds(0, tok)], sem.at[0])]
-    for k, ref in enumerate(refs[1:]):
-        at = pl.multiple_of(tok + lax.rem(x_ref[1] + k, tok // part) * part, part)
-        copies.append(pltpu.make_async_copy(ref, pair.at[pl.ds(at, part)], sem.at[k + 1]))
+def load_blocks(place_ref, refs, block, sem):
+    copies = []
+    for k, ref in enumerate(refs):
+        at = pl.multiple_of(place_ref[k + 1], ROW_STEP)
+        copies.append(pltpu.make_async_copy(ref, block.at[pl.ds(at, ref.shape[0])], sem.at[k]))
     for copy in copies:
         copy.start()
     for copy in copies:
@@ -161,7 +156,6 @@
 def logits_kernel(steps, n_pieces, place_ref, *rest):
     pieces_hbm, rest = rest[:n_pieces], rest[n_pieces:]
     (table_ref, weight_ref, weight_p_ref), rest = rest[:3], rest[3:]
-    tok = pieces_hbm[0].shape[0]
     spread = len(rest) > 6
     first_stat_ref, scale_ref = rest[:2] if spread else (None, None)
     rest = rest[2:] if spread else rest
@@ -172,7 +166,7 @@
 
     @pl.when(step == 0)
     def _():
-        load_pair(place_ref, pieces_hbm, pair, sem)
+        load_blocks(place_ref, pieces_hbm, pair, sem)
         student_ref[...] = pair[:, table_ref.shape[1] :]
 
     @pl.when(step < steps)
@@ -188,15 +182,16 @@
         @pl.when(step == 2 * steps - 1)
         def _():
             copies, _, wide = spread_ref.shape
+            tok = scale_ref.shape[1]
             n_y = wide // tok
             row = lax.broadcasted_iota(jnp.int32, (8, tok), 0)
             scale = jnp.broadcast_to(scale_ref[...], (8, tok))
             first, last = first_stat_ref[...], stat_ref[...]
             pieces = (
-                jnp.where(row == 5, scale, first[:, :tok]),
+                jnp.where(row == 5, scale, first),
+                last[:, tok : 2 * tok],
                 last[:, :tok],
-                first[:, tok:],
-                last[:, tok:],
+                last[:, 2 * tok :],
             )
             for r, piece in enumerate(pieces):
                 at = pl.multiple_of(lax.rem(place_ref[0] + r, n_y) * tok, tok)
@@ -207,8 +202,7 @@
 def logits_of(place, pieces, table, weight, weight_p, first_stats=None, scale=None, copies=0):
     width_t = table.shape[1]
     rows, width_s = weight.shape
-    tok = pieces[0].shape[0]
-    tokens = 2 * tok
+    tokens = sum(p.shape[0] for p in pieces)
     steps = rows // LOGIT_ROWS
     tile = pltpu.HBM((2 * rows, tokens), F32)
 
@@ -235,11 +229,12 @@
     ]
     operands = [place, *pieces, table, weight, weight_p]
     if first_stats is not None:
-        in_specs.append(pl.BlockSpec((8, tokens), lambda i, y: (0, 0)))
-        in_specs.append(pl.BlockSpec((1, tok), lambda i, y: (0, 0)))
+        every = tokens + first_stats.shape[1]
+        in_specs.append(pl.BlockSpec(first_stats.shape, lambda i, y: (0, 0)))
+        in_specs.append(pl.BlockSpec(scale.shape, lambda i, y: (0, 0)))
         operands += [first_stats, scale]
-        out_specs.append(pl.BlockSpec((copies, 8, 2 * tokens), lambda i, y: (0, 0, 0)))
-        out_shape.append(jax.ShapeDtypeStruct((copies, 8, 2 * tokens), F32))
+        out_specs.append(pl.BlockSpec((copies, 8, every), lambda i, y: (0, 0, 0)))
+        out_shape.append(jax.ShapeDtypeStruct((copies, 8, every), F32))
     return pl.pallas_call(
         functools.partial(logits_kernel, steps, len(pieces)),
         grid_spec=pltpu.PrefetchScalarGridSpec(
@@ -253,7 +248,7 @@
             ],
         ),
         out_shape=out_shape,
-        compiler_params=pltpu.CompilerParams(vmem_limit_bytes=22 * MIB),
+        compiler_params=pltpu.CompilerParams(vmem_limit_bytes=56 * MIB),
         cost_estimate=pl.CostEstimate(
             flops=4 * rows * tokens * (width_t + width_s),
             transcendentals=4 * rows * tokens,
@@ -269,8 +264,8 @@
 
     @pl.when(pl.program_id(0) == 0)
     def _():
-        for p, (t, s) in enumerate(((t0, s0), (t1, s1))):
-            at = slice(2 * p * tok, 2 * (p + 1) * tok)
+        split = t0.shape[1]
+        for t, s, at in ((t0, s0, slice(0, split)), (t1, s1, slice(split, None))):
             t_lse, s_lse, scale = (rows_ref[k : k + 1, at] for k in range(3))
             for q, ref in enumerate((own_ref, other_ref)):
                 rows = slice(q * half, (q + 1) * half)
@@ -286,12 +281,13 @@
 
 def gradients(y, rows, logits, turned, n_x, n_y):
     (t0, s0), (t1, s1) = logits
-    vocab, tokens = t0.shape
+    vocab, tokens = t0.shape[0], t0.shape[1] + t1.shape[1]
     width = turned.shape[0]
-    lg = pltpu.HBM((vocab // 2, 2 * tokens), BF16)
-    whole = pl.BlockSpec((vocab, tokens), lambda i, y: (0, 0))
-    lg_spec = pl.BlockSpec((vocab // 2, 2 * tokens), lambda i, y: (0, 0))
-    cut = (width // n_x, 2 * tokens // n_y)
+    lg = pltpu.HBM((vocab // 2, tokens), BF16)
+    first = pl.BlockSpec(t0.shape, lambda i, y: (0, 0))
+    others = pl.BlockSpec(t1.shape, lambda i, y: (0, 0))
+    lg_spec = pl.BlockSpec((vocab // 2, tokens), lambda i, y: (0, 0))
+    cut = (width // n_x, tokens // n_y)
     return pl.pallas_call(
         grad_kernel,
         grid_spec=pltpu.PrefetchScalarGridSpec(
@@ -299,10 +295,10 @@
             grid=(n_x,),
             in_specs=[
                 pl.BlockSpec(rows.shape, lambda i, y: (0, 0)),
-                whole,
-                whole,
-                whole,
-                whole,
+                first,
+                first,
+                others,
+                others,
                 pl.BlockSpec((width // n_x, vocab), lambda i, y: (i, 0)),
             ],
             out_specs=[lg_spec, lg_spec, pl.BlockSpec((1, n_y, *cut), lambda i, y: (i, 0, 0, 0))],
@@ -310,9 +306,9 @@
         out_shape=[lg, lg, pltpu.HBM((n_x, n_y, *cut), BF16)],
         compiler_params=pltpu.CompilerParams(vmem_limit_bytes=56 * MIB),
         cost_estimate=pl.CostEstimate(
-            flops=4 * vocab * tokens * width,
-            transcendentals=4 * vocab * tokens,
-            bytes_accessed=2 * width * (vocab + 2 * tokens) + 20 * vocab * tokens,
+            flops=2 * vocab * tokens * width,
+            transcendentals=2 * vocab * tokens,
+            bytes_accessed=2 * width * (vocab + tokens) + 10 * vocab * tokens,
         ),
         name="gradients",
     )(y, rows, t0, s0, t1, s1, turned)
@@ -350,19 +346,20 @@
 
 def weight_gradient(own, from_p, *students):
     rows, tokens = own.shape
-    half, width = students[0].shape
+    width = students[0].shape[1]
     whole = pl.BlockSpec((rows, tokens), lambda i: (0, 0))
     return pl.pallas_call(
         weight_kernel,
         grid=(width // WEIGHT_COLUMNS,),
-        in_specs=[whole, whole] + [pl.BlockSpec((half, WEIGHT_COLUMNS), lambda i: (0, i))] * 4,
+        in_specs=[whole, whole]
+        + [pl.BlockSpec((a.shape[0], WEIGHT_COLUMNS), lambda i: (0, i)) for a in students],
         out_specs=pl.BlockSpec((rows, WEIGHT_COLUMNS), lambda i: (0, i)),
         out_shape=jax.ShapeDtypeStruct((rows, width), BF16),
         compiler_params=pltpu.CompilerParams(vmem_limit_bytes=56 * MIB),
         cost_estimate=pl.CostEstimate(
             flops=4 * rows * tokens * width,
             transcendentals=0,
-            bytes_accessed=2 * width * (rows + 4 * half) + 4 * rows * tokens,
+            bytes_accessed=2 * width * (rows + 2 * tokens) + 4 * rows * tokens,
         ),
         name="weight_gradient",
     )(own, from_p, *students)
@@ -376,43 +373,56 @@
     n_x, n_z, n_y = (lax.axis_size(a) for a in ("x", "z", "y"))
     x, y = lax.axis_index("x"), lax.axis_index("y")
 
-    place = jnp.stack([y, x]).astype(jnp.int32)
-    eighth = tok // (2 * n_x)
+    def packed(start, size):
+        cut = [
+            lax.dynamic_slice_in_dim(a, start, size, 0) for a in (teacher_hidden, student_hidden)
+        ]
+        return jnp.concatenate(cut, axis=1)
+
+    def z_swapped(a):
+        return lax.ppermute(a, "z", [(i, i ^ 1) for i in range(n_z)])
+
+    eighth, share = tok // (2 * n_x), tok // 4
     odd = lax.rem(lax.axis_index("z"), 2)
-    piece = [
-        lax.dynamic_slice_in_dim(a, (2 * x + odd) * eighth, eighth, 0)
-        for a in (teacher_hidden, student_hidden)
+    hidden = packed(0, tok)
+    piece = shift(packed((2 * x + odd) * eighth, eighth), "y", 2)
+    piece, part = lax.optimization_barrier((piece, packed(odd * share, share)))
+    after, before = shift(part, "y", 1), shift(part, "y", 3)
+    after, before, rest = lax.optimization_barrier((after, before, packed(2 * share, 2 * share)))
+    blocks = [
+        [a, z_swapped(a), shift(rest, "y", by)] for a, by in ((after, 1), (before, 3))
     ]
-    piece = shift(jnp.concatenate(piece, axis=1), "y", 2)
-    hidden = jnp.concatenate([teacher_hidden, student_hidden], axis=1)
-    piece, whole = lax.optimization_barrier((piece, hidden))
-    swapped = lax.ppermute(piece, "z", [(i, i ^ 1) for i in range(n_z)])
+    swapped = z_swapped(piece)
     quarter = jnp.where(
         odd == 0, jnp.concatenate([piece, swapped]), jnp.concatenate([swapped, piece])
     )
-    after, before = shift(whole, "y", 1), shift(whole, "y", 3)
     codes_p = shift(teacher_codes, "c", 1)
     weight_p = shift(student_weight, "c", 1)
     scales_p = shift(teacher_scales, "c", 1)
     quarter, codes_p, weight_p, scales_p = lax.optimization_barrier(
         (quarter, codes_p, weight_p, scales_p)
     )
-    quarters = [quarter, *(shift(quarter, "x", k) for k in range(1, n_x))]
+    opposite = to_all(quarter, "x").reshape(tok, -1)
     table = dequantize(teacher_codes, codes_p, teacher_scales, scales_p)
-    turned = turned_over(student_weight, weight_p)
 
     tables = (table, student_weight, weight_p)
-    t0, s0, stats0, students0 = logits_of(place, [hidden, *quarters], *tables)
-    after, before, stats0, turned = lax.optimization_barrier((after, before, stats0, turned))
+    place = jnp.stack([y, jnp.zeros_like(y)]).astype(jnp.int32)
+    t0, s0, stats0, students0 = logits_of(place, [hidden], *tables)
     students0_p = shift(students0, "c", 1)
+    rows = [y, jnp.zeros_like(y)]
+    for k in (1, 2):
+        rows += [k * tok + odd * share, k * tok + (1 - odd) * share, y * 0 + k * tok + 2 * share]
+    pieces, stats0 = lax.optimization_barrier(([opposite, *blocks[0], *blocks[1]], stats0))
     t1, s1, _, students1, mine = logits_of(
-        place,
-        [after, before],
+        jnp.stack(rows).astype(jnp.int32),
+        pieces,
         *tables,
         first_stats=stats0,
         scale=loss_scale.astype(F32)[None],
         copies=n_x * n_y,
     )
+    mine, weight_own, weight_other = lax.optimization_barrier((mine, student_weight, weight_p))
+    turned = turned_over(weight_own, weight_other)
     seen = lax.all_to_all(mine, ("x", "y"), 0, 0, tiled=True)
     scales = jnp.sum(seen[:n_y, 5], axis=0)
     totals = combine(to_all(combine(seen), "z"))

time: 168 us -> 181 us (1.077)
  waiting for transfers between devices: 55 us -> 39.8 us
  Pallas kernels: 55.5 us -> 66.2 us
  starting transfers between devices: 28.8 us -> 36.5 us
  other arithmetic: 4.22 us -> 9.68 us
    pallas_call x2, Pallas kernels: 22.4 us -> 31 us  [logits_of(): pl.pallas_call(functools.partial(logits_kernel, steps, len(pieces)), grid...]
    all_to_all x1 -> x2, waiting for transfers between devices: 9.05 us -> 2.45 us  [to_all(): lax.all_to_all(jnp.broadcast_to(a[None], (n, *a.shape)), axes, 0, 0, tile...]
    concatenate x1 -> x4, other arithmetic: 0.02 us -> 4.44 us  [packed(): return jnp.concatenate(cut, axis=1)]
    ppermute x12 -> x11, waiting for transfers between devices: 9.42 us -> 5.26 us  [shift(): return lax.ppermute(a, axis, [((i + by) % n, i) for i in range(n)])]
    all_to_all x1 -> x2, starting transfers between devices: 8.29 us -> 12.4 us  [to_all(): lax.all_to_all(jnp.broadcast_to(a[None], (n, *a.shape)), axes, 0, 0, tile...]
    all_to_all x1, waiting for transfers between devices: 31.5 us -> 27.5 us  [local(): got = lax.all_to_all(blocks, ('x', 'y'), 0, 0, tiled=True)]
    pallas_call x1, Pallas kernels: 9.24 us -> 13 us  [dequantize(): pl.pallas_call(functools.partial(dequant_kernel, steps), grid=(2 * steps,...]
    all_to_all x1, starting transfers between devices: 3.38 us -> 6.55 us  [local(): got = lax.all_to_all(got, 'z', 0, 0, tiled=True)]
  transfers between devices with their start and end apart: 16 -> 18, of which waited for: 8 -> 6; matrix products, arithmetic and copies ran while one was open for 5% -> 9% of each run, Pallas kernels for 21% -> 22%
where the time goes in v8:
time: 181 us; the launch traced here: 179 us
  Pallas kernels  66.2 us (37%)
  waiting for transfers between devices  39.8 us (22%)
  starting transfers between devices  36.5 us (20%)
  blocking collectives  13.6 us (8%)
  local copies, waits for them, and re-layouts  12.2 us (7%)
  other arithmetic  9.68 us (5%)
    pallas_call x2, Pallas kernels, logits_of(): pl.pallas_call(functools.partial(logits_kernel, steps, len(pieces)), grid...  31 us
    all_to_all x1, waiting for transfers between devices, local(): got = lax.all_to_all(blocks, ('x', 'y'), 0, 0, tiled=True)  27.5 us
    all_to_all x1, blocking collectives, local(): seen = lax.all_to_all(mine, ('x', 'y'), 0, 0, tiled=True)  13.6 us
    pallas_call x1, Pallas kernels, dequantize(): pl.pallas_call(functools.partial(dequant_kernel, steps), grid=(2 * steps,...  13 us
    all_to_all x2, starting transfers between devices, to_all(): lax.all_to_all(jnp.broadcast_to(a[None], (n, *a.shape)), axes, 0, 0, tile...  12.4 us
    pallas_call x1, Pallas kernels, gradients(): pl.pallas_call(grad_kernel, grid_spec=pltpu.PrefetchScalarGridSpec(num_sc...  9.09 us
    ppermute x11, starting transfers between devices, shift(): return lax.ppermute(a, axis, [((i + by) % n, i) for i in range(n)])  8.35 us
    pallas_call x1, Pallas kernels, weight_gradient(): pl.pallas_call(weight_kernel, grid=(width // WEIGHT_COLUMNS,), in_specs=[...  8.29 us
  transfers between devices with their start and end apart: 18, of which 6 were waited for; matrix products, arithmetic and copies ran while one was open for 9% of the time, Pallas kernels for 22%

profile of v8, /device:TPU:8, one launch (start us, length us, event | category | flops | bytes accessed | tf_op | source)
XLA Modules:
  0.0 178.9 jit_solution(7532725161182414189)
XLA Ops:
  2.6 2.4 %collective-permute-start = (bf16[16,7936]{1,0:T(8,128)(2,1)S(1)}, bf16[16,7936]{1,0:T(8,128)(2,1)}, u32[]{:S(2)}, u32[]{:S(2)}) collective-permute-start(bf16[16,7936]{1,0:T(8,128)(2,1)S(1)} %pad_maximum_fusion.3), channel_id=1, source_target_pairs={{4,0},{6,2},{0,4},{2,6},{5,1},{7,3},{1,5},{3,7},{12,8},{14,10},{8,... | collective-permute-start | bytes 761864 | tf_op jit(solution)/shard_map/ppermute | solution.py:20
  8.0 4.9 %collective-permute-done = bf16[16,7936]{1,0:T(8,128)(2,1)} collective-permute-done((bf16[16,7936]{1,0:T(8,128)(2,1)S(1)}, bf16[16,7936]{1,0:T(8,128)(2,1)}, u32[]{:S(2)}, u32[]{:S(2)}) %collective-permute-start) | collective-permute-done | bytes 253984 | tf_op jit(solution)/shard_map/ppermute | solution.py:20
  12.8 1.9 %collective-permute-start.1 = (bf16[16,7936]{1,0:T(8,128)(2,1)}, bf16[16,7936]{1,0:T(8,128)(2,1)}, u32[]{:S(2)}, u32[]{:S(2)}) collective-permute-start(bf16[16,7936]{1,0:T(8,128)(2,1)} %collective-permute-done), channel_id=1, source_target_pairs={{0,8},{8,0},{16,24},{24,16},{32,40},{40,32},{48,56},{56,48},{1,9},... | collective-permute-start | bytes 761864 | tf_op jit(solution)/shard_map/ppermute | solution.py:383
  17.1 3.9 %collective-permute-done.1 = bf16[16,7936]{1,0:T(8,128)(2,1)} collective-permute-done((bf16[16,7936]{1,0:T(8,128)(2,1)}, bf16[16,7936]{1,0:T(8,128)(2,1)}, u32[]{:S(2)}, u32[]{:S(2)}) %collective-permute-start.1) | collective-permute-done | bytes 253984 | tf_op jit(solution)/shard_map/ppermute | solution.py:383
  21.0 1.6 collective-permute-start.6
  24.1 1.5 broadcast_in_dim.10
  26.2 4.4 %all-to-all-start = ((bf16[4,32,7936]{2,1,0:T(8,128)(2,1)}), bf16[4,32,7936]{2,1,0:T(8,128)(2,1)}, u32[]{:S(2)}, u32[]{:S(2)}) async-start(bf16[4,32,7936]{2,1,0:T(8,128)(2,1)} %broadcast_in_dim.10), calls=%async_computation | async-start | bytes 4063232 | tf_op jit(solution)/shard_map/all_to_all | solution.py:319
  30.7 2.1 %pad_maximum_fusion.1 = bf16[64,7936]{1,0:T(8,128)(2,1)} fusion(bf16[64,2560]{1,0:T(8,128)(2,1)} %dynamic_slice.26, bf16[64,5376]{1,0:T(8,128)(2,1)S(1)} %slice-done), kind=kLoop, calls=%fused_computation.1 | loop fusion | flops 2031616 | bytes 2031616 | tf_op jit(solution)/shard_map/concatenate | solution.py:380
  33.9 1.5 collective-permute-start.10
  36.9 1.5 pad_maximum_fusion.rest_0_
  38.9 1.5 collective-permute-start.9
  41.5 13.0 %dequantize.1.rest_1_.rest_7_ = bf16[1024,5376]{1,0:T(8,128)(2,1)} custom-call(bf16[512,5376]{1,0:T(8,128)(2,1)} %own_ref.1, bf16[512,5376]{1,0:T(8,128)(2,1)} %collective-permute-done.2.other_ref, f32[512,42]{1,0:T(8,128)} %copy-done.6, f32[512,42]{1,0:T(8,128)} %collective-permute-done.4.other_scale_ref), custom_call_target="tpu_custom_call" | custom-call | flops 5505024 | bytes 22020096 | tf_op jit(solution)/shard_map/dequantize/pallas_call | solution.py:58
  54.4 12.6 %logits.2 = (f32[1024,128]{1,0:T(8,128)}, f32[1024,128]{1,0:T(8,128)}, f32[8,128]{1,0:T(8,128)}, bf16[128,2560]{1,0:T(8,128)(2,1)}) custom-call(s32[2]{0:T(128)} %pad_add_fusion.place_ref.y_ref, bf16[128,7936]{1,0:T(8,128)(2,1)} %pad_maximum_fusion.rest_0_, bf16[1024,5376]{1,0:T(8,128)(2,1)} %dequantize.1.rest_1_.rest_7_, bf16[512,2560]{1,0:T(8,128)(2,1)} %own_ref.2, ...), custom_call_target="tpu_custom_call" | custom-call | flops 2080374784 | bytes 19333120 | tf_op jit(solution)/shard_map/logits/pallas_call | solution.py:238
  67.8 18.5 %logits.3 = (f32[1024,384]{1,0:T(8,128)}, f32[1024,384]{1,0:T(8,128)}, f32[8,384]{1,0:T(8,128)}, bf16[384,2560]{1,0:T(8,128)(2,1)}, f32[16,8,512]{2,1,0:T(8,128)}) custom-call(s32[8]{0:T(128)} %stack.51.place_ref, bf16[128,7936]{1,0:T(8,128)(2,1)} %bitcast.5.rest_0_, bf16[32,7936]{1,0:T(8,128)(2,1)} %collective-permute-done.5.rest_1_, ...), custom_call_target="tpu_custom_call" | custom-call | flops 6241124352 | bytes 25493504 | tf_op jit(solution)/shard_map/logits/pallas_call | solution.py:238
  86.3 13.6 %all_to_all.25 = f32[16,8,512]{2,1,0:T(8,128)S(1)} all-to-all(f32[16,8,512]{2,1,0:T(8,128)} %get-tuple-element.53), channel_id=1, replica_groups=mesh['x'=4,'z'=8,'y'=4,'c'=2] {'x','y'}, dimensions={0} | all-to-all | bytes 524288 | tf_op jit(solution)/shard_map/all_to_all | solution.py:426
  100.8 8.0 %all-to-all-start.2 = ((f32[8,5,512]{2,1,0:T(8,128)}), f32[8,5,512]{2,1,0:T(8,128)S(1)}, u32[]{:S(2)}, u32[]{:S(2)}) async-start(f32[8,5,512]{2,1,0:T(8,128)} %broadcast_in_dim.13), calls=%async_computation.2 | async-start | bytes 262144 | tf_op jit(solution)/shard_map/all_to_all | solution.py:319
  108.8 1.7 copy-done.2
  110.5 4.9 %turn.1.turned_ref = bf16[2560,1024]{1,0:T(8,128)(2,1)} custom-call(bf16[512,2560]{1,0:T(8,128)(2,1)S(1)} %copy-done, bf16[512,2560]{1,0:T(8,128)(2,1)S(1)} %copy-done.2), custom_call_target="tpu_custom_call" | custom-call | bytes 10485760 | tf_op jit(solution)/shard_map/turn/pallas_call | solution.py:90
  115.4 2.5 %all-to-all-done.2 = f32[8,5,512]{2,1,0:T(8,128)S(1)} async-done(((f32[8,5,512]{2,1,0:T(8,128)}), f32[8,5,512]{2,1,0:T(8,128)S(1)}, u32[]{:S(2)}, u32[]{:S(2)}) %all-to-all-start.2) | async-done | bytes 81952 | tf_op jit(solution)/shard_map/all_to_all | solution.py:319
  118.7 9.1 %gradients.1 = (bf16[512,512]{1,0:T(8,128)(2,1)}, bf16[512,512]{1,0:T(8,128)(2,1)}, bf16[4,4,640,128]{3,2,1,0:T(8,128)(2,1)}) custom-call(s32[2]{0:T(128)} %pad_add_fusion.place_ref.y_ref, f32[8,512]{1,0:T(8,128)} %pad_maximum_fusion.4.rows_ref, f32[1024,128]{1,0:T(8,128)} %get-tuple-element.54.t0, f32[1024,128]{1,0:T(8,128)} %get-tuple-element.55.s0, ...), custom_call_target="tpu_custom_call" | custom-call | flops 2684354560 | bytes 13107200 | tf_op jit(solution)/shard_map/gradients/pallas_call | solution.py:291
  127.8 5.3 %all-to-all-start.3 = ((bf16[16,640,128]{2,1,0:T(8,128)(2,1)}), bf16[16,640,128]{2,1,0:T(8,128)(2,1)S(1)}, u32[]{:S(2)}, u32[]{:S(2)}) async-start(bf16[16,640,128]{2,1,0:T(8,128)(2,1)} %bitcast.87), calls=%async_computation.3 | async-start | bytes 5242880 | tf_op jit(solution)/shard_map/all_to_all | solution.py:451
  133.7 27.5 %all-to-all-done.3 = bf16[16,640,128]{2,1,0:T(8,128)(2,1)S(1)} async-done(((bf16[16,640,128]{2,1,0:T(8,128)(2,1)}), bf16[16,640,128]{2,1,0:T(8,128)(2,1)S(1)}, u32[]{:S(2)}, u32[]{:S(2)}) %all-to-all-start.3) | async-done | bytes 2621472 | tf_op jit(solution)/shard_map/all_to_all | solution.py:451
  162.3 6.5 %all-to-all-start.4 = ((bf16[8,80,128]{2,1,0:T(8,128)(2,1)}), bf16[8,80,128]{2,1,0:T(8,128)(2,1)S(1)}, u32[]{:S(2)}, u32[]{:S(2)}) async-start(bf16[8,80,128]{2,1,0:T(8,128)(2,1)} %bitcast.24), calls=%async_computation.4 | async-start | bytes 327680 | tf_op jit(solution)/shard_map/all_to_all | solution.py:453
  169.4 8.3 %weight_gradient.1 = bf16[512,2560]{1,0:T(8,128)(2,1)} custom-call(bf16[512,512]{1,0:T(8,128)(2,1)} %get-tuple-element.61.own_ref, bf16[512,512]{1,0:T(8,128)(2,1)} %collective-permute-done.11.from_ref, bf16[128,2560]{1,0:T(8,128)(2,1)} %get-tuple-element.63.s0_ref, bf16[384,2560]{1,0:T(8,128)(2,1)} %get-tuple-element.64.s1_ref, ...), custom_call_target="tpu_custom_call" | custom-call | flops 2684354560 | bytes 8912896 | tf_op jit(solution)/shard_map/weight_gradient/pallas_call | solution.py:351
  (76 shorter events, 19.4 us)
Async XLA Ops:
  0.6 23.5 %collective-permute-start.2 = (bf16[512,5376]{1,0:T(8,128)(2,1)}, bf16[512,5376]{1,0:T(8,128)(2,1)}, u32[]{:S(2)}, u32[]{:S(2)}) collective-permute-start(bf16[512,5376]{1,0:T(8,128)(2,1)} %own_ref.1), channel_id=1, source_target_pairs={{1,0},{0,1},{3,2},{2,3},{5,4},{4,5},{7,6},{6,7},{9,8},{8,9},{11,10... | collective-permute-start | bytes 16515080 | tf_op jit(solution)/shard_map/ppermute | solution.py:20
  2.6 13.3 %copy-start.4 = (bf16[128,2560]{1,0:T(8,128)(2,1)S(1)}, bf16[128,2560]{1,0:T(8,128)(2,1)}, u32[]{:S(2)}) copy-start(bf16[128,2560]{1,0:T(8,128)(2,1)} %param.7) | copy-start | bytes 1966084
  2.6 10.2 %collective-permute-start = (bf16[16,7936]{1,0:T(8,128)(2,1)S(1)}, bf16[16,7936]{1,0:T(8,128)(2,1)}, u32[]{:S(2)}, u32[]{:S(2)}) collective-permute-start(bf16[16,7936]{1,0:T(8,128)(2,1)S(1)} %pad_maximum_fusion.3), channel_id=1, source_target_pairs={{4,0},{6,2},{0,4},{2,6},{5,1},{7,3},{1,5},{3,7},{12,8},{14,10},{8,... | collective-permute-start | bytes 761864 | tf_op jit(solution)/shard_map/ppermute | solution.py:20
  5.0 19.1 %collective-permute-start.3 = (bf16[512,2560]{1,0:T(8,128)(2,1)}, bf16[512,2560]{1,0:T(8,128)(2,1)S(1)}, u32[]{:S(2)}, u32[]{:S(2)}) collective-permute-start(bf16[512,2560]{1,0:T(8,128)(2,1)} %own_ref.2), channel_id=1, source_target_pairs={{1,0},{0,1},{3,2},{2,3},{5,4},{4,5},{7,6},{6,7},{9,8},{8,9},{11,10... | collective-permute-start | bytes 7864328 | tf_op jit(solution)/shard_map/ppermute | solution.py:20
  12.8 8.2 %collective-permute-start.1 = (bf16[16,7936]{1,0:T(8,128)(2,1)}, bf16[16,7936]{1,0:T(8,128)(2,1)}, u32[]{:S(2)}, u32[]{:S(2)}) collective-permute-start(bf16[16,7936]{1,0:T(8,128)(2,1)} %collective-permute-done), channel_id=1, source_target_pairs={{0,8},{8,0},{16,24},{24,16},{32,40},{40,32},{48,56},{56,48},{1,9},... | collective-permute-start | bytes 761864 | tf_op jit(solution)/shard_map/ppermute | solution.py:383
  15.8 8.3 %copy-start.6 = (f32[512,42]{1,0:T(8,128)}, f32[512,42]{1,0:T(8,128)S(1)}, u32[]{:S(2)}) copy-start(f32[512,42]{1,0:T(8,128)S(1)} %copy.22.own_scale_ref) | copy-start | bytes 258052
  15.8 8.3 %collective-permute-start.4 = (f32[512,42]{1,0:T(8,128)S(1)}, f32[512,42]{1,0:T(8,128)}, u32[]{:S(2)}, u32[]{:S(2)}) collective-permute-start(f32[512,42]{1,0:T(8,128)S(1)} %copy.22.own_scale_ref), channel_id=1, source_target_pairs={{1,0},{0,1},{3,2},{2,3},{5,4},{4,5},{7,6},{6,7},{9,8},{8,9},{11,10... | collective-permute-start | bytes 258056 | tf_op jit(solution)/shard_map/ppermute | solution.py:20
  16.7 16.9 %collective-permute-start.5 = (bf16[32,7936]{1,0:T(8,128)(2,1)}, bf16[32,7936]{1,0:T(8,128)(2,1)}, u32[]{:S(2)}, u32[]{:S(2)}) collective-permute-start(bf16[32,7936]{1,0:T(8,128)(2,1)} %pad_maximum_fusion.2), channel_id=1, source_target_pairs={{2,0},{4,2},{6,4},{0,6},{3,1},{5,3},{7,5},{1,7},{10,8},{12,10},{14... | collective-permute-start | bytes 1523720 | tf_op jit(solution)/shard_map/ppermute | solution.py:20
  21.0 12.9 %collective-permute-start.6 = (bf16[32,7936]{1,0:T(8,128)(2,1)}, bf16[32,7936]{1,0:T(8,128)(2,1)}, u32[]{:S(2)}, u32[]{:S(2)}) collective-permute-start(bf16[32,7936]{1,0:T(8,128)(2,1)} %pad_maximum_fusion.2), channel_id=1, source_target_pairs={{6,0},{0,2},{2,4},{4,6},{7,1},{1,3},{3,5},{5,7},{14,8},{8,10},{10,... | collective-permute-start | bytes 1523720 | tf_op jit(solution)/shard_map/ppermute | solution.py:20
  26.2 40.8 %all-to-all-start = ((bf16[4,32,7936]{2,1,0:T(8,128)(2,1)}), bf16[4,32,7936]{2,1,0:T(8,128)(2,1)}, u32[]{:S(2)}, u32[]{:S(2)}) async-start(bf16[4,32,7936]{2,1,0:T(8,128)(2,1)} %broadcast_in_dim.10), calls=%async_computation | async-start | bytes 4063232 | tf_op jit(solution)/shard_map/all_to_all | solution.py:319
  30.7 6.2 %copy-start.3 = (bf16[128,5376]{1,0:T(8,128)(2,1)S(1)}, bf16[128,5376]{1,0:T(8,128)(2,1)}, u32[]{:S(2)}) copy-start(bf16[128,5376]{1,0:T(8,128)(2,1)} %param.6) | copy-start | bytes 4128772
  30.7 6.2 %copy-start.5 = (bf16[128,2560]{1,0:T(8,128)(2,1)S(1)}, bf16[128,2560]{1,0:T(8,128)(2,1)}, u32[]{:S(2)}) copy-start(bf16[128,2560]{1,0:T(8,128)(2,1)} %param.7) | copy-start | bytes 1966084
  33.5 7.4 %copy-start.9 = (bf16[128]{0:T(256)(128)(2,1)S(1)}, bf16[128]{0:T(256)(128)(2,1)}, u32[]{:S(2)}) copy-start(bf16[128]{0:T(256)(128)(2,1)} %param.11) | copy-start | bytes 772
  33.9 33.1 %collective-permute-start.10 = (bf16[64,7936]{1,0:T(8,128)(2,1)}, bf16[64,7936]{1,0:T(8,128)(2,1)}, u32[]{:S(2)}, u32[]{:S(2)}) collective-permute-start(bf16[64,7936]{1,0:T(8,128)(2,1)} %pad_maximum_fusion.1), channel_id=1, source_target_pairs={{6,0},{0,2},{2,4},{4,6},{7,1},{1,3},{3,5},{5,7},{14,8},{8,10},{10,... | collective-permute-start | bytes 3047432 | tf_op jit(solution)/shard_map/ppermute | solution.py:20
  35.4 31.6 %collective-permute-start.8 = (bf16[64,7936]{1,0:T(8,128)(2,1)}, bf16[64,7936]{1,0:T(8,128)(2,1)}, u32[]{:S(2)}, u32[]{:S(2)}) collective-permute-start(bf16[64,7936]{1,0:T(8,128)(2,1)} %pad_maximum_fusion.1), channel_id=1, source_target_pairs={{2,0},{4,2},{6,4},{0,6},{3,1},{5,3},{7,5},{1,7},{10,8},{12,10},{14... | collective-permute-start | bytes 3047432 | tf_op jit(solution)/shard_map/ppermute | solution.py:20
  38.3 28.7 %collective-permute-start.7 = (bf16[32,7936]{1,0:T(8,128)(2,1)}, bf16[32,7936]{1,0:T(8,128)(2,1)S(1)}, u32[]{:S(2)}, u32[]{:S(2)}) collective-permute-start(bf16[32,7936]{1,0:T(8,128)(2,1)} %collective-permute-done.5.rest_1_), channel_id=1, source_target_pairs={{0,8},{8,0},{16,24},{24,16},{32,40},{40,32},{48,56},{56,48},{1,9},... | collective-permute-start | bytes 1523720 | tf_op jit(solution)/shard_map/ppermute | solution.py:383
  38.9 28.1 %collective-permute-start.9 = (bf16[32,7936]{1,0:T(8,128)(2,1)}, bf16[32,7936]{1,0:T(8,128)(2,1)}, u32[]{:S(2)}, u32[]{:S(2)}) collective-permute-start(bf16[32,7936]{1,0:T(8,128)(2,1)} %collective-permute-done.6.rest_4_), channel_id=1, source_target_pairs={{0,8},{8,0},{16,24},{24,16},{32,40},{40,32},{48,56},{56,48},{1,9},... | collective-permute-start | bytes 1523720 | tf_op jit(solution)/shard_map/ppermute | solution.py:383
  67.8 40.9 %copy-start = (bf16[512,2560]{1,0:T(8,128)(2,1)S(1)}, bf16[512,2560]{1,0:T(8,128)(2,1)}, u32[]{:S(2)}) copy-start(bf16[512,2560]{1,0:T(8,128)(2,1)} %own_ref.2) | copy-start | bytes 7864324
  100.8 17.0 %all-to-all-start.2 = ((f32[8,5,512]{2,1,0:T(8,128)}), f32[8,5,512]{2,1,0:T(8,128)S(1)}, u32[]{:S(2)}, u32[]{:S(2)}) async-start(f32[8,5,512]{2,1,0:T(8,128)} %broadcast_in_dim.13), calls=%async_computation.2 | async-start | bytes 262144 | tf_op jit(solution)/shard_map/all_to_all | solution.py:319
  127.8 33.5 %all-to-all-start.3 = ((bf16[16,640,128]{2,1,0:T(8,128)(2,1)}), bf16[16,640,128]{2,1,0:T(8,128)(2,1)S(1)}, u32[]{:S(2)}, u32[]{:S(2)}) async-start(bf16[16,640,128]{2,1,0:T(8,128)(2,1)} %bitcast.87), calls=%async_computation.3 | async-start | bytes 5242880 | tf_op jit(solution)/shard_map/all_to_all | solution.py:451
  133.1 36.3 %collective-permute-start.13 = (bf16[384,2560]{1,0:T(8,128)(2,1)}, bf16[384,2560]{1,0:T(8,128)(2,1)}, u32[]{:S(2)}, u32[]{:S(2)}) collective-permute-start(bf16[384,2560]{1,0:T(8,128)(2,1)} %get-tuple-element.64.s1_ref), channel_id=1, source_target_pairs={{1,0},{0,1},{3,2},{2,3},{5,4},{4,5},{7,6},{6,7},{9,8},{8,9},{11,10... | collective-permute-start | bytes 5898248 | tf_op jit(solution)/shard_map/ppermute | solution.py:20
  133.1 36.3 %collective-permute-start.12 = (bf16[128,2560]{1,0:T(8,128)(2,1)S(1)}, bf16[128,2560]{1,0:T(8,128)(2,1)}, u32[]{:S(2)}, u32[]{:S(2)}) collective-permute-start(bf16[128,2560]{1,0:T(8,128)(2,1)S(1)} %copy-done.7), channel_id=1, source_target_pairs={{1,0},{0,1},{3,2},{2,3},{5,4},{4,5},{7,6},{6,7},{9,8},{8,9},{11,10... | collective-permute-start | bytes 1966088 | tf_op jit(solution)/shard_map/ppermute | solution.py:20
  133.6 35.8 %collective-permute-start.11 = (bf16[512,512]{1,0:T(8,128)(2,1)}, bf16[512,512]{1,0:T(8,128)(2,1)}, u32[]{:S(2)}, u32[]{:S(2)}) collective-permute-start(bf16[512,512]{1,0:T(8,128)(2,1)} %get-tuple-element.62), channel_id=1, source_target_pairs={{1,0},{0,1},{3,2},{2,3},{5,4},{4,5},{7,6},{6,7},{9,8},{8,9},{11,10... | collective-permute-start | bytes 1572872 | tf_op jit(solution)/shard_map/ppermute | solution.py:20
  162.3 16.0 %all-to-all-start.4 = ((bf16[8,80,128]{2,1,0:T(8,128)(2,1)}), bf16[8,80,128]{2,1,0:T(8,128)(2,1)S(1)}, u32[]{:S(2)}, u32[]{:S(2)}) async-start(bf16[8,80,128]{2,1,0:T(8,128)(2,1)} %bitcast.24), calls=%async_computation.4 | async-start | bytes 327680 | tf_op jit(solution)/shard_map/all_to_all | solution.py:453
  (5 other events, 15.1 us)

commit v9 on v7

--- a/solution.py
+++ b/solution.py
@@ -27,6 +27,7 @@
 
 NT = (((1,), (1,)), ((), ()))
 MIB = 1024 * 1024
+VMEM_LOGITS = 18 * MIB
 DEQUANT_ROWS = 128
 LOGIT_ROWS = 256
 WEIGHT_COLUMNS = 512
@@ -108,42 +109,25 @@
     )(own, other)
 
 
-def logits_tile(pair, table_ref, weight_ref, t_ref, s_ref, stat_ref):
-    step = pl.program_id(0)
-    width_t = table_ref.shape[1]
-    t = lax.dot_general(table_ref[...], pair[:, :width_t], NT, preferred_element_type=F32)
-    s = lax.dot_general(weight_ref[...], pair[:, width_t:], NT, preferred_element_type=F32)
-    t_ref[...] = t
-    s_ref[...] = s
+def update_stats(first, t, s, stat_ref):
     t_top = jnp.max(t, axis=0, keepdims=True)
     s_top = jnp.max(s, axis=0, keepdims=True)
-
-    def sums(t_top, s_top):
-        e = jnp.exp(t - t_top)
-        return (
-            jnp.sum(e, axis=0, keepdims=True),
-            jnp.sum(e * (t - s), axis=0, keepdims=True),
-            jnp.sum(jnp.exp(s - s_top), axis=0, keepdims=True),
-        )
-
-    @pl.when(step == 0)
-    def _():
-        total, cross, s_total = sums(t_top, s_top)
-        for k, row in enumerate((t_top, total, cross, s_top, s_total)):
-            stat_ref[k : k + 1] = row
+    if not first:
+        t_old, s_old = stat_ref[0:1], stat_ref[3:4]
+        t_top, s_top = jnp.maximum(t_old, t_top), jnp.maximum(s_old, s_top)
+    e = jnp.exp(t - t_top)
+    total = jnp.sum(e, axis=0, keepdims=True)
+    cross = jnp.sum(e * (t - s), axis=0, keepdims=True)
+    s_total = jnp.sum(jnp.exp(s - s_top), axis=0, keepdims=True)
+    if first:
         stat_ref[5:8] = jnp.zeros((3, t.shape[1]), F32)
-
-    @pl.when(step > 0)
-    def _():
-        t_old, s_old = stat_ref[0:1], stat_ref[3:4]
-        t_new, s_new = jnp.maximum(t_old, t_top), jnp.maximum(s_old, s_top)
-        total, cross, s_total = sums(t_new, s_new)
-        t_keep, s_keep = jnp.exp(t_old - t_new), jnp.exp(s_old - s_new)
-        stat_ref[0:1] = t_new
-        stat_ref[1:2] = stat_ref[1:2] * t_keep + total
-        stat_ref[2:3] = stat_ref[2:3] * t_keep + cross
-        stat_ref[3:4] = s_new
-        stat_ref[4:5] = stat_ref[4:5] * s_keep + s_total
+    else:
+        t_keep, s_keep = jnp.exp(t_old - t_top), jnp.exp(s_old - s_top)
+        total += stat_ref[1:2] * t_keep
+        cross += stat_ref[2:3] * t_keep
+        s_total += stat_ref[4:5] * s_keep
+    for k, row in enumerate((t_top, total, cross, s_top, s_total)):
+        stat_ref[k : k + 1] = row
 
 
 def load_pair(x_ref, refs, pair, sem):
@@ -158,50 +142,68 @@
         copy.wait()
 
 
-def logits_kernel(steps, n_pieces, place_ref, *rest):
+def logits_kernel(n_pieces, place_ref, *rest):
     pieces_hbm, rest = rest[:n_pieces], rest[n_pieces:]
     (table_ref, weight_ref, weight_p_ref), rest = rest[:3], rest[3:]
     tok = pieces_hbm[0].shape[0]
-    spread = len(rest) > 6
+    spread = len(rest) > 9
     first_stat_ref, scale_ref = rest[:2] if spread else (None, None)
     rest = rest[2:] if spread else rest
-    t_ref, s_ref, stat_ref, student_ref = rest[:4]
+    t_hbm, s_hbm, stat_ref, student_hbm = rest[:4]
     spread_ref = rest[4] if spread else None
-    pair, sem = rest[-2:]
-    step = pl.program_id(0)
-
-    @pl.when(step == 0)
-    def _():
-        load_pair(place_ref, pieces_hbm, pair, sem)
-        student_ref[...] = pair[:, table_ref.shape[1] :]
-
-    @pl.when(step < steps)
-    def _():
-        logits_tile(pair, table_ref, weight_ref, t_ref, s_ref, stat_ref)
-
-    @pl.when(step >= steps)
-    def _():
-        logits_tile(pair, table_ref, weight_p_ref, t_ref, s_ref, stat_ref)
+    pair, t_buf, s_buf, load_sem, out_sem = rest[-5:]
+    width_t = table_ref.shape[1]
+    rows = weight_ref.shape[0]
+
+    load_pair(place_ref, pieces_hbm, pair, load_sem)
+    students = pltpu.make_async_copy(pair.at[:, pl.ds(width_t, weight_ref.shape[1])], student_hbm, out_sem.at[2, 0])
+    students.start()
+    waiting = []
+    for i in range(2 * rows // LOGIT_ROWS):
+        slot, at = i % 2, i * LOGIT_ROWS
+        source, low = (weight_ref, at) if at < rows else (weight_p_ref, at - rows)
+        t = lax.dot_general(
+            table_ref[at : at + LOGIT_ROWS], pair[:, :width_t], NT, preferred_element_type=F32
+        )
+        s = lax.dot_general(
+            source[low : low + LOGIT_ROWS], pair[:, width_t:], NT, preferred_element_type=F32
+        )
+        if i >= 2:
+            for copy in waiting[i - 2]:
+                copy.wait()
+        t_buf[slot] = t
+        s_buf[slot] = s
+        copies = [
+            pltpu.make_async_copy(
+                buf.at[slot], hbm.at[pl.ds(at, LOGIT_ROWS)], out_sem.at[k, slot]
+            )
+            for k, (buf, hbm) in enumerate(((t_buf, t_hbm), (s_buf, s_hbm)))
+        ]
+        for copy in copies:
+            copy.start()
+        waiting.append(copies)
+        update_stats(i == 0, t, s, stat_ref)
 
     if spread:
-
-        @pl.when(step == 2 * steps - 1)
-        def _():
-            copies, _, wide = spread_ref.shape
-            n_y = wide // tok
-            row = lax.broadcasted_iota(jnp.int32, (8, tok), 0)
-            scale = jnp.broadcast_to(scale_ref[...], (8, tok))
-            first, last = first_stat_ref[...], stat_ref[...]
-            pieces = (
-                jnp.where(row == 5, scale, first[:, :tok]),
-                last[:, :tok],
-                first[:, tok:],
-                last[:, tok:],
-            )
-            for r, piece in enumerate(pieces):
-                at = pl.multiple_of(lax.rem(place_ref[0] + r, n_y) * tok, tok)
-                for k in range(copies):
-                    spread_ref[k, :, pl.ds(at, tok)] = piece
+        copies, _, wide = spread_ref.shape
+        n_y = wide // tok
+        row = lax.broadcasted_iota(jnp.int32, (8, tok), 0)
+        scale = jnp.broadcast_to(scale_ref[...], (8, tok))
+        first, last = first_stat_ref[...], stat_ref[...]
+        pieces = (
+            jnp.where(row == 5, scale, first[:, :tok]),
+            last[:, :tok],
+            first[:, tok:],
+            last[:, tok:],
+        )
+        for r, piece in enumerate(pieces):
+            at = pl.multiple_of(lax.rem(place_ref[0] + r, n_y) * tok, tok)
+            for k in range(copies):
+                spread_ref[k, :, pl.ds(at, tok)] = piece
+    for copies in waiting[-2:]:
+        for copy in copies:
+            copy.wait()
+    students.wait()
 
 
 def logits_of(place, pieces, table, weight, weight_p, first_stats=None, scale=None, copies=0):
@@ -209,55 +211,35 @@
     rows, width_s = weight.shape
     tok = pieces[0].shape[0]
     tokens = 2 * tok
-    steps = rows // LOGIT_ROWS
+    anywhere, on_chip = pl.BlockSpec(memory_space=pl.ANY), pl.BlockSpec(memory_space=pltpu.VMEM)
+    in_specs = [pl.BlockSpec(memory_space=pltpu.SMEM)]
+    in_specs += [anywhere] * len(pieces) + [on_chip] * 3
+    out_specs = [anywhere, anywhere, on_chip, anywhere]
     tile = pltpu.HBM((2 * rows, tokens), F32)
-
-    def source(width, k):
-        return pl.BlockSpec((LOGIT_ROWS, width), lambda i, y: two_sources(i, steps)[k])
-
-    in_specs = [
-        *[pl.BlockSpec(memory_space=pl.ANY) for _ in pieces],
-        pl.BlockSpec((LOGIT_ROWS, width_t), lambda i, y: (i, 0)),
-        source(width_s, 0),
-        source(width_s, 1),
-    ]
-    out_specs = [
-        pl.BlockSpec((LOGIT_ROWS, tokens), lambda i, y: (i, 0)),
-        pl.BlockSpec((LOGIT_ROWS, tokens), lambda i, y: (i, 0)),
-        pl.BlockSpec((8, tokens), lambda i, y: (0, 0)),
-        pl.BlockSpec((tokens, width_s), lambda i, y: (0, 0)),
-    ]
-    out_shape = [
-        tile,
-        tile,
-        jax.ShapeDtypeStruct((8, tokens), F32),
-        pltpu.HBM((tokens, width_s), BF16),
-    ]
+    out_shape = [tile, tile, jax.ShapeDtypeStruct((8, tokens), F32), pltpu.HBM((tokens, width_s), BF16)]
     operands = [place, *pieces, table, weight, weight_p]
     if first_stats is not None:
-        in_specs.append(pl.BlockSpec((8, tokens), lambda i, y: (0, 0)))
-        in_specs.append(pl.BlockSpec((1, tok), lambda i, y: (0, 0)))
+        in_specs += [on_chip, on_chip]
         operands += [first_stats, scale]
-        out_specs.append(pl.BlockSpec((copies, 8, 2 * tokens), lambda i, y: (0, 0, 0)))
+        out_specs.append(on_chip)
         out_shape.append(jax.ShapeDtypeStruct((copies, 8, 2 * tokens), F32))
     return pl.pallas_call(
-        functools.partial(logits_kernel, steps, len(pieces)),
-        grid_spec=pltpu.PrefetchScalarGridSpec(
-            num_scalar_prefetch=1,
-            grid=(2 * steps,),
-            in_specs=in_specs,
-            out_specs=out_specs,
-            scratch_shapes=[
-                pltpu.VMEM((tokens, width_t + width_s), BF16),
-                pltpu.SemaphoreType.DMA((len(pieces),)),
-            ],
-        ),
+        functools.partial(logits_kernel, len(pieces)),
+        in_specs=in_specs,
+        out_specs=out_specs,
         out_shape=out_shape,
-        compiler_params=pltpu.CompilerParams(vmem_limit_bytes=22 * MIB),
+        scratch_shapes=[
+            pltpu.VMEM((tokens, width_t + width_s), BF16),
+            pltpu.VMEM((2, LOGIT_ROWS, tokens), F32),
+            pltpu.VMEM((2, LOGIT_ROWS, tokens), F32),
+            pltpu.SemaphoreType.DMA((len(pieces),)),
+            pltpu.SemaphoreType.DMA((3, 2)),
+        ],
+        compiler_params=pltpu.CompilerParams(vmem_limit_bytes=VMEM_LOGITS),
         cost_estimate=pl.CostEstimate(
             flops=4 * rows * tokens * (width_t + width_s),
             transcendentals=4 * rows * tokens,
-            bytes_accessed=2 * (2 * rows + tokens) * (width_t + width_s) + 16 * rows * tokens,
+            bytes_accessed=2 * tokens * (width_t + 2 * width_s) + 16 * rows * tokens,
         ),
         name="logits",
     )(*operands)

time: 168 us -> 167 us (level)
  transfers between devices with their start and end apart: 16 -> 16, of which waited for: 8 -> 8; matrix products, arithmetic and copies ran while one was open for 5% -> 5% of each run, Pallas kernels for 21% -> 20%
where the time goes in v9:
time: 167 us; the launch traced here: 166 us
  waiting for transfers between devices  54.8 us (33%)
  Pallas kernels  54.2 us (32%)
  starting transfers between devices  28.4 us (17%)
  blocking collectives  13.1 us (8%)
  local copies, waits for them, and re-layouts  10.6 us (6%)
  other arithmetic  4.22 us (3%)
    all_to_all x1, waiting for transfers between devices, local(): got = lax.all_to_all(blocks, ('x', 'y'), 0, 0, tiled=True)  31.3 us
    pallas_call x2, Pallas kernels, logits_of(): pl.pallas_call(functools.partial(logits_kernel, len(pieces)), in_specs=in...  21.1 us
    all_to_all x1, blocking collectives, local(): seen = lax.all_to_all(mine, ('x', 'y'), 0, 0, tiled=True)  13.1 us
    ppermute x12, starting transfers between devices, shift(): return lax.ppermute(a, axis, [((i + by) % n, i) for i in range(n)])  10 us
    ppermute x12, waiting for transfers between devices, shift(): return lax.ppermute(a, axis, [((i + by) % n, i) for i in range(n)])  9.42 us
    pallas_call x1, Pallas kernels, dequantize(): pl.pallas_call(functools.partial(dequant_kernel, steps), grid=(2 * steps,...  9.24 us
    pallas_call x1, Pallas kernels, gradients(): pl.pallas_call(grad_kernel, grid_spec=pltpu.PrefetchScalarGridSpec(num_sc...  9.22 us
    all_to_all x1, waiting for transfers between devices, to_all(): lax.all_to_all(jnp.broadcast_to(a[None], (n, *a.shape)), axes, 0, 0, tile...  9.05 us
  transfers between devices with their start and end apart: 16, of which 8 were waited for; matrix products, arithmetic and copies ran while one was open for 5% of the time, Pallas kernels for 20%

profile of v9, /device:TPU:8, one launch (start us, length us, event | category | flops | bytes accessed | tf_op | source)
XLA Modules:
  0.0 166.2 jit_solution(7306584938315110010)
XLA Ops:
  3.1 2.4 %collective-permute-start = (bf16[16,7936]{1,0:T(8,128)(2,1)S(1)}, bf16[16,7936]{1,0:T(8,128)(2,1)}, u32[]{:S(2)}, u32[]{:S(2)}) collective-permute-start(bf16[16,7936]{1,0:T(8,128)(2,1)S(1)} %pad_maximum_fusion), channel_id=1, source_target_pairs={{4,0},{6,2},{0,4},{2,6},{5,1},{7,3},{1,5},{3,7},{12,8},{14,10},{8,... | collective-permute-start | bytes 761864 | tf_op jit(solution)/shard_map/ppermute | solution.py:20
  5.5 2.5 %constant_dynamic-update-slice_fusion.1 = bf16[128,7936]{1,0:T(8,128)(2,1)} fusion(bf16[128,5376]{1,0:T(8,128)(2,1)} %param.6), kind=kLoop, calls=%fused_computation.34 | loop fusion | bytes 2752512
  8.9 4.1 %collective-permute-done = bf16[16,7936]{1,0:T(8,128)(2,1)} collective-permute-done((bf16[16,7936]{1,0:T(8,128)(2,1)S(1)}, bf16[16,7936]{1,0:T(8,128)(2,1)}, u32[]{:S(2)}, u32[]{:S(2)}) %collective-permute-start) | collective-permute-done | bytes 253984 | tf_op jit(solution)/shard_map/ppermute | solution.py:20
  12.9 1.9 %collective-permute-start.3 = (bf16[16,7936]{1,0:T(8,128)(2,1)}, bf16[16,7936]{1,0:T(8,128)(2,1)S(1)}, u32[]{:S(2)}, u32[]{:S(2)}) collective-permute-start(bf16[16,7936]{1,0:T(8,128)(2,1)} %collective-permute-done), channel_id=1, source_target_pairs={{0,8},{8,0},{16,24},{24,16},{32,40},{40,32},{48,56},{56,48},{1,9},... | collective-permute-start | bytes 761864 | tf_op jit(solution)/shard_map/ppermute | solution.py:371
  15.3 1.6 collective-permute-start.2
  17.0 3.6 %collective-permute-done.3 = bf16[16,7936]{1,0:T(8,128)(2,1)S(1)} collective-permute-done((bf16[16,7936]{1,0:T(8,128)(2,1)}, bf16[16,7936]{1,0:T(8,128)(2,1)S(1)}, u32[]{:S(2)}, u32[]{:S(2)}) %collective-permute-start.3) | collective-permute-done | bytes 253984 | tf_op jit(solution)/shard_map/ppermute | solution.py:371
  21.3 1.4 maximum_select_fusion.rest_1_
  23.6 2.8 %collective-permute-start.7 = (bf16[32,7936]{1,0:T(8,128)(2,1)S(1)}, bf16[32,7936]{1,0:T(8,128)(2,1)}, u32[]{:S(2)}, u32[]{:S(2)}) collective-permute-start(bf16[32,7936]{1,0:T(8,128)(2,1)S(1)} %maximum_select_fusion.rest_1_), channel_id=1, source_target_pairs={{64,0},{128,64},{192,128},{0,192},{65,1},{129,65},{193,129},{1,193... | collective-permute-start | bytes 1523720 | tf_op jit(solution)/shard_map/ppermute | solution.py:20
  28.1 7.3 %turn.1.turned_ref = bf16[2560,1024]{1,0:T(8,128)(2,1)} custom-call(bf16[512,2560]{1,0:T(8,128)(2,1)S(1)} %copy-done, bf16[512,2560]{1,0:T(8,128)(2,1)} %collective-permute-done.5.rest_7_.other_ref.rest_4_), custom_call_target="tpu_custom_call" | custom-call | bytes 10485760 | tf_op jit(solution)/shard_map/turn/pallas_call | solution.py:95
  35.4 2.6 %copy-done.1 = bf16[512,5376]{1,0:T(8,128)(2,1)S(1)} copy-done((bf16[512,5376]{1,0:T(8,128)(2,1)S(1)}, bf16[512,5376]{1,0:T(8,128)(2,1)}, u32[]{:S(2)}) %copy-start.1) | copy-done | bytes 5505048
  38.0 9.2 %dequantize.1.rest_5_.rest_2_ = bf16[1024,5376]{1,0:T(8,128)(2,1)S(1)} custom-call(bf16[512,5376]{1,0:T(8,128)(2,1)S(1)} %copy-done.1, bf16[512,5376]{1,0:T(8,128)(2,1)} %collective-permute-done.4.other_ref, f32[512,42]{1,0:T(8,128)S(1)} %copy.22.own_scale_ref, f32[512,42]{1,0:T(8,128)S(1)} %copy-done.3), custom_call_target="tpu_custom_call" | custom-call | flops 5505024 | bytes 22020096 | tf_op jit(solution)/shard_map/dequantize/pallas_call | solution.py:63
  47.2 1.5 collective-permute-done.7.rest_2_
  48.7 3.8 %collective-permute-done.9.rest_4_ = bf16[32,7936]{1,0:T(8,128)(2,1)} collective-permute-done((bf16[32,7936]{1,0:T(8,128)(2,1)S(1)}, bf16[32,7936]{1,0:T(8,128)(2,1)}, u32[]{:S(2)}, u32[]{:S(2)}) %collective-permute-start.9) | collective-permute-done | bytes 507936 | tf_op jit(solution)/shard_map/ppermute | solution.py:20
  52.5 10.2 %logits.2 = (f32[1024,256]{1,0:T(8,128)}, f32[1024,256]{1,0:T(8,128)}, f32[8,256]{1,0:T(8,128)S(1)}, bf16[256,2560]{1,0:T(8,128)(2,1)}) custom-call(s32[2]{0:T(128)S(1)} %pad_add_fusion.place_ref.y_ref, bf16[128,7936]{1,0:T(8,128)(2,1)} %constant_dynamic-update-slice_fusion.rest_0_, bf16[32,7936]{1,0:T(8,128)(2,1)S(1)} %maximum_select_fusion.rest_1_, ...), custom_call_target="tpu_custom_call" | custom-call | flops 4160749568 | bytes 7471104 | tf_op jit(solution)/shard_map/logits/pallas_call | solution.py:226
  62.7 10.9 %logits.3 = (f32[1024,256]{1,0:T(8,128)}, f32[1024,256]{1,0:T(8,128)}, f32[8,256]{1,0:T(8,128)}, bf16[256,2560]{1,0:T(8,128)(2,1)}, f32[16,8,512]{2,1,0:T(8,128)S(1)}) custom-call(s32[2]{0:T(128)S(1)} %pad_add_fusion.place_ref.y_ref, bf16[128,7936]{1,0:T(8,128)(2,1)} %collective-permute-done.1.rest_0_, bf16[128,7936]{1,0:T(8,128)(2,1)} %collective-permute-done.2.rest_1_, ...), custom_call_target="tpu_custom_call" | custom-call | flops 4160749568 | bytes 7471104 | tf_op jit(solution)/shard_map/logits/pallas_call | solution.py:226
  73.6 13.1 %all_to_all.20 = f32[16,8,512]{2,1,0:T(8,128)S(1)} all-to-all(f32[16,8,512]{2,1,0:T(8,128)S(1)} %get-tuple-element.34), channel_id=1, replica_groups=mesh['x'=4,'z'=8,'y'=4,'c'=2] {'x','y'}, dimensions={0} | all-to-all | bytes 524288 | tf_op jit(solution)/shard_map/all_to_all | solution.py:398
  87.6 7.6 %all-to-all-start.1 = ((f32[8,5,512]{2,1,0:T(8,128)}), f32[8,5,512]{2,1,0:T(8,128)S(1)}, u32[]{:S(2)}, u32[]{:S(2)}) async-start(f32[8,5,512]{2,1,0:T(8,128)} %broadcast_in_dim.20), calls=%async_computation.1 | async-start | bytes 262144 | tf_op jit(solution)/shard_map/all_to_all | solution.py:305
  95.2 9.1 %all-to-all-done.1 = f32[8,5,512]{2,1,0:T(8,128)S(1)} async-done(((f32[8,5,512]{2,1,0:T(8,128)}), f32[8,5,512]{2,1,0:T(8,128)S(1)}, u32[]{:S(2)}, u32[]{:S(2)}) %all-to-all-start.1) | async-done | bytes 81952 | tf_op jit(solution)/shard_map/all_to_all | solution.py:305
  105.1 9.2 %gradients.1 = (bf16[512,512]{1,0:T(8,128)(2,1)}, bf16[512,512]{1,0:T(8,128)(2,1)}, bf16[4,4,640,128]{3,2,1,0:T(8,128)(2,1)}) custom-call(s32[2]{0:T(128)} %copy-done.4, f32[8,512]{1,0:T(8,128)} %pad_maximum_fusion.1.rows_ref, f32[1024,256]{1,0:T(8,128)} %get-tuple-element.35.t0, f32[1024,256]{1,0:T(8,128)} %get-tuple-element.36.s0, ...), custom_call_target="tpu_custom_call" | custom-call | flops 2684354560 | bytes 13107200 | tf_op jit(solution)/shard_map/gradients/pallas_call | solution.py:277
  114.3 5.5 %all-to-all-start.2 = ((bf16[16,640,128]{2,1,0:T(8,128)(2,1)}), bf16[16,640,128]{2,1,0:T(8,128)(2,1)S(1)}, u32[]{:S(2)}, u32[]{:S(2)}) async-start(bf16[16,640,128]{2,1,0:T(8,128)(2,1)} %bitcast.83), calls=%async_computation.2 | async-start | bytes 5242880 | tf_op jit(solution)/shard_map/all_to_all | solution.py:423
  120.5 31.3 %all-to-all-done.2 = bf16[16,640,128]{2,1,0:T(8,128)(2,1)S(1)} async-done(((bf16[16,640,128]{2,1,0:T(8,128)(2,1)}), bf16[16,640,128]{2,1,0:T(8,128)(2,1)S(1)}, u32[]{:S(2)}, u32[]{:S(2)}) %all-to-all-start.2) | async-done | bytes 2621472 | tf_op jit(solution)/shard_map/all_to_all | solution.py:423
  152.8 3.4 %all-to-all-start.3 = ((bf16[8,80,128]{2,1,0:T(8,128)(2,1)}), bf16[8,80,128]{2,1,0:T(8,128)(2,1)S(1)}, u32[]{:S(2)}, u32[]{:S(2)}) async-start(bf16[8,80,128]{2,1,0:T(8,128)(2,1)} %bitcast.20), calls=%async_computation.3 | async-start | bytes 327680 | tf_op jit(solution)/shard_map/all_to_all | solution.py:425
  156.8 7.4 %weight_gradient.1 = bf16[512,2560]{1,0:T(8,128)(2,1)} custom-call(bf16[512,512]{1,0:T(8,128)(2,1)} %get-tuple-element.41.own_ref, bf16[512,512]{1,0:T(8,128)(2,1)} %collective-permute-done.10.from_ref, bf16[256,2560]{1,0:T(8,128)(2,1)} %get-tuple-element.43.s0_ref, bf16[256,2560]{1,0:T(8,128)(2,1)} %get-tuple-element.44.s1_ref, ...), custom_call_target="tpu_custom_call" | custom-call | flops 2684354560 | bytes 8912896 | tf_op jit(solution)/shard_map/weight_gradient/pallas_call | solution.py:337
  164.1 1.5 all-to-all-done.3
  (64 shorter events, 11.7 us)
Async XLA Ops:
  0.6 7.4 %copy-start.5 = (bf16[128,2560]{1,0:T(8,128)(2,1)S(1)}, bf16[128,2560]{1,0:T(8,128)(2,1)}, u32[]{:S(2)}) copy-start(bf16[128,2560]{1,0:T(8,128)(2,1)} %param.7) | copy-start | bytes 1966084
  0.6 22.9 %collective-permute-start.4 = (bf16[512,5376]{1,0:T(8,128)(2,1)}, bf16[512,5376]{1,0:T(8,128)(2,1)}, u32[]{:S(2)}, u32[]{:S(2)}) collective-permute-start(bf16[512,5376]{1,0:T(8,128)(2,1)} %own_ref.2), channel_id=1, source_target_pairs={{1,0},{0,1},{3,2},{2,3},{5,4},{4,5},{7,6},{6,7},{9,8},{8,9},{11,10... | collective-permute-start | bytes 16515080 | tf_op jit(solution)/shard_map/ppermute | solution.py:20
  0.7 22.8 %collective-permute-start.5 = (bf16[512,2560]{1,0:T(8,128)(2,1)}, bf16[512,2560]{1,0:T(8,128)(2,1)}, u32[]{:S(2)}, u32[]{:S(2)}) collective-permute-start(bf16[512,2560]{1,0:T(8,128)(2,1)} %rest_3_.1), channel_id=1, source_target_pairs={{1,0},{0,1},{3,2},{2,3},{5,4},{4,5},{7,6},{6,7},{9,8},{8,9},{11,10... | collective-permute-start | bytes 7864328 | tf_op jit(solution)/shard_map/ppermute | solution.py:20
  3.1 13.8 %copy-start.7 = (f32[512,42]{0,1:T(8,128)S(1)}, f32[512,42]{0,1:T(8,128)}, u32[]{:S(2)}) copy-start(f32[512,42]{0,1:T(8,128)} %param.9) | copy-start | bytes 258052
  3.1 9.8 %collective-permute-start = (bf16[16,7936]{1,0:T(8,128)(2,1)S(1)}, bf16[16,7936]{1,0:T(8,128)(2,1)}, u32[]{:S(2)}, u32[]{:S(2)}) collective-permute-start(bf16[16,7936]{1,0:T(8,128)(2,1)S(1)} %pad_maximum_fusion), channel_id=1, source_target_pairs={{4,0},{6,2},{0,4},{2,6},{5,1},{7,3},{1,5},{3,7},{12,8},{14,10},{8,... | collective-permute-start | bytes 761864 | tf_op jit(solution)/shard_map/ppermute | solution.py:20
  8.0 20.1 %copy-start.9 = (bf16[128]{0:T(256)(128)(2,1)S(1)}, bf16[128]{0:T(256)(128)(2,1)}, u32[]{:S(2)}) copy-start(bf16[128]{0:T(256)(128)(2,1)} %param.11) | copy-start | bytes 772
  8.0 20.1 %copy-start = (bf16[512,2560]{1,0:T(8,128)(2,1)S(1)}, bf16[512,2560]{1,0:T(8,128)(2,1)}, u32[]{:S(2)}) copy-start(bf16[512,2560]{1,0:T(8,128)(2,1)} %rest_3_.1) | copy-start | bytes 7864324
  12.9 7.7 %collective-permute-start.3 = (bf16[16,7936]{1,0:T(8,128)(2,1)}, bf16[16,7936]{1,0:T(8,128)(2,1)S(1)}, u32[]{:S(2)}, u32[]{:S(2)}) collective-permute-start(bf16[16,7936]{1,0:T(8,128)(2,1)} %collective-permute-done), channel_id=1, source_target_pairs={{0,8},{8,0},{16,24},{24,16},{32,40},{40,32},{48,56},{56,48},{1,9},... | collective-permute-start | bytes 761864 | tf_op jit(solution)/shard_map/ppermute | solution.py:371
  14.9 47.8 %collective-permute-start.1 = (bf16[128,7936]{1,0:T(8,128)(2,1)}, bf16[128,7936]{1,0:T(8,128)(2,1)}, u32[]{:S(2)}, u32[]{:S(2)}) collective-permute-start(bf16[128,7936]{1,0:T(8,128)(2,1)} %constant_dynamic-update-slice_fusion.rest_0_), channel_id=1, source_target_pairs={{2,0},{4,2},{6,4},{0,6},{3,1},{5,3},{7,5},{1,7},{10,8},{12,10},{14... | collective-permute-start | bytes 6094856 | tf_op jit(solution)/shard_map/ppermute | solution.py:20
  15.3 47.4 %collective-permute-start.2 = (bf16[128,7936]{1,0:T(8,128)(2,1)}, bf16[128,7936]{1,0:T(8,128)(2,1)}, u32[]{:S(2)}, u32[]{:S(2)}) collective-permute-start(bf16[128,7936]{1,0:T(8,128)(2,1)} %constant_dynamic-update-slice_fusion.rest_0_), channel_id=1, source_target_pairs={{6,0},{0,2},{2,4},{4,6},{7,1},{1,3},{3,5},{5,7},{14,8},{8,10},{10,... | collective-permute-start | bytes 6094856 | tf_op jit(solution)/shard_map/ppermute | solution.py:20
  21.3 1.5 collective-permute-start.6
  23.6 25.1 %collective-permute-start.7 = (bf16[32,7936]{1,0:T(8,128)(2,1)S(1)}, bf16[32,7936]{1,0:T(8,128)(2,1)}, u32[]{:S(2)}, u32[]{:S(2)}) collective-permute-start(bf16[32,7936]{1,0:T(8,128)(2,1)S(1)} %maximum_select_fusion.rest_1_), channel_id=1, source_target_pairs={{64,0},{128,64},{192,128},{0,192},{65,1},{129,65},{193,129},{1,193... | collective-permute-start | bytes 1523720 | tf_op jit(solution)/shard_map/ppermute | solution.py:20
  26.3 22.4 %collective-permute-start.8 = (bf16[32,7936]{1,0:T(8,128)(2,1)S(1)}, bf16[32,7936]{1,0:T(8,128)(2,1)}, u32[]{:S(2)}, u32[]{:S(2)}) collective-permute-start(bf16[32,7936]{1,0:T(8,128)(2,1)S(1)} %maximum_select_fusion.rest_1_), channel_id=1, source_target_pairs={{128,0},{192,64},{0,128},{64,192},{129,1},{193,65},{1,129},{65,193... | collective-permute-start | bytes 1523720 | tf_op jit(solution)/shard_map/ppermute | solution.py:20
  27.1 25.3 %collective-permute-start.9 = (bf16[32,7936]{1,0:T(8,128)(2,1)S(1)}, bf16[32,7936]{1,0:T(8,128)(2,1)}, u32[]{:S(2)}, u32[]{:S(2)}) collective-permute-start(bf16[32,7936]{1,0:T(8,128)(2,1)S(1)} %maximum_select_fusion.rest_1_), channel_id=1, source_target_pairs={{192,0},{0,64},{64,128},{128,192},{193,1},{1,65},{65,129},{129,193... | collective-permute-start | bytes 1523720 | tf_op jit(solution)/shard_map/ppermute | solution.py:20
  28.1 34.6 %copy-start.4 = (s32[2]{0:T(128)}, s32[2]{0:T(128)S(1)}, u32[]{:S(2)}) copy-start(s32[2]{0:T(128)S(1)} %pad_add_fusion.place_ref.y_ref) | copy-start | bytes 28
  28.1 7.3 %copy-start.3 = (f32[512,42]{1,0:T(8,128)S(1)}, f32[512,42]{1,0:T(8,128)}, u32[]{:S(2)}) copy-start(f32[512,42]{1,0:T(8,128)} %copy-done.2) | copy-start | bytes 258052
  35.4 2.6 %copy-start.1 = (bf16[512,5376]{1,0:T(8,128)(2,1)S(1)}, bf16[512,5376]{1,0:T(8,128)(2,1)}, u32[]{:S(2)}) copy-start(bf16[512,5376]{1,0:T(8,128)(2,1)} %own_ref.2) | copy-start | bytes 16515076
  87.6 16.7 %all-to-all-start.1 = ((f32[8,5,512]{2,1,0:T(8,128)}), f32[8,5,512]{2,1,0:T(8,128)S(1)}, u32[]{:S(2)}, u32[]{:S(2)}) async-start(f32[8,5,512]{2,1,0:T(8,128)} %broadcast_in_dim.20), calls=%async_computation.1 | async-start | bytes 262144 | tf_op jit(solution)/shard_map/all_to_all | solution.py:305
  114.3 6.0 %copy-start.8 = (bf16[512,512]{1,0:T(8,128)(2,1)S(1)}, bf16[512,512]{1,0:T(8,128)(2,1)}, u32[]{:S(2)}) copy-start(bf16[512,512]{1,0:T(8,128)(2,1)} %get-tuple-element.42) | copy-start | bytes 1572868
  114.3 37.4 %all-to-all-start.2 = ((bf16[16,640,128]{2,1,0:T(8,128)(2,1)}), bf16[16,640,128]{2,1,0:T(8,128)(2,1)S(1)}, u32[]{:S(2)}, u32[]{:S(2)}) async-start(bf16[16,640,128]{2,1,0:T(8,128)(2,1)} %bitcast.83), calls=%async_computation.2 | async-start | bytes 5242880 | tf_op jit(solution)/shard_map/all_to_all | solution.py:423
  119.9 36.9 %collective-permute-start.12 = (bf16[256,2560]{1,0:T(8,128)(2,1)}, bf16[256,2560]{1,0:T(8,128)(2,1)}, u32[]{:S(2)}, u32[]{:S(2)}) collective-permute-start(bf16[256,2560]{1,0:T(8,128)(2,1)} %get-tuple-element.44.s1_ref), channel_id=1, source_target_pairs={{1,0},{0,1},{3,2},{2,3},{5,4},{4,5},{7,6},{6,7},{9,8},{8,9},{11,10... | collective-permute-start | bytes 3932168 | tf_op jit(solution)/shard_map/ppermute | solution.py:20
  119.9 36.9 %collective-permute-start.11 = (bf16[256,2560]{1,0:T(8,128)(2,1)}, bf16[256,2560]{1,0:T(8,128)(2,1)}, u32[]{:S(2)}, u32[]{:S(2)}) collective-permute-start(bf16[256,2560]{1,0:T(8,128)(2,1)} %get-tuple-element.43.s0_ref), channel_id=1, source_target_pairs={{1,0},{0,1},{3,2},{2,3},{5,4},{4,5},{7,6},{6,7},{9,8},{8,9},{11,10... | collective-permute-start | bytes 3932168 | tf_op jit(solution)/shard_map/ppermute | solution.py:20
  120.4 36.4 %collective-permute-start.10 = (bf16[512,512]{1,0:T(8,128)(2,1)S(1)}, bf16[512,512]{1,0:T(8,128)(2,1)}, u32[]{:S(2)}, u32[]{:S(2)}) collective-permute-start(bf16[512,512]{1,0:T(8,128)(2,1)S(1)} %copy-done.8), channel_id=1, source_target_pairs={{1,0},{0,1},{3,2},{2,3},{5,4},{4,5},{7,6},{6,7},{9,8},{8,9},{11,10... | collective-permute-start | bytes 1572872 | tf_op jit(solution)/shard_map/ppermute | solution.py:20
  152.8 12.7 %all-to-all-start.3 = ((bf16[8,80,128]{2,1,0:T(8,128)(2,1)}), bf16[8,80,128]{2,1,0:T(8,128)(2,1)S(1)}, u32[]{:S(2)}, u32[]{:S(2)}) async-start(bf16[8,80,128]{2,1,0:T(8,128)(2,1)} %bitcast.20), calls=%async_computation.3 | async-start | bytes 327680 | tf_op jit(solution)/shard_map/all_to_all | solution.py:425
  (2 other events, 1.4 us)

commit v10 on v9

--- a/solution.py
+++ b/solution.py
@@ -27,9 +27,9 @@
 
 NT = (((1,), (1,)), ((), ()))
 MIB = 1024 * 1024
-VMEM_LOGITS = 18 * MIB
+VMEM_LOGITS = 20 * MIB
 DEQUANT_ROWS = 128
-LOGIT_ROWS = 256
+LOGIT_ROWS = 512
 WEIGHT_COLUMNS = 512
 
 

time: 167 us -> 166 us (level)
  no operation moved by 1% of the time
where the time goes in v10:
time: 166 us; the launch traced here: 164 us
  waiting for transfers between devices  54.2 us (33%)
  Pallas kernels  52.6 us (32%)
  starting transfers between devices  28.2 us (17%)
  blocking collectives  13.9 us (8%)
  local copies, waits for them, and re-layouts  10.6 us (6%)
  other arithmetic  4.22 us (3%)
    all_to_all x1, waiting for transfers between devices, local(): got = lax.all_to_all(blocks, ('x', 'y'), 0, 0, tiled=True)  30.6 us
    pallas_call x2, Pallas kernels, logits_of(): pl.pallas_call(functools.partial(logits_kernel, len(pieces)), in_specs=in...  19.5 us
    all_to_all x1, blocking collectives, local(): seen = lax.all_to_all(mine, ('x', 'y'), 0, 0, tiled=True)  13.9 us
    ppermute x12, starting transfers between devices, shift(): return lax.ppermute(a, axis, [((i + by) % n, i) for i in range(n)])  10 us
    ppermute x12, waiting for transfers between devices, shift(): return lax.ppermute(a, axis, [((i + by) % n, i) for i in range(n)])  9.42 us
    pallas_call x1, Pallas kernels, dequantize(): pl.pallas_call(functools.partial(dequant_kernel, steps), grid=(2 * steps,...  9.24 us
    pallas_call x1, Pallas kernels, gradients(): pl.pallas_call(grad_kernel, grid_spec=pltpu.PrefetchScalarGridSpec(num_sc...  9.22 us
    all_to_all x1, waiting for transfers between devices, to_all(): lax.all_to_all(jnp.broadcast_to(a[None], (n, *a.shape)), axes, 0, 0, tile...  9.05 us
  transfers between devices with their start and end apart: 16, of which 8 were waited for; matrix products, arithmetic and copies ran while one was open for 5% of the time, Pallas kernels for 20%

profile of v10, /device:TPU:8, one launch (start us, length us, event | category | flops | bytes accessed | tf_op | source)
XLA Modules:
  0.0 164.5 jit_solution(14162806332510603495)
XLA Ops:
  3.1 2.4 %collective-permute-start = (bf16[16,7936]{1,0:T(8,128)(2,1)S(1)}, bf16[16,7936]{1,0:T(8,128)(2,1)}, u32[]{:S(2)}, u32[]{:S(2)}) collective-permute-start(bf16[16,7936]{1,0:T(8,128)(2,1)S(1)} %pad_maximum_fusion), channel_id=1, source_target_pairs={{4,0},{6,2},{0,4},{2,6},{5,1},{7,3},{1,5},{3,7},{12,8},{14,10},{8,... | collective-permute-start | bytes 761864 | tf_op jit(solution)/shard_map/ppermute | solution.py:20
  5.5 2.5 %constant_dynamic-update-slice_fusion.1 = bf16[128,7936]{1,0:T(8,128)(2,1)} fusion(bf16[128,5376]{1,0:T(8,128)(2,1)} %param.6), kind=kLoop, calls=%fused_computation.34 | loop fusion | bytes 2752512
  8.9 4.1 %collective-permute-done = bf16[16,7936]{1,0:T(8,128)(2,1)} collective-permute-done((bf16[16,7936]{1,0:T(8,128)(2,1)S(1)}, bf16[16,7936]{1,0:T(8,128)(2,1)}, u32[]{:S(2)}, u32[]{:S(2)}) %collective-permute-start) | collective-permute-done | bytes 253984 | tf_op jit(solution)/shard_map/ppermute | solution.py:20
  12.9 1.9 %collective-permute-start.3 = (bf16[16,7936]{1,0:T(8,128)(2,1)}, bf16[16,7936]{1,0:T(8,128)(2,1)S(1)}, u32[]{:S(2)}, u32[]{:S(2)}) collective-permute-start(bf16[16,7936]{1,0:T(8,128)(2,1)} %collective-permute-done), channel_id=1, source_target_pairs={{0,8},{8,0},{16,24},{24,16},{32,40},{40,32},{48,56},{56,48},{1,9},... | collective-permute-start | bytes 761864 | tf_op jit(solution)/shard_map/ppermute | solution.py:371
  15.3 1.6 collective-permute-start.2
  17.0 3.6 %collective-permute-done.3 = bf16[16,7936]{1,0:T(8,128)(2,1)S(1)} collective-permute-done((bf16[16,7936]{1,0:T(8,128)(2,1)}, bf16[16,7936]{1,0:T(8,128)(2,1)S(1)}, u32[]{:S(2)}, u32[]{:S(2)}) %collective-permute-start.3) | collective-permute-done | bytes 253984 | tf_op jit(solution)/shard_map/ppermute | solution.py:371
  21.3 1.4 maximum_select_fusion.rest_1_
  23.6 2.8 %collective-permute-start.7 = (bf16[32,7936]{1,0:T(8,128)(2,1)S(1)}, bf16[32,7936]{1,0:T(8,128)(2,1)}, u32[]{:S(2)}, u32[]{:S(2)}) collective-permute-start(bf16[32,7936]{1,0:T(8,128)(2,1)S(1)} %maximum_select_fusion.rest_1_), channel_id=1, source_target_pairs={{64,0},{128,64},{192,128},{0,192},{65,1},{129,65},{193,129},{1,193... | collective-permute-start | bytes 1523720 | tf_op jit(solution)/shard_map/ppermute | solution.py:20
  28.1 7.3 %turn.1.turned_ref = bf16[2560,1024]{1,0:T(8,128)(2,1)} custom-call(bf16[512,2560]{1,0:T(8,128)(2,1)S(1)} %copy-done, bf16[512,2560]{1,0:T(8,128)(2,1)} %collective-permute-done.5.rest_7_.other_ref.rest_4_), custom_call_target="tpu_custom_call" | custom-call | bytes 10485760 | tf_op jit(solution)/shard_map/turn/pallas_call | solution.py:95
  35.4 2.6 %copy-done.1 = bf16[512,5376]{1,0:T(8,128)(2,1)S(1)} copy-done((bf16[512,5376]{1,0:T(8,128)(2,1)S(1)}, bf16[512,5376]{1,0:T(8,128)(2,1)}, u32[]{:S(2)}) %copy-start.1) | copy-done | bytes 5505048
  38.0 9.2 %dequantize.1.rest_5_.rest_2_ = bf16[1024,5376]{1,0:T(8,128)(2,1)S(1)} custom-call(bf16[512,5376]{1,0:T(8,128)(2,1)S(1)} %copy-done.1, bf16[512,5376]{1,0:T(8,128)(2,1)} %collective-permute-done.4.other_ref, f32[512,42]{1,0:T(8,128)S(1)} %copy.22.own_scale_ref, f32[512,42]{1,0:T(8,128)S(1)} %copy-done.3), custom_call_target="tpu_custom_call" | custom-call | flops 5505024 | bytes 22020096 | tf_op jit(solution)/shard_map/dequantize/pallas_call | solution.py:63
  47.2 1.5 collective-permute-done.7.rest_2_
  48.7 3.8 %collective-permute-done.9.rest_4_ = bf16[32,7936]{1,0:T(8,128)(2,1)} collective-permute-done((bf16[32,7936]{1,0:T(8,128)(2,1)S(1)}, bf16[32,7936]{1,0:T(8,128)(2,1)}, u32[]{:S(2)}, u32[]{:S(2)}) %collective-permute-start.9) | collective-permute-done | bytes 507936 | tf_op jit(solution)/shard_map/ppermute | solution.py:20
  52.5 9.3 %logits.2 = (f32[1024,256]{1,0:T(8,128)}, f32[1024,256]{1,0:T(8,128)}, f32[8,256]{1,0:T(8,128)S(1)}, bf16[256,2560]{1,0:T(8,128)(2,1)}) custom-call(s32[2]{0:T(128)S(1)} %pad_add_fusion.place_ref.y_ref, bf16[128,7936]{1,0:T(8,128)(2,1)} %constant_dynamic-update-slice_fusion.rest_0_, bf16[32,7936]{1,0:T(8,128)(2,1)S(1)} %maximum_select_fusion.rest_1_, ...), custom_call_target="tpu_custom_call" | custom-call | flops 4160749568 | bytes 7471104 | tf_op jit(solution)/shard_map/logits/pallas_call | solution.py:226
  61.9 10.1 %logits.3 = (f32[1024,256]{1,0:T(8,128)}, f32[1024,256]{1,0:T(8,128)}, f32[8,256]{1,0:T(8,128)}, bf16[256,2560]{1,0:T(8,128)(2,1)}, f32[16,8,512]{2,1,0:T(8,128)S(1)}) custom-call(s32[2]{0:T(128)S(1)} %pad_add_fusion.place_ref.y_ref, bf16[128,7936]{1,0:T(8,128)(2,1)} %collective-permute-done.1.rest_0_, bf16[128,7936]{1,0:T(8,128)(2,1)} %collective-permute-done.2.rest_1_, ...), custom_call_target="tpu_custom_call" | custom-call | flops 4160749568 | bytes 7471104 | tf_op jit(solution)/shard_map/logits/pallas_call | solution.py:226
  72.0 13.9 %all_to_all.20 = f32[16,8,512]{2,1,0:T(8,128)S(1)} all-to-all(f32[16,8,512]{2,1,0:T(8,128)S(1)} %get-tuple-element.34), channel_id=1, replica_groups=mesh['x'=4,'z'=8,'y'=4,'c'=2] {'x','y'}, dimensions={0} | all-to-all | bytes 524288 | tf_op jit(solution)/shard_map/all_to_all | solution.py:398
  86.8 7.6 %all-to-all-start.1 = ((f32[8,5,512]{2,1,0:T(8,128)}), f32[8,5,512]{2,1,0:T(8,128)S(1)}, u32[]{:S(2)}, u32[]{:S(2)}) async-start(f32[8,5,512]{2,1,0:T(8,128)} %broadcast_in_dim.20), calls=%async_computation.1 | async-start | bytes 262144 | tf_op jit(solution)/shard_map/all_to_all | solution.py:305
  94.4 9.1 %all-to-all-done.1 = f32[8,5,512]{2,1,0:T(8,128)S(1)} async-done(((f32[8,5,512]{2,1,0:T(8,128)}), f32[8,5,512]{2,1,0:T(8,128)S(1)}, u32[]{:S(2)}, u32[]{:S(2)}) %all-to-all-start.1) | async-done | bytes 81952 | tf_op jit(solution)/shard_map/all_to_all | solution.py:305
  104.3 9.2 %gradients.1 = (bf16[512,512]{1,0:T(8,128)(2,1)}, bf16[512,512]{1,0:T(8,128)(2,1)}, bf16[4,4,640,128]{3,2,1,0:T(8,128)(2,1)}) custom-call(s32[2]{0:T(128)} %copy-done.4, f32[8,512]{1,0:T(8,128)} %pad_maximum_fusion.1.rows_ref, f32[1024,256]{1,0:T(8,128)} %get-tuple-element.35.t0, f32[1024,256]{1,0:T(8,128)} %get-tuple-element.36.s0, ...), custom_call_target="tpu_custom_call" | custom-call | flops 2684354560 | bytes 13107200 | tf_op jit(solution)/shard_map/gradients/pallas_call | solution.py:277
  113.5 5.3 %all-to-all-start.2 = ((bf16[16,640,128]{2,1,0:T(8,128)(2,1)}), bf16[16,640,128]{2,1,0:T(8,128)(2,1)S(1)}, u32[]{:S(2)}, u32[]{:S(2)}) async-start(bf16[16,640,128]{2,1,0:T(8,128)(2,1)} %bitcast.83), calls=%async_computation.2 | async-start | bytes 5242880 | tf_op jit(solution)/shard_map/all_to_all | solution.py:423
  119.4 30.6 %all-to-all-done.2 = bf16[16,640,128]{2,1,0:T(8,128)(2,1)S(1)} async-done(((bf16[16,640,128]{2,1,0:T(8,128)(2,1)}), bf16[16,640,128]{2,1,0:T(8,128)(2,1)S(1)}, u32[]{:S(2)}, u32[]{:S(2)}) %all-to-all-start.2) | async-done | bytes 2621472 | tf_op jit(solution)/shard_map/all_to_all | solution.py:423
  151.1 3.4 %all-to-all-start.3 = ((bf16[8,80,128]{2,1,0:T(8,128)(2,1)}), bf16[8,80,128]{2,1,0:T(8,128)(2,1)S(1)}, u32[]{:S(2)}, u32[]{:S(2)}) async-start(bf16[8,80,128]{2,1,0:T(8,128)(2,1)} %bitcast.20), calls=%async_computation.3 | async-start | bytes 327680 | tf_op jit(solution)/shard_map/all_to_all | solution.py:425
  155.0 7.4 %weight_gradient.1 = bf16[512,2560]{1,0:T(8,128)(2,1)} custom-call(bf16[512,512]{1,0:T(8,128)(2,1)} %get-tuple-element.41.own_ref, bf16[512,512]{1,0:T(8,128)(2,1)} %collective-permute-done.10.from_ref, bf16[256,2560]{1,0:T(8,128)(2,1)} %get-tuple-element.43.s0_ref, bf16[256,2560]{1,0:T(8,128)(2,1)} %get-tuple-element.44.s1_ref, ...), custom_call_target="tpu_custom_call" | custom-call | flops 2684354560 | bytes 8912896 | tf_op jit(solution)/shard_map/weight_gradient/pallas_call | solution.py:337
  162.4 1.5 all-to-all-done.3
  (64 shorter events, 11.7 us)
Async XLA Ops:
  0.6 7.4 %copy-start.5 = (bf16[128,2560]{1,0:T(8,128)(2,1)S(1)}, bf16[128,2560]{1,0:T(8,128)(2,1)}, u32[]{:S(2)}) copy-start(bf16[128,2560]{1,0:T(8,128)(2,1)} %param.7) | copy-start | bytes 1966084
  0.6 22.9 %collective-permute-start.4 = (bf16[512,5376]{1,0:T(8,128)(2,1)}, bf16[512,5376]{1,0:T(8,128)(2,1)}, u32[]{:S(2)}, u32[]{:S(2)}) collective-permute-start(bf16[512,5376]{1,0:T(8,128)(2,1)} %own_ref.2), channel_id=1, source_target_pairs={{1,0},{0,1},{3,2},{2,3},{5,4},{4,5},{7,6},{6,7},{9,8},{8,9},{11,10... | collective-permute-start | bytes 16515080 | tf_op jit(solution)/shard_map/ppermute | solution.py:20
  0.7 22.8 %collective-permute-start.5 = (bf16[512,2560]{1,0:T(8,128)(2,1)}, bf16[512,2560]{1,0:T(8,128)(2,1)}, u32[]{:S(2)}, u32[]{:S(2)}) collective-permute-start(bf16[512,2560]{1,0:T(8,128)(2,1)} %rest_3_.1), channel_id=1, source_target_pairs={{1,0},{0,1},{3,2},{2,3},{5,4},{4,5},{7,6},{6,7},{9,8},{8,9},{11,10... | collective-permute-start | bytes 7864328 | tf_op jit(solution)/shard_map/ppermute | solution.py:20
  3.1 13.8 %copy-start.7 = (f32[512,42]{0,1:T(8,128)S(1)}, f32[512,42]{0,1:T(8,128)}, u32[]{:S(2)}) copy-start(f32[512,42]{0,1:T(8,128)} %param.9) | copy-start | bytes 258052
  3.1 9.8 %collective-permute-start = (bf16[16,7936]{1,0:T(8,128)(2,1)S(1)}, bf16[16,7936]{1,0:T(8,128)(2,1)}, u32[]{:S(2)}, u32[]{:S(2)}) collective-permute-start(bf16[16,7936]{1,0:T(8,128)(2,1)S(1)} %pad_maximum_fusion), channel_id=1, source_target_pairs={{4,0},{6,2},{0,4},{2,6},{5,1},{7,3},{1,5},{3,7},{12,8},{14,10},{8,... | collective-permute-start | bytes 761864 | tf_op jit(solution)/shard_map/ppermute | solution.py:20
  8.0 20.1 %copy-start.9 = (bf16[128]{0:T(256)(128)(2,1)S(1)}, bf16[128]{0:T(256)(128)(2,1)}, u32[]{:S(2)}) copy-start(bf16[128]{0:T(256)(128)(2,1)} %param.11) | copy-start | bytes 772
  8.0 20.1 %copy-start = (bf16[512,2560]{1,0:T(8,128)(2,1)S(1)}, bf16[512,2560]{1,0:T(8,128)(2,1)}, u32[]{:S(2)}) copy-start(bf16[512,2560]{1,0:T(8,128)(2,1)} %rest_3_.1) | copy-start | bytes 7864324
  12.9 7.7 %collective-permute-start.3 = (bf16[16,7936]{1,0:T(8,128)(2,1)}, bf16[16,7936]{1,0:T(8,128)(2,1)S(1)}, u32[]{:S(2)}, u32[]{:S(2)}) collective-permute-start(bf16[16,7936]{1,0:T(8,128)(2,1)} %collective-permute-done), channel_id=1, source_target_pairs={{0,8},{8,0},{16,24},{24,16},{32,40},{40,32},{48,56},{56,48},{1,9},... | collective-permute-start | bytes 761864 | tf_op jit(solution)/shard_map/ppermute | solution.py:371
  14.9 47.0 %collective-permute-start.1 = (bf16[128,7936]{1,0:T(8,128)(2,1)}, bf16[128,7936]{1,0:T(8,128)(2,1)}, u32[]{:S(2)}, u32[]{:S(2)}) collective-permute-start(bf16[128,7936]{1,0:T(8,128)(2,1)} %constant_dynamic-update-slice_fusion.rest_0_), channel_id=1, source_target_pairs={{2,0},{4,2},{6,4},{0,6},{3,1},{5,3},{7,5},{1,7},{10,8},{12,10},{14... | collective-permute-start | bytes 6094856 | tf_op jit(solution)/shard_map/ppermute | solution.py:20
  15.3 46.5 %collective-permute-start.2 = (bf16[128,7936]{1,0:T(8,128)(2,1)}, bf16[128,7936]{1,0:T(8,128)(2,1)}, u32[]{:S(2)}, u32[]{:S(2)}) collective-permute-start(bf16[128,7936]{1,0:T(8,128)(2,1)} %constant_dynamic-update-slice_fusion.rest_0_), channel_id=1, source_target_pairs={{6,0},{0,2},{2,4},{4,6},{7,1},{1,3},{3,5},{5,7},{14,8},{8,10},{10,... | collective-permute-start | bytes 6094856 | tf_op jit(solution)/shard_map/ppermute | solution.py:20
  21.3 1.5 collective-permute-start.6
  23.6 25.1 %collective-permute-start.7 = (bf16[32,7936]{1,0:T(8,128)(2,1)S(1)}, bf16[32,7936]{1,0:T(8,128)(2,1)}, u32[]{:S(2)}, u32[]{:S(2)}) collective-permute-start(bf16[32,7936]{1,0:T(8,128)(2,1)S(1)} %maximum_select_fusion.rest_1_), channel_id=1, source_target_pairs={{64,0},{128,64},{192,128},{0,192},{65,1},{129,65},{193,129},{1,193... | collective-permute-start | bytes 1523720 | tf_op jit(solution)/shard_map/ppermute | solution.py:20
  26.3 22.4 %collective-permute-start.8 = (bf16[32,7936]{1,0:T(8,128)(2,1)S(1)}, bf16[32,7936]{1,0:T(8,128)(2,1)}, u32[]{:S(2)}, u32[]{:S(2)}) collective-permute-start(bf16[32,7936]{1,0:T(8,128)(2,1)S(1)} %maximum_select_fusion.rest_1_), channel_id=1, source_target_pairs={{128,0},{192,64},{0,128},{64,192},{129,1},{193,65},{1,129},{65,193... | collective-permute-start | bytes 1523720 | tf_op jit(solution)/shard_map/ppermute | solution.py:20
  27.1 25.3 %collective-permute-start.9 = (bf16[32,7936]{1,0:T(8,128)(2,1)S(1)}, bf16[32,7936]{1,0:T(8,128)(2,1)}, u32[]{:S(2)}, u32[]{:S(2)}) collective-permute-start(bf16[32,7936]{1,0:T(8,128)(2,1)S(1)} %maximum_select_fusion.rest_1_), channel_id=1, source_target_pairs={{192,0},{0,64},{64,128},{128,192},{193,1},{1,65},{65,129},{129,193... | collective-permute-start | bytes 1523720 | tf_op jit(solution)/shard_map/ppermute | solution.py:20
  28.1 33.7 %copy-start.4 = (s32[2]{0:T(128)}, s32[2]{0:T(128)S(1)}, u32[]{:S(2)}) copy-start(s32[2]{0:T(128)S(1)} %pad_add_fusion.place_ref.y_ref) | copy-start | bytes 28
  28.1 7.3 %copy-start.3 = (f32[512,42]{1,0:T(8,128)S(1)}, f32[512,42]{1,0:T(8,128)}, u32[]{:S(2)}) copy-start(f32[512,42]{1,0:T(8,128)} %copy-done.2) | copy-start | bytes 258052
  35.4 2.6 %copy-start.1 = (bf16[512,5376]{1,0:T(8,128)(2,1)S(1)}, bf16[512,5376]{1,0:T(8,128)(2,1)}, u32[]{:S(2)}) copy-start(bf16[512,5376]{1,0:T(8,128)(2,1)} %own_ref.2) | copy-start | bytes 16515076
  86.8 16.6 %all-to-all-start.1 = ((f32[8,5,512]{2,1,0:T(8,128)}), f32[8,5,512]{2,1,0:T(8,128)S(1)}, u32[]{:S(2)}, u32[]{:S(2)}) async-start(f32[8,5,512]{2,1,0:T(8,128)} %broadcast_in_dim.20), calls=%async_computation.1 | async-start | bytes 262144 | tf_op jit(solution)/shard_map/all_to_all | solution.py:305
  113.5 5.8 %copy-start.8 = (bf16[512,512]{1,0:T(8,128)(2,1)S(1)}, bf16[512,512]{1,0:T(8,128)(2,1)}, u32[]{:S(2)}) copy-start(bf16[512,512]{1,0:T(8,128)(2,1)} %get-tuple-element.42) | copy-start | bytes 1572868
  113.5 36.6 %all-to-all-start.2 = ((bf16[16,640,128]{2,1,0:T(8,128)(2,1)}), bf16[16,640,128]{2,1,0:T(8,128)(2,1)S(1)}, u32[]{:S(2)}, u32[]{:S(2)}) async-start(bf16[16,640,128]{2,1,0:T(8,128)(2,1)} %bitcast.83), calls=%async_computation.2 | async-start | bytes 5242880 | tf_op jit(solution)/shard_map/all_to_all | solution.py:423
  118.8 36.2 %collective-permute-start.12 = (bf16[256,2560]{1,0:T(8,128)(2,1)}, bf16[256,2560]{1,0:T(8,128)(2,1)}, u32[]{:S(2)}, u32[]{:S(2)}) collective-permute-start(bf16[256,2560]{1,0:T(8,128)(2,1)} %get-tuple-element.44.s1_ref), channel_id=1, source_target_pairs={{1,0},{0,1},{3,2},{2,3},{5,4},{4,5},{7,6},{6,7},{9,8},{8,9},{11,10... | collective-permute-start | bytes 3932168 | tf_op jit(solution)/shard_map/ppermute | solution.py:20
  118.8 36.2 %collective-permute-start.11 = (bf16[256,2560]{1,0:T(8,128)(2,1)}, bf16[256,2560]{1,0:T(8,128)(2,1)}, u32[]{:S(2)}, u32[]{:S(2)}) collective-permute-start(bf16[256,2560]{1,0:T(8,128)(2,1)} %get-tuple-element.43.s0_ref), channel_id=1, source_target_pairs={{1,0},{0,1},{3,2},{2,3},{5,4},{4,5},{7,6},{6,7},{9,8},{8,9},{11,10... | collective-permute-start | bytes 3932168 | tf_op jit(solution)/shard_map/ppermute | solution.py:20
  119.3 35.7 %collective-permute-start.10 = (bf16[512,512]{1,0:T(8,128)(2,1)S(1)}, bf16[512,512]{1,0:T(8,128)(2,1)}, u32[]{:S(2)}, u32[]{:S(2)}) collective-permute-start(bf16[512,512]{1,0:T(8,128)(2,1)S(1)} %copy-done.8), channel_id=1, source_target_pairs={{1,0},{0,1},{3,2},{2,3},{5,4},{4,5},{7,6},{6,7},{9,8},{8,9},{11,10... | collective-permute-start | bytes 1572872 | tf_op jit(solution)/shard_map/ppermute | solution.py:20
  151.1 12.7 %all-to-all-start.3 = ((bf16[8,80,128]{2,1,0:T(8,128)(2,1)}), bf16[8,80,128]{2,1,0:T(8,128)(2,1)S(1)}, u32[]{:S(2)}, u32[]{:S(2)}) async-start(bf16[8,80,128]{2,1,0:T(8,128)(2,1)} %bitcast.20), calls=%async_computation.3 | async-start | bytes 327680 | tf_op jit(solution)/shard_map/all_to_all | solution.py:425
  (2 other events, 1.4 us)

commit v11 on v10

--- a/solution.py
+++ b/solution.py
@@ -130,16 +130,19 @@
         stat_ref[k : k + 1] = row
 
 
-def load_pair(x_ref, refs, pair, sem):
+def load_pair(x_ref, refs, pair, sem, turn, columns):
     tok, part = refs[0].shape[0], refs[1].shape[0]
-    copies = [pltpu.make_async_copy(refs[0], pair.at[pl.ds(0, tok)], sem.at[0])]
-    for k, ref in enumerate(refs[1:]):
+    places = [pl.ds(0, tok)]
+    for k in range(len(refs) - 1):
         at = pl.multiple_of(tok + lax.rem(x_ref[1] + k, tok // part) * part, part)
-        copies.append(pltpu.make_async_copy(ref, pair.at[pl.ds(at, part)], sem.at[k + 1]))
+        places.append(pl.ds(at, part))
+    copies = [
+        pltpu.make_async_copy(ref.at[:, columns], pair.at[rows, columns], sem.at[turn, k])
+        for k, (ref, rows) in enumerate(zip(refs, places))
+    ]
     for copy in copies:
         copy.start()
-    for copy in copies:
-        copy.wait()
+    return copies
 
 
 def logits_kernel(n_pieces, place_ref, *rest):
@@ -155,18 +158,25 @@
     width_t = table_ref.shape[1]
     rows = weight_ref.shape[0]
 
-    load_pair(place_ref, pieces_hbm, pair, load_sem)
+    width_s = weight_ref.shape[1]
+    student_in = load_pair(place_ref, pieces_hbm, pair, load_sem, 0, pl.ds(width_t, width_s))
+    teacher_in = load_pair(place_ref, pieces_hbm, pair, load_sem, 1, pl.ds(0, width_t))
+    for copy in student_in:
+        copy.wait()
     students = pltpu.make_async_copy(pair.at[:, pl.ds(width_t, weight_ref.shape[1])], student_hbm, out_sem.at[2, 0])
     students.start()
     waiting = []
     for i in range(2 * rows // LOGIT_ROWS):
         slot, at = i % 2, i * LOGIT_ROWS
         source, low = (weight_ref, at) if at < rows else (weight_p_ref, at - rows)
+        s = lax.dot_general(
+            source[low : low + LOGIT_ROWS], pair[:, width_t:], NT, preferred_element_type=F32
+        )
+        if i == 0:
+            for copy in teacher_in:
+                copy.wait()
         t = lax.dot_general(
             table_ref[at : at + LOGIT_ROWS], pair[:, :width_t], NT, preferred_element_type=F32
-        )
-        s = lax.dot_general(
-            source[low : low + LOGIT_ROWS], pair[:, width_t:], NT, preferred_element_type=F32
         )
         if i >= 2:
             for copy in waiting[i - 2]:
@@ -232,7 +242,7 @@
             pltpu.VMEM((tokens, width_t + width_s), BF16),
             pltpu.VMEM((2, LOGIT_ROWS, tokens), F32),
             pltpu.VMEM((2, LOGIT_ROWS, tokens), F32),
-            pltpu.SemaphoreType.DMA((len(pieces),)),
+            pltpu.SemaphoreType.DMA((2, len(pieces))),
             pltpu.SemaphoreType.DMA((3, 2)),
         ],
         compiler_params=pltpu.CompilerParams(vmem_limit_bytes=VMEM_LOGITS),

time: 166 us -> 167 us (level)
  transfers between devices with their start and end apart: 16 -> 16, of which waited for: 8 -> 8; matrix products, arithmetic and copies ran while one was open for 5% -> 5% of each run, Pallas kernels for 20% -> 21%
where the time goes in v11:
time: 167 us; the launch traced here: 166 us
  waiting for transfers between devices  54.9 us (33%)
  Pallas kernels  54.2 us (32%)
  starting transfers between devices  28.2 us (17%)
  blocking collectives  13 us (8%)
  local copies, waits for them, and re-layouts  10.6 us (6%)
  other arithmetic  4.22 us (3%)
    all_to_all x1, waiting for transfers between devices, local(): got = lax.all_to_all(blocks, ('x', 'y'), 0, 0, tiled=True)  31.3 us
    pallas_call x2, Pallas kernels, logits_of(): pl.pallas_call(functools.partial(logits_kernel, len(pieces)), in_specs=in...  21.1 us
    all_to_all x1, blocking collectives, local(): seen = lax.all_to_all(mine, ('x', 'y'), 0, 0, tiled=True)  13 us
    ppermute x12, starting transfers between devices, shift(): return lax.ppermute(a, axis, [((i + by) % n, i) for i in range(n)])  10 us
    ppermute x12, waiting for transfers between devices, shift(): return lax.ppermute(a, axis, [((i + by) % n, i) for i in range(n)])  9.42 us
    pallas_call x1, Pallas kernels, dequantize(): pl.pallas_call(functools.partial(dequant_kernel, steps), grid=(2 * steps,...  9.24 us
    pallas_call x1, Pallas kernels, gradients(): pl.pallas_call(grad_kernel, grid_spec=pltpu.PrefetchScalarGridSpec(num_sc...  9.22 us
    all_to_all x1, waiting for transfers between devices, to_all(): lax.all_to_all(jnp.broadcast_to(a[None], (n, *a.shape)), axes, 0, 0, tile...  9.05 us
  transfers between devices with their start and end apart: 16, of which 8 were waited for; matrix products, arithmetic and copies ran while one was open for 5% of the time, Pallas kernels for 21%

profile of v11, /device:TPU:8, one launch (start us, length us, event | category | flops | bytes accessed | tf_op | source)
XLA Modules:
  0.0 165.9 jit_solution(4653139770700723846)
XLA Ops:
  3.1 2.4 %collective-permute-start = (bf16[16,7936]{1,0:T(8,128)(2,1)S(1)}, bf16[16,7936]{1,0:T(8,128)(2,1)}, u32[]{:S(2)}, u32[]{:S(2)}) collective-permute-start(bf16[16,7936]{1,0:T(8,128)(2,1)S(1)} %pad_maximum_fusion), channel_id=1, source_target_pairs={{4,0},{6,2},{0,4},{2,6},{5,1},{7,3},{1,5},{3,7},{12,8},{14,10},{8,... | collective-permute-start | bytes 761864 | tf_op jit(solution)/shard_map/ppermute | solution.py:20
  5.5 2.5 %constant_dynamic-update-slice_fusion.1 = bf16[128,7936]{1,0:T(8,128)(2,1)} fusion(bf16[128,5376]{1,0:T(8,128)(2,1)} %param.6), kind=kLoop, calls=%fused_computation.34 | loop fusion | bytes 2752512
  8.9 4.1 %collective-permute-done = bf16[16,7936]{1,0:T(8,128)(2,1)} collective-permute-done((bf16[16,7936]{1,0:T(8,128)(2,1)S(1)}, bf16[16,7936]{1,0:T(8,128)(2,1)}, u32[]{:S(2)}, u32[]{:S(2)}) %collective-permute-start) | collective-permute-done | bytes 253984 | tf_op jit(solution)/shard_map/ppermute | solution.py:20
  12.9 1.9 %collective-permute-start.3 = (bf16[16,7936]{1,0:T(8,128)(2,1)}, bf16[16,7936]{1,0:T(8,128)(2,1)S(1)}, u32[]{:S(2)}, u32[]{:S(2)}) collective-permute-start(bf16[16,7936]{1,0:T(8,128)(2,1)} %collective-permute-done), channel_id=1, source_target_pairs={{0,8},{8,0},{16,24},{24,16},{32,40},{40,32},{48,56},{56,48},{1,9},... | collective-permute-start | bytes 761864 | tf_op jit(solution)/shard_map/ppermute | solution.py:381
  15.3 1.6 collective-permute-start.2
  17.0 3.6 %collective-permute-done.3 = bf16[16,7936]{1,0:T(8,128)(2,1)S(1)} collective-permute-done((bf16[16,7936]{1,0:T(8,128)(2,1)}, bf16[16,7936]{1,0:T(8,128)(2,1)S(1)}, u32[]{:S(2)}, u32[]{:S(2)}) %collective-permute-start.3) | collective-permute-done | bytes 253984 | tf_op jit(solution)/shard_map/ppermute | solution.py:381
  21.3 1.4 maximum_select_fusion.rest_1_
  23.6 2.8 %collective-permute-start.7 = (bf16[32,7936]{1,0:T(8,128)(2,1)S(1)}, bf16[32,7936]{1,0:T(8,128)(2,1)}, u32[]{:S(2)}, u32[]{:S(2)}) collective-permute-start(bf16[32,7936]{1,0:T(8,128)(2,1)S(1)} %maximum_select_fusion.rest_1_), channel_id=1, source_target_pairs={{64,0},{128,64},{192,128},{0,192},{65,1},{129,65},{193,129},{1,193... | collective-permute-start | bytes 1523720 | tf_op jit(solution)/shard_map/ppermute | solution.py:20
  28.1 7.3 %turn.1.turned_ref = bf16[2560,1024]{1,0:T(8,128)(2,1)} custom-call(bf16[512,2560]{1,0:T(8,128)(2,1)S(1)} %copy-done, bf16[512,2560]{1,0:T(8,128)(2,1)} %collective-permute-done.5.rest_7_.other_ref.rest_4_), custom_call_target="tpu_custom_call" | custom-call | bytes 10485760 | tf_op jit(solution)/shard_map/turn/pallas_call | solution.py:95
  35.4 2.6 %copy-done.1 = bf16[512,5376]{1,0:T(8,128)(2,1)S(1)} copy-done((bf16[512,5376]{1,0:T(8,128)(2,1)S(1)}, bf16[512,5376]{1,0:T(8,128)(2,1)}, u32[]{:S(2)}) %copy-start.1) | copy-done | bytes 5505048
  38.0 9.2 %dequantize.1.rest_5_.rest_2_ = bf16[1024,5376]{1,0:T(8,128)(2,1)S(1)} custom-call(bf16[512,5376]{1,0:T(8,128)(2,1)S(1)} %copy-done.1, bf16[512,5376]{1,0:T(8,128)(2,1)} %collective-permute-done.4.other_ref, f32[512,42]{1,0:T(8,128)S(1)} %copy.22.own_scale_ref, f32[512,42]{1,0:T(8,128)S(1)} %copy-done.3), custom_call_target="tpu_custom_call" | custom-call | flops 5505024 | bytes 22020096 | tf_op jit(solution)/shard_map/dequantize/pallas_call | solution.py:63
  47.2 1.5 collective-permute-done.7.rest_2_
  48.7 3.8 %collective-permute-done.9.rest_4_ = bf16[32,7936]{1,0:T(8,128)(2,1)} collective-permute-done((bf16[32,7936]{1,0:T(8,128)(2,1)S(1)}, bf16[32,7936]{1,0:T(8,128)(2,1)}, u32[]{:S(2)}, u32[]{:S(2)}) %collective-permute-start.9) | collective-permute-done | bytes 507936 | tf_op jit(solution)/shard_map/ppermute | solution.py:20
  52.5 10.2 %logits.2 = (f32[1024,256]{1,0:T(8,128)}, f32[1024,256]{1,0:T(8,128)}, f32[8,256]{1,0:T(8,128)S(1)}, bf16[256,2560]{1,0:T(8,128)(2,1)}) custom-call(s32[2]{0:T(128)S(1)} %pad_add_fusion.place_ref.y_ref, bf16[128,7936]{1,0:T(8,128)(2,1)} %constant_dynamic-update-slice_fusion.rest_0_, bf16[32,7936]{1,0:T(8,128)(2,1)S(1)} %maximum_select_fusion.rest_1_, ...), custom_call_target="tpu_custom_call" | custom-call | flops 4160749568 | bytes 7471104 | tf_op jit(solution)/shard_map/logits/pallas_call | solution.py:236
  62.8 10.9 %logits.3 = (f32[1024,256]{1,0:T(8,128)}, f32[1024,256]{1,0:T(8,128)}, f32[8,256]{1,0:T(8,128)}, bf16[256,2560]{1,0:T(8,128)(2,1)}, f32[16,8,512]{2,1,0:T(8,128)S(1)}) custom-call(s32[2]{0:T(128)S(1)} %pad_add_fusion.place_ref.y_ref, bf16[128,7936]{1,0:T(8,128)(2,1)} %collective-permute-done.1.rest_0_, bf16[128,7936]{1,0:T(8,128)(2,1)} %collective-permute-done.2.rest_1_, ...), custom_call_target="tpu_custom_call" | custom-call | flops 4160749568 | bytes 7471104 | tf_op jit(solution)/shard_map/logits/pallas_call | solution.py:236
  73.6 13.0 %all_to_all.20 = f32[16,8,512]{2,1,0:T(8,128)S(1)} all-to-all(f32[16,8,512]{2,1,0:T(8,128)S(1)} %get-tuple-element.34), channel_id=1, replica_groups=mesh['x'=4,'z'=8,'y'=4,'c'=2] {'x','y'}, dimensions={0} | all-to-all | bytes 524288 | tf_op jit(solution)/shard_map/all_to_all | solution.py:408
  87.5 7.6 %all-to-all-start.1 = ((f32[8,5,512]{2,1,0:T(8,128)}), f32[8,5,512]{2,1,0:T(8,128)S(1)}, u32[]{:S(2)}, u32[]{:S(2)}) async-start(f32[8,5,512]{2,1,0:T(8,128)} %broadcast_in_dim.20), calls=%async_computation.1 | async-start | bytes 262144 | tf_op jit(solution)/shard_map/all_to_all | solution.py:315
  95.1 9.1 %all-to-all-done.1 = f32[8,5,512]{2,1,0:T(8,128)S(1)} async-done(((f32[8,5,512]{2,1,0:T(8,128)}), f32[8,5,512]{2,1,0:T(8,128)S(1)}, u32[]{:S(2)}, u32[]{:S(2)}) %all-to-all-start.1) | async-done | bytes 81952 | tf_op jit(solution)/shard_map/all_to_all | solution.py:315
  105.1 9.2 %gradients.1 = (bf16[512,512]{1,0:T(8,128)(2,1)}, bf16[512,512]{1,0:T(8,128)(2,1)}, bf16[4,4,640,128]{3,2,1,0:T(8,128)(2,1)}) custom-call(s32[2]{0:T(128)} %copy-done.4, f32[8,512]{1,0:T(8,128)} %pad_maximum_fusion.1.rows_ref, f32[1024,256]{1,0:T(8,128)} %get-tuple-element.35.t0, f32[1024,256]{1,0:T(8,128)} %get-tuple-element.36.s0, ...), custom_call_target="tpu_custom_call" | custom-call | flops 2684354560 | bytes 13107200 | tf_op jit(solution)/shard_map/gradients/pallas_call | solution.py:287
  114.3 5.3 %all-to-all-start.2 = ((bf16[16,640,128]{2,1,0:T(8,128)(2,1)}), bf16[16,640,128]{2,1,0:T(8,128)(2,1)S(1)}, u32[]{:S(2)}, u32[]{:S(2)}) async-start(bf16[16,640,128]{2,1,0:T(8,128)(2,1)} %bitcast.83), calls=%async_computation.2 | async-start | bytes 5242880 | tf_op jit(solution)/shard_map/all_to_all | solution.py:433
  120.2 31.3 %all-to-all-done.2 = bf16[16,640,128]{2,1,0:T(8,128)(2,1)S(1)} async-done(((bf16[16,640,128]{2,1,0:T(8,128)(2,1)}), bf16[16,640,128]{2,1,0:T(8,128)(2,1)S(1)}, u32[]{:S(2)}, u32[]{:S(2)}) %all-to-all-start.2) | async-done | bytes 2621472 | tf_op jit(solution)/shard_map/all_to_all | solution.py:433
  152.6 3.4 %all-to-all-start.3 = ((bf16[8,80,128]{2,1,0:T(8,128)(2,1)}), bf16[8,80,128]{2,1,0:T(8,128)(2,1)S(1)}, u32[]{:S(2)}, u32[]{:S(2)}) async-start(bf16[8,80,128]{2,1,0:T(8,128)(2,1)} %bitcast.20), calls=%async_computation.3 | async-start | bytes 327680 | tf_op jit(solution)/shard_map/all_to_all | solution.py:435
  156.5 7.4 %weight_gradient.1 = bf16[512,2560]{1,0:T(8,128)(2,1)} custom-call(bf16[512,512]{1,0:T(8,128)(2,1)} %get-tuple-element.41.own_ref, bf16[512,512]{1,0:T(8,128)(2,1)} %collective-permute-done.10.from_ref, bf16[256,2560]{1,0:T(8,128)(2,1)} %get-tuple-element.43.s0_ref, bf16[256,2560]{1,0:T(8,128)(2,1)} %get-tuple-element.44.s1_ref, ...), custom_call_target="tpu_custom_call" | custom-call | flops 2684354560 | bytes 8912896 | tf_op jit(solution)/shard_map/weight_gradient/pallas_call | solution.py:347
  163.8 1.5 all-to-all-done.3
  (64 shorter events, 11.7 us)
Async XLA Ops:
  0.6 7.4 %copy-start.5 = (bf16[128,2560]{1,0:T(8,128)(2,1)S(1)}, bf16[128,2560]{1,0:T(8,128)(2,1)}, u32[]{:S(2)}) copy-start(bf16[128,2560]{1,0:T(8,128)(2,1)} %param.7) | copy-start | bytes 1966084
  0.6 22.9 %collective-permute-start.4 = (bf16[512,5376]{1,0:T(8,128)(2,1)}, bf16[512,5376]{1,0:T(8,128)(2,1)}, u32[]{:S(2)}, u32[]{:S(2)}) collective-permute-start(bf16[512,5376]{1,0:T(8,128)(2,1)} %own_ref.2), channel_id=1, source_target_pairs={{1,0},{0,1},{3,2},{2,3},{5,4},{4,5},{7,6},{6,7},{9,8},{8,9},{11,10... | collective-permute-start | bytes 16515080 | tf_op jit(solution)/shard_map/ppermute | solution.py:20
  0.7 22.8 %collective-permute-start.5 = (bf16[512,2560]{1,0:T(8,128)(2,1)}, bf16[512,2560]{1,0:T(8,128)(2,1)}, u32[]{:S(2)}, u32[]{:S(2)}) collective-permute-start(bf16[512,2560]{1,0:T(8,128)(2,1)} %rest_3_.1), channel_id=1, source_target_pairs={{1,0},{0,1},{3,2},{2,3},{5,4},{4,5},{7,6},{6,7},{9,8},{8,9},{11,10... | collective-permute-start | bytes 7864328 | tf_op jit(solution)/shard_map/ppermute | solution.py:20
  3.1 13.8 %copy-start.7 = (f32[512,42]{0,1:T(8,128)S(1)}, f32[512,42]{0,1:T(8,128)}, u32[]{:S(2)}) copy-start(f32[512,42]{0,1:T(8,128)} %param.9) | copy-start | bytes 258052
  3.1 9.8 %collective-permute-start = (bf16[16,7936]{1,0:T(8,128)(2,1)S(1)}, bf16[16,7936]{1,0:T(8,128)(2,1)}, u32[]{:S(2)}, u32[]{:S(2)}) collective-permute-start(bf16[16,7936]{1,0:T(8,128)(2,1)S(1)} %pad_maximum_fusion), channel_id=1, source_target_pairs={{4,0},{6,2},{0,4},{2,6},{5,1},{7,3},{1,5},{3,7},{12,8},{14,10},{8,... | collective-permute-start | bytes 761864 | tf_op jit(solution)/shard_map/ppermute | solution.py:20
  8.0 20.1 %copy-start.9 = (bf16[128]{0:T(256)(128)(2,1)S(1)}, bf16[128]{0:T(256)(128)(2,1)}, u32[]{:S(2)}) copy-start(bf16[128]{0:T(256)(128)(2,1)} %param.11) | copy-start | bytes 772
  8.0 20.1 %copy-start = (bf16[512,2560]{1,0:T(8,128)(2,1)S(1)}, bf16[512,2560]{1,0:T(8,128)(2,1)}, u32[]{:S(2)}) copy-start(bf16[512,2560]{1,0:T(8,128)(2,1)} %rest_3_.1) | copy-start | bytes 7864324
  12.9 7.7 %collective-permute-start.3 = (bf16[16,7936]{1,0:T(8,128)(2,1)}, bf16[16,7936]{1,0:T(8,128)(2,1)S(1)}, u32[]{:S(2)}, u32[]{:S(2)}) collective-permute-start(bf16[16,7936]{1,0:T(8,128)(2,1)} %collective-permute-done), channel_id=1, source_target_pairs={{0,8},{8,0},{16,24},{24,16},{32,40},{40,32},{48,56},{56,48},{1,9},... | collective-permute-start | bytes 761864 | tf_op jit(solution)/shard_map/ppermute | solution.py:381
  14.9 47.9 %collective-permute-start.1 = (bf16[128,7936]{1,0:T(8,128)(2,1)}, bf16[128,7936]{1,0:T(8,128)(2,1)}, u32[]{:S(2)}, u32[]{:S(2)}) collective-permute-start(bf16[128,7936]{1,0:T(8,128)(2,1)} %constant_dynamic-update-slice_fusion.rest_0_), channel_id=1, source_target_pairs={{2,0},{4,2},{6,4},{0,6},{3,1},{5,3},{7,5},{1,7},{10,8},{12,10},{14... | collective-permute-start | bytes 6094856 | tf_op jit(solution)/shard_map/ppermute | solution.py:20
  15.3 47.4 %collective-permute-start.2 = (bf16[128,7936]{1,0:T(8,128)(2,1)}, bf16[128,7936]{1,0:T(8,128)(2,1)}, u32[]{:S(2)}, u32[]{:S(2)}) collective-permute-start(bf16[128,7936]{1,0:T(8,128)(2,1)} %constant_dynamic-update-slice_fusion.rest_0_), channel_id=1, source_target_pairs={{6,0},{0,2},{2,4},{4,6},{7,1},{1,3},{3,5},{5,7},{14,8},{8,10},{10,... | collective-permute-start | bytes 6094856 | tf_op jit(solution)/shard_map/ppermute | solution.py:20
  21.3 1.5 collective-permute-start.6
  23.6 25.1 %collective-permute-start.7 = (bf16[32,7936]{1,0:T(8,128)(2,1)S(1)}, bf16[32,7936]{1,0:T(8,128)(2,1)}, u32[]{:S(2)}, u32[]{:S(2)}) collective-permute-start(bf16[32,7936]{1,0:T(8,128)(2,1)S(1)} %maximum_select_fusion.rest_1_), channel_id=1, source_target_pairs={{64,0},{128,64},{192,128},{0,192},{65,1},{129,65},{193,129},{1,193... | collective-permute-start | bytes 1523720 | tf_op jit(solution)/shard_map/ppermute | solution.py:20
  26.3 22.4 %collective-permute-start.8 = (bf16[32,7936]{1,0:T(8,128)(2,1)S(1)}, bf16[32,7936]{1,0:T(8,128)(2,1)}, u32[]{:S(2)}, u32[]{:S(2)}) collective-permute-start(bf16[32,7936]{1,0:T(8,128)(2,1)S(1)} %maximum_select_fusion.rest_1_), channel_id=1, source_target_pairs={{128,0},{192,64},{0,128},{64,192},{129,1},{193,65},{1,129},{65,193... | collective-permute-start | bytes 1523720 | tf_op jit(solution)/shard_map/ppermute | solution.py:20
  27.1 25.3 %collective-permute-start.9 = (bf16[32,7936]{1,0:T(8,128)(2,1)S(1)}, bf16[32,7936]{1,0:T(8,128)(2,1)}, u32[]{:S(2)}, u32[]{:S(2)}) collective-permute-start(bf16[32,7936]{1,0:T(8,128)(2,1)S(1)} %maximum_select_fusion.rest_1_), channel_id=1, source_target_pairs={{192,0},{0,64},{64,128},{128,192},{193,1},{1,65},{65,129},{129,193... | collective-permute-start | bytes 1523720 | tf_op jit(solution)/shard_map/ppermute | solution.py:20
  28.1 34.6 %copy-start.4 = (s32[2]{0:T(128)}, s32[2]{0:T(128)S(1)}, u32[]{:S(2)}) copy-start(s32[2]{0:T(128)S(1)} %pad_add_fusion.place_ref.y_ref) | copy-start | bytes 28
  28.1 7.3 %copy-start.3 = (f32[512,42]{1,0:T(8,128)S(1)}, f32[512,42]{1,0:T(8,128)}, u32[]{:S(2)}) copy-start(f32[512,42]{1,0:T(8,128)} %copy-done.2) | copy-start | bytes 258052
  35.4 2.6 %copy-start.1 = (bf16[512,5376]{1,0:T(8,128)(2,1)S(1)}, bf16[512,5376]{1,0:T(8,128)(2,1)}, u32[]{:S(2)}) copy-start(bf16[512,5376]{1,0:T(8,128)(2,1)} %own_ref.2) | copy-start | bytes 16515076
  87.5 16.6 %all-to-all-start.1 = ((f32[8,5,512]{2,1,0:T(8,128)}), f32[8,5,512]{2,1,0:T(8,128)S(1)}, u32[]{:S(2)}, u32[]{:S(2)}) async-start(f32[8,5,512]{2,1,0:T(8,128)} %broadcast_in_dim.20), calls=%async_computation.1 | async-start | bytes 262144 | tf_op jit(solution)/shard_map/all_to_all | solution.py:315
  114.3 5.8 %copy-start.8 = (bf16[512,512]{1,0:T(8,128)(2,1)S(1)}, bf16[512,512]{1,0:T(8,128)(2,1)}, u32[]{:S(2)}) copy-start(bf16[512,512]{1,0:T(8,128)(2,1)} %get-tuple-element.42) | copy-start | bytes 1572868
  114.3 37.2 %all-to-all-start.2 = ((bf16[16,640,128]{2,1,0:T(8,128)(2,1)}), bf16[16,640,128]{2,1,0:T(8,128)(2,1)S(1)}, u32[]{:S(2)}, u32[]{:S(2)}) async-start(bf16[16,640,128]{2,1,0:T(8,128)(2,1)} %bitcast.83), calls=%async_computation.2 | async-start | bytes 5242880 | tf_op jit(solution)/shard_map/all_to_all | solution.py:433
  119.6 36.9 %collective-permute-start.12 = (bf16[256,2560]{1,0:T(8,128)(2,1)}, bf16[256,2560]{1,0:T(8,128)(2,1)}, u32[]{:S(2)}, u32[]{:S(2)}) collective-permute-start(bf16[256,2560]{1,0:T(8,128)(2,1)} %get-tuple-element.44.s1_ref), channel_id=1, source_target_pairs={{1,0},{0,1},{3,2},{2,3},{5,4},{4,5},{7,6},{6,7},{9,8},{8,9},{11,10... | collective-permute-start | bytes 3932168 | tf_op jit(solution)/shard_map/ppermute | solution.py:20
  119.6 36.9 %collective-permute-start.11 = (bf16[256,2560]{1,0:T(8,128)(2,1)}, bf16[256,2560]{1,0:T(8,128)(2,1)}, u32[]{:S(2)}, u32[]{:S(2)}) collective-permute-start(bf16[256,2560]{1,0:T(8,128)(2,1)} %get-tuple-element.43.s0_ref), channel_id=1, source_target_pairs={{1,0},{0,1},{3,2},{2,3},{5,4},{4,5},{7,6},{6,7},{9,8},{8,9},{11,10... | collective-permute-start | bytes 3932168 | tf_op jit(solution)/shard_map/ppermute | solution.py:20
  120.1 36.4 %collective-permute-start.10 = (bf16[512,512]{1,0:T(8,128)(2,1)S(1)}, bf16[512,512]{1,0:T(8,128)(2,1)}, u32[]{:S(2)}, u32[]{:S(2)}) collective-permute-start(bf16[512,512]{1,0:T(8,128)(2,1)S(1)} %copy-done.8), channel_id=1, source_target_pairs={{1,0},{0,1},{3,2},{2,3},{5,4},{4,5},{7,6},{6,7},{9,8},{8,9},{11,10... | collective-permute-start | bytes 1572872 | tf_op jit(solution)/shard_map/ppermute | solution.py:20
  152.6 12.7 %all-to-all-start.3 = ((bf16[8,80,128]{2,1,0:T(8,128)(2,1)}), bf16[8,80,128]{2,1,0:T(8,128)(2,1)S(1)}, u32[]{:S(2)}, u32[]{:S(2)}) async-start(bf16[8,80,128]{2,1,0:T(8,128)(2,1)} %bitcast.20), calls=%async_computation.3 | async-start | bytes 327680 | tf_op jit(solution)/shard_map/all_to_all | solution.py:435
  (2 other events, 1.4 us)
